TPU v7x, 512 devices: a whole 4x8x8 slice. The times are simulated.
512 devices in a mesh: ens: 16 (over y, x_hi), grid: 32 (over x_lo, z, core).
Axes of the slice: x: 4 (x_hi: 2, x_lo: 2; x = x_hi * 2 + x_lo), y: 8, z: 8, core: 2. Of those that a mesh axis runs over, the one named last changes fastest.
Arguments:
- latent: bfloat16 [16, 1024, 8192], P('ens', None, 'grid'), may hold values from -24 to 24
- w_in: bfloat16 [1024, 1024], replicated, may hold values from -0.1875 to 0.1875
- w_out: bfloat16 [99, 1024], replicated, may hold values from -0.1875 to 0.1875
- target: float32 [99, 8192], P(None, 'grid'), may hold values from -6 to 6
- area: float32 [8192], P('grid'), may hold values from 0.05 to 3, as said below
- var_weight: float32 [99], replicated, may hold values from 0.2 to 2
Outputs:
- loss: float32 [], replicated
- grad_latent: bfloat16 [16, 1024, 8192], P('ens', None, 'grid')
- grad_in: float32 [1024, 1024], P('ens', 'grid')
- grad_out: float32 [99, 1024], P(None, 'grid')
Inputs may be any that keep to these rules, and one draw needn't show every extreme that they name: Every area weight is positive.
All inputs are finite; a program needn't handle non-finite values.
Results may differ from a plain program's by a relative error of at most 0.013.
Values may be sent and summed in bfloat16 or wider, within the bound.
No kernel may reach another device: no remote copies, remote signals or barrier semaphores. Data moves between devices by JAX's collectives and lax.ppermute only.
A program may use at most 64 MiB of HBM per device.

v0:
```python
import jax
import jax.numpy as jnp
from jax import lax
from jax.sharding import PartitionSpec as P

VARS = 99


smooth_sq = 0.01
gelu_c = 0.7978845608
gelu_k = 0.044715


def gelu_value(value):
    inner = jnp.tanh(gelu_c * (value + gelu_k * value * value * value))
    return 0.5 * value * (1.0 + inner)


def gelu_slope(value):
    inner = jnp.tanh(gelu_c * (value + gelu_k * value * value * value))
    return 0.5 * (1.0 + inner) + 0.5 * value * (1.0 - inner * inner) * gelu_c * (
        1.0 + 3.0 * gelu_k * value * value
    )


def distance(value):
    return jnp.sqrt(value * value + smooth_sq)


def distance_slope(value):
    return value / jnp.sqrt(value * value + smooth_sq)


def per_device(latent, w_in, w_out, target, area, var_weight):
    count = float(lax.axis_size("ens"))
    points_all = lax.axis_size("grid") * area.shape[0]
    features = latent[0]
    preact = jnp.dot(w_in, features, preferred_element_type=jnp.float32)
    hidden = gelu_value(preact).astype(jnp.bfloat16)
    decoded = jnp.dot(w_out, hidden, preferred_element_type=jnp.float32)
    weight_total = lax.psum(jnp.sum(area), "grid")
    spread = decoded[None] - lax.all_gather(decoded[None], "ens", axis=0, tiled=True)
    pair_sum = jnp.sum(distance(spread), 0)
    pair_slope = jnp.sum(distance_slope(spread), 0)
    weight = area[None, :] * var_weight[:, None]
    local = distance(decoded - target) / count - pair_sum / (2.0 * count * (count - 1.0))
    loss = lax.psum(jnp.sum(weight * local), ("ens", "grid")) / (weight_total * VARS)
    factor = points_all / (weight_total * VARS)
    dout = (
        factor
        * weight
        * (distance_slope(decoded - target) / count - pair_slope / (count * (count - 1.0)))
    ).astype(jnp.bfloat16)
    dhidden = lax.dot_general(
        w_out, dout, (((0,), (0,)), ((), ())), preferred_element_type=jnp.float32
    )
    dpre = (dhidden * gelu_slope(preact)).astype(jnp.bfloat16)
    grad_lat = lax.dot_general(
        w_in, dpre, (((0,), (0,)), ((), ())), preferred_element_type=jnp.float32
    ).astype(jnp.bfloat16)
    term_in = lax.dot_general(
        dpre, features, (((1,), (1,)), ((), ())), preferred_element_type=jnp.float32
    )
    term_out = lax.dot_general(
        dout, hidden, (((1,), (1,)), ((), ())), preferred_element_type=jnp.float32
    )
    part_in = lax.psum_scatter(
        term_in.astype(jnp.bfloat16), "ens", scatter_dimension=0, tiled=True
    ).astype(jnp.float32)
    total_in = lax.psum_scatter(part_in, "grid", scatter_dimension=1, tiled=True)
    part_out = lax.psum(term_out.astype(jnp.bfloat16), "ens").astype(jnp.float32)
    total_out = lax.psum_scatter(part_out, "grid", scatter_dimension=1, tiled=True)
    ratio = 1.0 / jnp.sqrt(jnp.float32(points_all) * jnp.float32(count))
    return (loss, grad_lat[None], ratio * total_in, ratio * total_out)


def solution(mesh):
    in_specs = (P("ens", None, "grid"), P(), P(), P(None, "grid"), P("grid"), P())
    out_specs = (P(), P("ens", None, "grid"), P("ens", "grid"), P(None, "grid"))
    return jax.shard_map(
        per_device, mesh=mesh, in_specs=in_specs, out_specs=out_specs, check_vma=False
    )
```

profile of v0, /device:TPU:12, one launch (start us, length us, event | category | flops | bytes accessed | tf_op | source)
XLA Modules:
  0.0 740.1 jit_solution(3120073708774309567)
XLA Ops:
  7.2 1.5 copy-done
  8.8 2.8 multiply_convert_fusion
  11.6 0.9 fusion.17
  12.6 0.6 reduce_sum.38
  13.2 62.8 %psum.22 = f32[]{:T(128)} all-reduce(f32[]{:T(128)} %reduce_sum.38), channel_id=1, replica_groups=mesh['ens'=16,'grid'=32] {'grid'}, use_global_device_ids=true, to_apply=%region_4.0 | all-reduce | flops 1 | bytes 8 | tf_op jit(solution)/shard_map/psum | solution.py:41
  76.7 25.9 %all-gather.4.cloned.1.call-done = f32[16,99,256]{2,1,0:T(8,128)} async-done(((f32[1,99,256]{2,1,0:T(8,128)}), f32[16,99,256]{2,1,0:T(8,128)}) %all-gather.4.cloned.1.call-update) | async-done | bytes 1622032 | tf_op jit(solution)/shard_map/all_gather | solution.py:42
  102.6 2.3 fusion.2
  104.9 0.7 fusion.16
  105.6 1.0 convolution_convert_fusion.2
  106.6 2.1 fusion.4
  108.8 2.1 convolution_convert_fusion
  111.0 159.8 %all-reduce.2.cloned.1.call-done = bf16[99,1024]{0,1:T(8,128)(2,1)} async-done(((bf16[99,1024]{0,1:T(8,128)(2,1)}), bf16[99,1024]{0,1:T(8,128)(2,1)}) %all-reduce.2.cloned.1.call-update) | async-done | bytes 202768 | tf_op jit(solution)/shard_map/psum | solution.py:71
  270.7 1.8 convert_element_type.35
  272.5 0.0 reduce-scatter.10.cloned.1.call-start
  272.6 215.5 %reduce-scatter.6.cloned.1.call-done = bf16[64,1024]{1,0:T(8,128)(2,1)} async-done(((bf16[1024,1024]{1,0:T(8,128)(2,1)}), bf16[64,1024]{1,0:T(8,128)(2,1)}) %reduce-scatter.6.cloned.1.call-update) | async-done | bytes 131088 | tf_op jit(solution)/shard_map/reduce_scatter | solution.py:67
  488.1 1.8 copy.17
  490.0 95.5 %psum.21 = f32[]{:T(128)} all-reduce(f32[]{:T(128)} %get-tuple-element.15), channel_id=1, replica_groups=mesh['ens'=16,'grid'=32] {'ens','grid'}, use_global_device_ids=true, to_apply=%region_2.0 | all-reduce | flops 1 | bytes 8 | tf_op jit(solution)/shard_map/psum | solution.py:47
  585.5 0.7 fusion.5
  586.2 1.0 copy.14
  587.8 23.7 %reduce-scatter.8.cloned.1.call-done = f32[99,32]{0,1:T(8,128)} async-done(((f32[99,1024]{0,1:T(8,128)}), f32[99,32]{0,1:T(8,128)}) %reduce-scatter.8.cloned.1.call-update) | async-done | bytes 12688 | tf_op jit(solution)/shard_map/reduce_scatter | solution.py:72
  611.6 1.3 broadcast_multiply_fusion.1
  612.9 118.0 %reduce-scatter.10.cloned.1.call-done = f32[32,64]{1,0:T(8,128)} async-done(((f32[1024,64]{1,0:T(8,128)}), f32[32,64]{1,0:T(8,128)}) %reduce-scatter.10.cloned.1.call-update) | async-done | bytes 8208
  730.9 0.8 copy.18
  731.7 0.7 copy.15
  (23 shorter events, 0.3 us)
Async XLA Ops:
  7.2 1.6 copy-start
  7.2 4.4 copy-start.3
  7.2 5.4 copy-start.5
  7.2 95.4 %all-gather.4.cloned.1.call-start = ((), (), s32[]{:S(2)}) async-start(), calls=%async_computation.6 | async-start | bytes 1810432 | tf_op jit(solution)/shard_map/all_gather | solution.py:42
  11.6 93.3 %copy-start.4 = (f32[99,256]{1,0:T(8,128)S(1)}, f32[99,256]{1,0:T(8,128)}, u32[]{:S(2)}) copy-start(f32[99,256]{1,0:T(8,128)} %param.9) | copy-start | bytes 304132
  11.6 93.3 %copy-start.6 = (f32[99]{0:T(128)S(1)}, f32[99]{0:T(128)}, u32[]{:S(2)}) copy-start(f32[99]{0:T(128)} %param.11) | copy-start | bytes 1192
  12.5 92.4 %copy-start.1 = (f32[256,99]{0,1:T(8,128)S(1)}, f32[256,99]{0,1:T(8,128)}, u32[]{:S(2)}) copy-start(f32[256,99]{0,1:T(8,128)} %fusion.17) | copy-start | bytes 304132
  12.5 258.2 %all-reduce.2.cloned.1.call-start = ((), (), s32[]{:S(2)}) async-start(), calls=%async_computation.4 | async-start | bytes 524288 | tf_op jit(solution)/shard_map/psum | solution.py:71
  106.6 2.2 copy-start.2
  108.7 379.4 %reduce-scatter.6.cloned.1.call-start = ((), (), s32[]{:S(2)}) async-start(), calls=%async_computation.3 | async-start | bytes 2228224 | tf_op jit(solution)/shard_map/reduce_scatter | solution.py:67
  110.9 500.7 %reduce-scatter.8.cloned.1.call-start = ((), (), s32[]{:S(2)}) async-start(), calls=%async_computation.5 | async-start | bytes 540672 | tf_op jit(solution)/shard_map/reduce_scatter | solution.py:72
  272.5 458.4 %reduce-scatter.10.cloned.1.call-start = ((), (), s32[]{:S(2)}) async-start(), calls=%async_computation.7 | async-start | bytes 540672
Sparse Core Ops, SparseCore 0:
  12.6 89.8 all-gather.3
  108.9 161.8 all-reduce.1
  275.2 212.8 reduce-scatter.5
  490.8 120.7 reduce-scatter.7
  614.2 116.6 reduce-scatter.9
where the time goes:
time: 741 us; the launch traced here: 740 us
  waiting for transfers between devices  543 us (73%)
  blocking collectives  158 us (21%)
  between operations  16.4 us (2%)
  matrix products  9.62 us (1%)
    reduce_scatter x1, waiting for transfers between devices, per_device(): lax.psum_scatter(term_in.astype(jnp.bfloat16), 'ens', scatter_dimension=0...  216 us
    psum x1, waiting for transfers between devices, per_device(): lax.psum(term_out.astype(jnp.bfloat16), 'ens').astype(jnp.float32)  160 us
    unnamed x6, waiting for transfers between devices  118 us
    psum x1, blocking collectives, per_device(): lax.psum(jnp.sum(weight * local), ('ens', 'grid')) / (weight_total * VARS)  95.5 us
    psum x1, blocking collectives, per_device(): weight_total = lax.psum(jnp.sum(area), 'grid')  62.8 us
    all_gather x1, waiting for transfers between devices, per_device(): lax.all_gather(decoded[None], 'ens', axis=0, tiled=True)  25.9 us
    reduce_scatter x1, waiting for transfers between devices, per_device(): lax.psum_scatter(part_out, 'grid', scatter_dimension=1, tiled=True)  23.7 us
  transfers between devices with their start and end apart: 5, of which 5 were waited for; matrix products, arithmetic and copies ran while one was open for 1% of the time, Pallas kernels for 0%

commit v1 on v0

v1 whole, which is shorter than its diff:
```python
import jax
import jax.numpy as jnp
from jax import lax
from jax.sharding import Mesh, PartitionSpec as P

VARS = 99
PAD = 128
ENS = ("y", "xh")
PLANE = ("xl", "z")

smooth_sq = 0.01
gelu_c = 0.7978845608
gelu_k = 0.044715
f32 = jnp.float32
bf16 = jnp.bfloat16


def gelu_value(value):
    inner = jnp.tanh(gelu_c * (value + gelu_k * value * value * value))
    return 0.5 * value * (1.0 + inner)


def gelu_slope(value):
    inner = jnp.tanh(gelu_c * (value + gelu_k * value * value * value))
    return 0.5 * (1.0 + inner) + 0.5 * value * (1.0 - inner * inner) * gelu_c * (
        1.0 + 3.0 * gelu_k * value * value
    )


def distance(value):
    return jnp.sqrt(value * value + smooth_sq)


def distance_slope(value):
    return value / jnp.sqrt(value * value + smooth_sq)


def exchange(pieces, axes):
    return lax.all_to_all(pieces, axes, split_axis=0, concat_axis=0, tiled=True)


def halves(value):
    high = lax.reduce_precision(value, 8, 7)
    return high, value - high


def with_scalars(rows, loss, area):
    row = lax.broadcasted_iota(jnp.int32, rows.shape, rows.ndim - 2)
    col = lax.broadcasted_iota(jnp.int32, rows.shape, rows.ndim - 1)
    for k, part in enumerate(halves(loss) + halves(area)):
        rows = jnp.where((row == 0) & (col == VARS + 1 + k), part, rows)
    return rows


def scalars(rows):
    at = VARS + 1
    return rows[0, at] + rows[0, at + 1], rows[0, at + 2] + rows[0, at + 3]


def per_device(latent, w_in, w_out, target, area, var_weight):
    n_ens = lax.axis_size(ENS)
    n_plane = lax.axis_size(PLANE)
    n_core = lax.axis_size("c")
    count = float(n_ens)
    pts = area.shape[0]
    points_all = n_plane * n_core * pts
    hid, lat = w_in.shape
    vars_own = PAD // n_ens
    cols = lat // (n_plane * n_core)
    me = lax.axis_index(ENS)
    core = lax.axis_index("c")
    features = latent[0]
    w_out_pad = jnp.pad(w_out, ((0, PAD - VARS), (0, 0)))

    preact = jnp.dot(w_in, features, preferred_element_type=f32)
    hidden = gelu_value(preact).astype(bf16)
    decoded = jnp.dot(w_out_pad, hidden, preferred_element_type=f32)

    fields = exchange(decoded.reshape(n_ens, vars_own, pts), ENS)
    target_own = lax.dynamic_slice_in_dim(
        jnp.pad(target, ((0, PAD - VARS), (0, 0))), me * vars_own, vars_own
    )
    weight_own = lax.dynamic_slice_in_dim(
        jnp.pad(var_weight, (0, PAD - VARS)), me * vars_own, vars_own
    )
    spread = fields[:, None] - fields[None]
    pair_sum = jnp.sum(distance(spread), 1)
    pair_slope = jnp.sum(distance_slope(spread), 1)
    weight = area[None, :] * weight_own[:, None]
    miss = fields - target_own[None]
    local = distance(miss) / count - pair_sum / (2.0 * count * (count - 1.0))
    loss = jnp.sum(weight[None] * local)
    dout_own = (
        weight[None]
        * (distance_slope(miss) / count - pair_slope / (count * (count - 1.0)))
    ).astype(bf16)
    dout = exchange(dout_own, ENS).reshape(PAD, pts)

    dhidden = lax.dot_general(
        w_out_pad, dout, (((0,), (0,)), ((), ())), preferred_element_type=f32
    )
    dpre = (dhidden * gelu_slope(preact)).astype(bf16)
    grad_lat = lax.dot_general(
        w_in, dpre, (((0,), (0,)), ((), ())), preferred_element_type=f32
    )
    grad_lat = lax.optimization_barrier(grad_lat)

    def rows_of(value, which):
        split = value.reshape(n_plane, n_core, cols, pts)
        return lax.dynamic_index_in_dim(split, which, 1, keepdims=False).reshape(-1, pts)

    def terms(which):
        contract = (((1,), (1,)), ((), ()))
        part_in = lax.dot_general(
            rows_of(features, which), dpre, contract, preferred_element_type=f32
        )
        part_out = lax.dot_general(
            rows_of(hidden, which), dout, contract, preferred_element_type=f32
        )
        return part_in, part_out.reshape(n_plane, cols, PAD)

    def packed(part_in, part_out):
        return jnp.concatenate(
            [part_in.astype(bf16), part_out.reshape(-1, PAD).astype(bf16)], 1
        )

    area_sum = jnp.sum(area)
    part_in, part_out = terms(1 - core)
    away = packed(part_in, with_scalars(part_out, loss, area_sum))
    came = lax.ppermute(away, "c", [(0, 1), (1, 0)]).astype(f32)
    part_in, part_out = terms(core)
    came_out = came[:, hid:].reshape(n_plane, cols, PAD)
    came_loss, came_area = scalars(came_out[0])
    sums = packed(
        part_in + came[:, :hid],
        with_scalars(part_out + came_out, loss + came_loss, area_sum + came_area),
    )

    got = exchange(sums.reshape(n_plane, cols, hid + PAD), PLANE)
    got = jnp.sum(got.astype(f32), 0)
    block_in = got[:, :hid].reshape(2, cols // 2, n_ens, hid // n_ens)
    block_in = block_in.transpose(2, 1, 0, 3).reshape(n_ens, cols // 2, PAD)
    block_out = with_scalars(got[:, hid:], *scalars(got[:, hid:]))
    pieces = jnp.concatenate(
        [
            block_in.astype(bf16),
            jnp.broadcast_to(block_out.astype(bf16)[None], (n_ens, cols, PAD)),
        ],
        1,
    )
    final = jnp.sum(exchange(pieces, ENS).astype(f32), 0)
    final_in = final[: cols // 2].reshape(cols // 2, 2, hid // n_ens)
    final_in = final_in.transpose(2, 1, 0).reshape(hid // n_ens, cols)
    final_out = final[cols // 2 :]
    loss_sum, area_all = scalars(final_out)
    weight_total = area_all / count
    factor = points_all / (weight_total * VARS)
    ratio = factor / jnp.sqrt(f32(points_all) * f32(count))
    return (
        loss_sum / (weight_total * VARS),
        (factor * grad_lat).astype(bf16)[None],
        ratio * final_in,
        ratio * final_out[:, :VARS].T,
    )


def solution(mesh):
    ens, grid_all = mesh.devices.shape
    split = (ens // 2, 2, 2, grid_all // 4, 2)
    fine = Mesh(mesh.devices.reshape(split), ENS + PLANE + ("c",))
    grid = PLANE + ("c",)
    in_specs = (P(ENS, None, grid), P(), P(), P(None, grid), P(grid), P())
    out_specs = (P(), P(ENS, None, grid), P(ENS, grid), P(None, grid))
    return jax.shard_map(
        per_device, mesh=fine, in_specs=in_specs, out_specs=out_specs, check_vma=False
    )
```

time: 741 us -> 139 us (0.19)
  the two profiles are of different devices: /device:TPU:12 before, /device:TPU:2 now
where the time goes in v1:
time: 139 us; the launch traced here: 138 us
  blocking collectives  41.9 us (30%)
  waiting for transfers between devices  27.9 us (20%)
  between operations  20.7 us (15%)
  starting transfers between devices  17.7 us (13%)
  matrix products  11.2 us (8%)
  other arithmetic  10.5 us (8%)
  local copies, waits for them, and re-layouts  8.32 us (6%)
    all_to_all x1, blocking collectives, exchange(): return lax.all_to_all(pieces, axes, split_axis=0, concat_axis=0, tiled=True)  41.9 us
    all_to_all x3, waiting for transfers between devices, exchange(): return lax.all_to_all(pieces, axes, split_axis=0, concat_axis=0, tiled=True)  25.4 us
    all_to_all x3, starting transfers between devices, exchange(): return lax.all_to_all(pieces, axes, split_axis=0, concat_axis=0, tiled=True)  15.8 us
    unnamed x15, local copies, waits for them, and re-layouts  3.6 us
    dot_general x1, matrix products, per_device(): preact = jnp.dot(w_in, features, preferred_element_type=f32)  2.88 us
  transfers between devices with their start and end apart: 4, of which 4 were waited for; matrix products, arithmetic and copies ran while one was open for 2% of the time, Pallas kernels for 0%

profile of v1, /device:TPU:2, one launch (start us, length us, event | category | flops | bytes accessed | tf_op | source)
XLA Modules:
  0.0 138.3 jit_solution(6672123580274148838)
XLA Ops:
  0.7 1.6 %copy-done = bf16[1024,1024]{1,0:T(8,128)(2,1)S(1)} copy-done((bf16[1024,1024]{1,0:T(8,128)(2,1)S(1)}, bf16[1024,1024]{1,0:T(8,128)(2,1)}, u32[]{:S(2)}) %copy-start) | copy-done | bytes 2097176
  2.2 2.9 %multiply_convert_fusion.1 = (bf16[1024,256]{1,0:T(8,128)(2,1)S(1)}, f32[1024,256]{1,0:T(8,128)}) fusion(bf16[1024,1024]{1,0:T(8,128)(2,1)S(1)} %copy-done, bf16[1,1024,256]{2,1,0:T(8,128)(2,1)} %param.6), kind=kOutput, calls=%fused_computation.29 | convolution fusion | flops 539230208 | bytes 4194304 | tf_op jit(solution)/shard_map/dot_general | solution.py:75
  6.0 8.8 %all-to-all-start = ((f32[16,8,256]{2,1,0:T(8,128)}), f32[16,8,256]{2,1,0:T(8,128)S(1)}, u32[]{:S(2)}, u32[]{:S(2)}) async-start(f32[16,8,256]{2,1,0:T(8,128)} %convolution_bitcast_fusion.1), calls=%async_computation | async-start | bytes 262144 | tf_op jit(solution)/shard_map/all_to_all | solution.py:39
  18.1 7.8 %all-to-all-done = f32[16,8,256]{2,1,0:T(8,128)S(1)} async-done(((f32[16,8,256]{2,1,0:T(8,128)}), f32[16,8,256]{2,1,0:T(8,128)S(1)}, u32[]{:S(2)}, u32[]{:S(2)}) %all-to-all-start) | async-done | bytes 131104 | tf_op jit(solution)/shard_map/all_to_all | solution.py:39
  25.9 1.2 fusion.2
  27.1 1.3 multiply_reduce_fusion
  28.4 3.5 %all-to-all-start.1 = ((bf16[16,8,256]{2,1,0:T(8,128)(2,1)}), bf16[16,8,256]{2,1,0:T(8,128)(2,1)S(1)}, u32[]{:S(2)}, u32[]{:S(2)}) async-start(bf16[16,8,256]{2,1,0:T(8,128)(2,1)} %get-tuple-element.33), calls=%async_computation.1 | async-start | bytes 131072 | tf_op jit(solution)/shard_map/all_to_all | solution.py:39
  35.2 7.3 %all-to-all-done.1 = bf16[16,8,256]{2,1,0:T(8,128)(2,1)S(1)} async-done(((bf16[16,8,256]{2,1,0:T(8,128)(2,1)}), bf16[16,8,256]{2,1,0:T(8,128)(2,1)S(1)}, u32[]{:S(2)}, u32[]{:S(2)}) %all-to-all-start.1) | async-done | bytes 65568 | tf_op jit(solution)/shard_map/all_to_all | solution.py:39
  42.5 2.1 %fusion.5 = bf16[1024,256]{1,0:T(8,128)(2,1)S(1)} fusion(f32[1024,256]{1,0:T(8,128)} %get-tuple-element.39, bf16[99,1024]{1,0:T(8,128)(2,1)} %param.8, bf16[16,8,256]{2,1,0:T(8,128)(2,1)S(1)} %all-to-all-done.1), kind=kOutput, calls=%fused_computation.14 | convolution fusion | flops 72089600 | bytes 1841152 | tf_op jit(solution)/shard_map/dot_general | solution.py:99
  45.1 1.5 %fusion.9 = bf16[16,32,128]{2,1,0:T(8,128)(2,1)S(1)} fusion(bf16[16,2,32,256]{3,2,1,0:T(8,128)(2,1)S(1)} %bitcast.54, s32[]{:T(128)S(6)} %select_n.53, f32[]{:T(128)} %reduce_precision.19, bf16[]{:T(256)S(6)} %sub.61, f32[]{:T(128)} %reduce_precision.18, bf16[]{:T(256)S(6)} %sub.59, pred[128]{0:T(512)(128)(4,1)S(1)} %get-tuple-element.42, ...), kind=kOutput, calls=%fused_computation.21 | convolution fusion | flops 34078720 | bytes 461328 | tf_op jit(solution)/shard_map/dot_general | solution.py:117
  46.7 1.9 %collective-permute-start = (bf16[512,1152]{1,0:T(8,128)(2,1)S(1)}, bf16[512,1152]{1,0:T(8,128)(2,1)S(1)}, u32[]{:S(2)}, u32[]{:S(2)}) collective-permute-start(bf16[512,1152]{1,0:T(8,128)(2,1)S(1)} %pad_maximum_fusion), channel_id=1, source_target_pairs={{0,1},{1,0},{2,3},{3,2},{4,5},{5,4},{6,7},{7,6},{8,9},{9,8},{10,11... | collective-permute-start | bytes 3538952 | tf_op jit(solution)/shard_map/ppermute | solution.py:130
  48.9 2.6 %collective-permute-done = bf16[512,1152]{1,0:T(8,128)(2,1)S(1)} collective-permute-done((bf16[512,1152]{1,0:T(8,128)(2,1)S(1)}, bf16[512,1152]{1,0:T(8,128)(2,1)S(1)}, u32[]{:S(2)}, u32[]{:S(2)}) %collective-permute-start) | collective-permute-done | bytes 1179680 | tf_op jit(solution)/shard_map/ppermute | solution.py:130
  51.5 1.0 copy-done.1
  59.4 1.4 %convert_element_type.64 = f32[512,1152]{1,0:T(8,128)S(1)} convert(bf16[512,1152]{1,0:T(8,128)(2,1)} %copy-done.1) | non-fusion elementwise | flops 589824 | bytes 3538944 | tf_op jit(solution)/shard_map/convert_element_type | solution.py:130
  60.8 1.4 %fusion.4 = bf16[512,1024]{1,0:T(8,128)(2,1)S(1)} fusion(f32[512,1152]{1,0:T(8,128)S(1)} %convert_element_type.64, bf16[512,256]{1,0:T(8,128)(2,1)} %bitcast.58, bf16[1024,256]{1,0:T(8,128)(2,1)S(1)} %fusion.5), kind=kOutput, calls=%fused_computation.8 | convolution fusion | flops 269484032 | bytes 3932160 | tf_op jit(solution)/shard_map/dot_general | solution.py:114
  62.3 0.9 slice.96
  63.2 1.4 %fusion.18 = bf16[16,32,128]{2,1,0:T(8,128)(2,1)S(1)} fusion(f32[16,32,128]{2,1,0:T(8,128)S(1)} %fusion.19, f32[16,32,128]{2,1,0:T(8,128)S(1)} %bitcast.57, f32[]{:T(128)} %reduce_precision.21, bf16[]{:T(256)S(6)} %sub.63, f32[]{:T(128)} %reduce_precision.20, bf16[]{:T(256)S(6)} %sub.62, pred[128]{0:T(512)(128)(4,1)S(1)} %get-tuple-element.42, ...), kind=kLoop, calls=%fused_computation.38 | loop fusion | flops 589824 | bytes 655916 | tf_op jit(solution)/shard_map/convert_element_type | solution.py:124
  64.7 41.9 %all_to_all.20 = bf16[16,32,1152]{2,1,0:T(8,128)(2,1)S(1)} all-to-all(bf16[16,32,1152]{2,1,0:T(8,128)(2,1)S(1)} %bitcast.53), channel_id=1, replica_groups=mesh['y'=8,'xh'=2,'xl'=2,'z'=8,'c'=2] {'xl','z'}, dimensions={0} | all-to-all | bytes 2359296 | tf_op jit(solution)/shard_map/all_to_all | solution.py:39
  112.8 1.4 fusion.33
  114.9 3.5 %all-to-all-start.3 = ((bf16[16,48,128]{2,1,0:T(8,128)(2,1)}), bf16[16,48,128]{2,1,0:T(8,128)(2,1)S(1)}, u32[]{:S(2)}, u32[]{:S(2)}) async-start(bf16[16,48,128]{2,1,0:T(8,128)(2,1)} %pad_maximum_fusion.2), calls=%async_computation.3 | async-start | bytes 393216 | tf_op jit(solution)/shard_map/all_to_all | solution.py:39
  118.4 1.7 %convolution_bitcast_fusion = f32[1024,256]{0,1:T(8,128)} fusion(bf16[1024,256]{1,0:T(8,128)(2,1)S(1)} %fusion.5, bf16[1024,1024]{1,0:T(8,128)(2,1)S(1)} %copy-done), kind=kOutput, calls=%fused_computation.12 | convolution fusion | flops 536870912 | bytes 3670016 | tf_op jit(solution)/shard_map/dot_general | solution.py:103
  120.1 10.2 %all-to-all-done.3 = bf16[16,48,128]{2,1,0:T(8,128)(2,1)S(1)} async-done(((bf16[16,48,128]{2,1,0:T(8,128)(2,1)}), bf16[16,48,128]{2,1,0:T(8,128)(2,1)S(1)}, u32[]{:S(2)}, u32[]{:S(2)}) %all-to-all-start.3) | async-done | bytes 196640 | tf_op jit(solution)/shard_map/all_to_all | solution.py:39
  134.2 1.3 fusion.15
  135.5 1.0 copy.19
  (39 shorter events, 7.8 us)
Async XLA Ops:
  0.6 1.6 %copy-start = (bf16[1024,1024]{1,0:T(8,128)(2,1)S(1)}, bf16[1024,1024]{1,0:T(8,128)(2,1)}, u32[]{:S(2)}) copy-start(bf16[1024,1024]{1,0:T(8,128)(2,1)} %param.7) | copy-start | bytes 6291460
  0.6 4.5 %copy-start.3 = (bf16[99,1024]{1,0:T(8,128)(2,1)S(1)}, bf16[99,1024]{1,0:T(8,128)(2,1)}, u32[]{:S(2)}) copy-start(bf16[99,1024]{1,0:T(8,128)(2,1)} %param.8) | copy-start | bytes 608260
  0.7 14.2 %copy-start.6 = (f32[99]{0:T(128)S(1)}, f32[99]{0:T(128)}, u32[]{:S(2)}) copy-start(f32[99]{0:T(128)} %param.11) | copy-start | bytes 1192
  0.7 14.3 %copy-start.5 = (f32[256]{0:T(256)S(1)}, f32[256]{0:T(256)}, u32[]{:S(2)}) copy-start(f32[256]{0:T(256)} %param.10) | copy-start | bytes 3076
  2.2 15.8 %copy-start.4 = (f32[99,256]{1,0:T(8,128)S(1)}, f32[99,256]{1,0:T(8,128)}, u32[]{:S(2)}) copy-start(f32[99,256]{1,0:T(8,128)} %param.9) | copy-start | bytes 304132
  5.1 26.8 %copy-start.2 = (bf16[1,1024,256]{2,1,0:T(8,128)(2,1)S(1)}, bf16[1,1024,256]{2,1,0:T(8,128)(2,1)}, u32[]{:S(2)}) copy-start(bf16[1,1024,256]{2,1,0:T(8,128)(2,1)} %param.6) | copy-start | bytes 1572868
  6.0 19.9 %all-to-all-start = ((f32[16,8,256]{2,1,0:T(8,128)}), f32[16,8,256]{2,1,0:T(8,128)S(1)}, u32[]{:S(2)}, u32[]{:S(2)}) async-start(f32[16,8,256]{2,1,0:T(8,128)} %convolution_bitcast_fusion.1), calls=%async_computation | async-start | bytes 262144 | tf_op jit(solution)/shard_map/all_to_all | solution.py:39
  28.4 14.1 %all-to-all-start.1 = ((bf16[16,8,256]{2,1,0:T(8,128)(2,1)}), bf16[16,8,256]{2,1,0:T(8,128)(2,1)S(1)}, u32[]{:S(2)}, u32[]{:S(2)}) async-start(bf16[16,8,256]{2,1,0:T(8,128)(2,1)} %get-tuple-element.33), calls=%async_computation.1 | async-start | bytes 131072 | tf_op jit(solution)/shard_map/all_to_all | solution.py:39
  46.7 4.7 %collective-permute-start = (bf16[512,1152]{1,0:T(8,128)(2,1)S(1)}, bf16[512,1152]{1,0:T(8,128)(2,1)S(1)}, u32[]{:S(2)}, u32[]{:S(2)}) collective-permute-start(bf16[512,1152]{1,0:T(8,128)(2,1)S(1)} %pad_maximum_fusion), channel_id=1, source_target_pairs={{0,1},{1,0},{2,3},{3,2},{4,5},{5,4},{6,7},{7,6},{8,9},{9,8},{10,11... | collective-permute-start | bytes 3538952 | tf_op jit(solution)/shard_map/ppermute | solution.py:130
  51.5 1.0 copy-start.1
  114.9 15.4 %all-to-all-start.3 = ((bf16[16,48,128]{2,1,0:T(8,128)(2,1)}), bf16[16,48,128]{2,1,0:T(8,128)(2,1)S(1)}, u32[]{:S(2)}, u32[]{:S(2)}) async-start(bf16[16,48,128]{2,1,0:T(8,128)(2,1)} %pad_maximum_fusion.2), calls=%async_computation.3 | async-start | bytes 393216 | tf_op jit(solution)/shard_map/all_to_all | solution.py:39

commit v2 on v0

v2 whole, which is shorter than its diff:
```python
import functools

import jax
import jax.numpy as jnp
from jax import lax
from jax.experimental import pallas as pl
from jax.experimental.pallas import tpu as pltpu
from jax.sharding import Mesh, PartitionSpec as P

VARS = 99
PAD = 128
HALF = PAD // 2
SPARE = VARS + 1
ENS = ("y", "xh")
PLANE = ("xl", "z")
CHIP_X = ("xh", "xl")
BLOCK = 256

smooth_sq = 0.01
gelu_c = 0.7978845608
gelu_k = 0.044715
f32 = jnp.float32
bf16 = jnp.bfloat16
NT = (((1,), (1,)), ((), ()))


def gelu_value(value):
    inner = jnp.tanh(gelu_c * (value + gelu_k * value * value * value))
    return 0.5 * value * (1.0 + inner)


def gelu_slope(value):
    inner = jnp.tanh(gelu_c * (value + gelu_k * value * value * value))
    return 0.5 * (1.0 + inner) + 0.5 * value * (1.0 - inner * inner) * gelu_c * (
        1.0 + 3.0 * gelu_k * value * value
    )


def exchange(pieces, axes):
    return lax.all_to_all(pieces, axes, split_axis=0, concat_axis=0, tiled=True)


def dot(a, b):
    return jnp.dot(a, b, preferred_element_type=f32)


def dot_nt(a, b):
    return lax.dot_general(a, b, NT, preferred_element_type=f32)


def whole():
    return pl.BlockSpec(memory_space=pltpu.VMEM)


def smem():
    return pl.BlockSpec(memory_space=pltpu.SMEM)


def params(mib):
    return pltpu.CompilerParams(vmem_limit_bytes=mib << 20)


def lanes(shape):
    return lax.broadcasted_iota(jnp.int32, shape, len(shape) - 1)


def forward_kernel(w_in, latent, w_out, hidden, preact, decoded):
    step = pl.program_id(0)

    @pl.when(step == 0)
    def _():
        decoded[...] = jnp.zeros_like(decoded)

    value = dot(w_in[...], latent[...])
    preact[...] = value
    rounded = gelu_value(value).astype(bf16)
    hidden[...] = rounded
    decoded[0:VARS, :] += dot(w_out[...], rounded)


def forward(w_in, latent, w_out):
    hid, lat = w_in.shape
    pts = latent.shape[1]
    return pl.pallas_call(
        forward_kernel,
        grid=(hid // BLOCK,),
        in_specs=[
            pl.BlockSpec((BLOCK, lat), lambda i: (i, 0)),
            pl.BlockSpec((lat, pts), lambda i: (0, 0)),
            pl.BlockSpec((VARS, BLOCK), lambda i: (0, i)),
        ],
        out_specs=[
            pl.BlockSpec((BLOCK, pts), lambda i: (i, 0)),
            pl.BlockSpec((BLOCK, pts), lambda i: (i, 0)),
            pl.BlockSpec((PAD, pts), lambda i: (0, 0)),
        ],
        out_shape=[
            jax.ShapeDtypeStruct((hid, pts), bf16),
            jax.ShapeDtypeStruct((hid, pts), f32),
            jax.ShapeDtypeStruct((PAD, pts), f32),
        ],
        compiler_params=params(16),
        name="forward",
    )(w_in, latent, w_out)


def pairs_kernel(members, cores, fields, target, area, weight_own, dout, sums):
    count = float(members)
    weight = area[...] * weight_own[...]
    slopes = [None] * members
    total = None
    for m in range(1, members):
        for k in range(m):
            diff = fields[m] - fields[k]
            square = diff * diff + smooth_sq
            inverse = lax.rsqrt(square)
            slope = diff * inverse
            apart = square * inverse
            total = apart if total is None else total + apart
            slopes[m] = slope if slopes[m] is None else slopes[m] + slope
            slopes[k] = -slope if slopes[k] is None else slopes[k] - slope
    total = 2.0 * total + count * smooth_sq**0.5
    local = total * (-1.0 / (2.0 * count * (count - 1.0)))
    for m in range(members):
        miss = fields[m] - target[...]
        square = miss * miss + smooth_sq
        inverse = lax.rsqrt(square)
        local = local + square * inverse * (1.0 / count)
        value = weight * (
            miss * inverse * (1.0 / count) - slopes[m] * (1.0 / (count * (count - 1.0)))
        )
        for c in range(cores):
            dout[m * cores + c] = value.astype(bf16)
    loss = jnp.sum(weight * local, keepdims=True)
    here = jnp.sum(area[...], keepdims=True)
    lane = lanes(sums.shape)
    sums[...] = jnp.where(lane == 0, loss, jnp.where(lane == 1, here, 0.0))


def pairs(fields, target, area, weight_own, cores):
    members, own, pts = fields.shape
    return pl.pallas_call(
        functools.partial(pairs_kernel, members, cores),
        in_specs=[whole()] * 4,
        out_specs=[whole()] * 2,
        out_shape=[
            jax.ShapeDtypeStruct((members * cores, own, pts), bf16),
            jax.ShapeDtypeStruct((8, PAD), f32),
        ],
        compiler_params=params(8),
        name="pairs",
    )(fields, target, area, weight_own)


def backward_kernel(
    steps, core, dout, sums, sums_far, w_out_t, slope, slope_far,
    latent, latent_far, hidden, hidden_far, terms, dpre_out, dout_near, dout_far,
):
    step = pl.program_id(0)
    me = core[0]
    rows = terms.shape[1]

    def spread(which):
        value = dout[:, pl.ds(which, 1)].astype(f32)
        return value.reshape(PAD, dout.shape[-1]).astype(bf16)

    @pl.when(step == 0)
    def _():
        dout_near[...] = spread(me)
        dout_far[...] = spread(1 - me)

    def rows_of(ref, part, parts):
        value = ref[:, pl.ds(part, parts)]
        return value.reshape(-1, value.shape[-1])

    @pl.when(step < steps)
    def _():
        first = second = None
        for half, feats in ((slope, latent), (slope_far, latent_far)):
            near = half is slope
            dh = dot(w_out_t[...], (dout_near if near else dout_far)[...])
            dpre = (dh * half[...]).astype(bf16)
            if near:
                dpre_out[...] = dpre
            swapped = jnp.concatenate(
                [
                    dpre[at + off : at + off + HALF]
                    for at in range(0, BLOCK, PAD)
                    for off in (HALF, 0)
                ],
                0,
            )
            a = dot_nt(rows_of(feats, 2 * me, 1), dpre)
            b = dot_nt(rows_of(feats, 2 * me + 1, 1), swapped)
            first = a if first is None else first + a
            second = b if second is None else second + b
        low = lax.rem(lanes(first.shape), PAD) < HALF
        for xh, value in enumerate(
            (jnp.where(low, first, second), jnp.where(low, second, first))
        ):
            for xl in range(2):
                terms[2 * xh + xl] = value[xl * rows : (xl + 1) * rows].astype(bf16)

    @pl.when(step == steps)
    def _():
        out = dot_nt(rows_of(hidden, 2 * me, 2), dout_near[...])
        out += dot_nt(rows_of(hidden_far, 2 * me, 2), dout_far[...])
        out = out.reshape(-1, 2, 16, PAD)
        left = out[:, 0].reshape(-1, PAD)
        right = out[:, 1].reshape(-1, PAD)
        both = sums[0:1, :] + sums_far[0:1, :]
        lane = lanes(both.shape)
        high = both.astype(bf16).astype(f32)
        low = both - high
        parts = jnp.zeros_like(both)
        for k in range(2):
            for j, part in enumerate((high, low)):
                value = jnp.sum(jnp.where(lane == k, part, 0.0), axis=1, keepdims=True)
                parts = jnp.where(lane == SPARE + 2 * k + j, value, parts)
        row = lax.broadcasted_iota(jnp.int32, left.shape, 0)
        left = left + jnp.where(lax.rem(row, 16) == 0, parts, 0.0)
        for xh in range(2):
            for xl in range(2):
                at = slice(xl * rows, (xl + 1) * rows)
                terms[2 * xh + xl, :, 0:PAD] = left[at].astype(bf16)
                terms[2 * xh + xl, :, PAD : 2 * PAD] = right[at].astype(bf16)


def backward(core, dout, sums, sums_far, w_out_t, slope, slope_far, latent, latent_far, hidden, hidden_far):
    hid, pts = slope.shape
    plane = latent.shape[0]
    steps = hid // BLOCK
    rows = plane * 16 // 2
    keep = lambda *shape: pl.BlockSpec(shape, lambda i: (0,) * len(shape))
    block = lambda i: (jnp.minimum(i, steps - 1), 0)
    return pl.pallas_call(
        functools.partial(backward_kernel, steps),
        grid=(steps + 1,),
        in_specs=[
            smem(),
            keep(*dout.shape),
            keep(*sums.shape),
            keep(*sums.shape),
            pl.BlockSpec((BLOCK, PAD), block),
            pl.BlockSpec((BLOCK, pts), block),
            pl.BlockSpec((BLOCK, pts), block),
            keep(*latent.shape),
            keep(*latent.shape),
            keep(*hidden.shape),
            keep(*hidden.shape),
        ],
        out_specs=[
            pl.BlockSpec((4, rows, 2 * PAD), lambda i: (0, 0, i)),
            pl.BlockSpec((BLOCK, pts), block),
        ],
        out_shape=[
            jax.ShapeDtypeStruct((4, rows, hid + 2 * PAD), bf16),
            jax.ShapeDtypeStruct((hid, pts), bf16),
        ],
        scratch_shapes=[pltpu.VMEM((PAD, pts), bf16)] * 2,
        compiler_params=params(24),
        name="backward",
    )(core, dout, sums, sums_far, w_out_t, slope, slope_far, latent, latent_far, hidden, hidden_far)


def split_again(tile):
    lane = lanes(tile.shape)
    value = tile + pltpu.roll(tile, PAD - 1, 1)
    high = value.astype(bf16).astype(f32)
    low = pltpu.roll(value - high, 1, 1)
    odd = (lane == SPARE + 1) | (lane == SPARE + 3)
    even = (lane == SPARE) | (lane == SPARE + 2)
    return jnp.where(even, high, jnp.where(odd, low, tile))


def add_x_kernel(hid, got, out):
    value = got[0].astype(f32)
    for k in range(1, got.shape[0]):
        value = value + got[k].astype(f32)
    out[:, 0:hid] = value[:, 0:hid].astype(bf16)
    out[:, hid : hid + PAD] = split_again(value[:, hid : hid + PAD]).astype(bf16)
    out[:, hid + PAD :] = value[:, hid + PAD :].astype(bf16)


def add_x(got, hid):
    return pl.pallas_call(
        functools.partial(add_x_kernel, hid),
        in_specs=[whole()],
        out_specs=whole(),
        out_shape=jax.ShapeDtypeStruct(got.shape[1:], bf16),
        compiler_params=params(8),
        name="add_x",
    )(got)


def add_z_kernel(hid, got, out):
    value = got[0].astype(f32)
    for k in range(1, got.shape[0]):
        value = value + got[k].astype(f32)
    left = split_again(value[:, hid : hid + PAD]).astype(bf16)
    right = value[:, hid + PAD :].astype(bf16)
    for y in range(out.shape[0]):
        out[y, :, 0:PAD] = value[:, y * PAD : (y + 1) * PAD].astype(bf16)
        out[y, :, PAD : 2 * PAD] = left
        out[y, :, 2 * PAD :] = right


def add_z(got, hid):
    return pl.pallas_call(
        functools.partial(add_z_kernel, hid),
        in_specs=[whole()],
        out_specs=whole(),
        out_shape=jax.ShapeDtypeStruct((hid // PAD, got.shape[1], 3 * PAD), bf16),
        compiler_params=params(4),
        name="add_z",
    )(got)


def finish_kernel(count, points_all, turn, got, grad, loss, grad_lat, grad_in, grad_out, factor):
    @pl.when(pl.program_id(0) == 0)
    def _():
        value = got[0].astype(f32)
        for k in range(1, got.shape[0]):
            value = value + got[k].astype(f32)
        left = value[:, PAD : 2 * PAD]
        head = left[0:1, :]
        lane = lanes(head.shape)

        def pick(at):
            mine = (lane == at) | (lane == at + 1)
            return jnp.sum(jnp.where(mine, head, 0.0), axis=1, keepdims=True)

        weight_total = pick(SPARE + 2) * (1.0 / count)
        scale = 1.0 / (weight_total * VARS)
        loss[...] = pick(SPARE) * scale
        scale = points_all * scale
        factor[...] = jnp.broadcast_to(scale, factor.shape)
        ratio = scale * (1.0 / (points_all * count) ** 0.5)
        tile = value[:, 0:PAD] * ratio
        other = pltpu.roll(tile, HALF, 1)
        even = turn[0] == 0
        grad_in[0:16, :] = jnp.where(even, tile, other)[:, 0:HALF]
        grad_in[16:32, :] = jnp.where(even, other, tile)[:, 0:HALF]
        grad_out[0:16, :] = (left * ratio)[:, 0:VARS]
        grad_out[16:32, :] = (value[:, 2 * PAD :] * ratio)[:, 0:VARS]

    grad_lat[...] = (grad[...] * factor[0:1, 0:1]).astype(bf16)


def finish(turn, got, grad, count, points_all):
    lat, pts = grad.shape
    keep = lambda *shape: pl.BlockSpec(shape, lambda i: (0,) * len(shape))
    return pl.pallas_call(
        functools.partial(finish_kernel, count, points_all),
        grid=(lat // BLOCK,),
        in_specs=[
            smem(),
            keep(*got.shape),
            pl.BlockSpec((BLOCK, pts), lambda i: (i, 0)),
        ],
        out_specs=[
            keep(1, 1),
            pl.BlockSpec((BLOCK, pts), lambda i: (i, 0)),
            keep(32, HALF),
            keep(32, VARS),
        ],
        out_shape=[
            jax.ShapeDtypeStruct((1, 1), f32),
            jax.ShapeDtypeStruct((lat, pts), bf16),
            jax.ShapeDtypeStruct((32, HALF), f32),
            jax.ShapeDtypeStruct((32, VARS), f32),
        ],
        scratch_shapes=[pltpu.VMEM((8, PAD), f32)],
        compiler_params=params(8),
        name="finish",
    )(turn, got, grad)


def per_device(latent, w_in, w_out, target, area, var_weight):
    n_ens = lax.axis_size(ENS)
    n_plane = lax.axis_size(PLANE)
    n_core = lax.axis_size("c")
    n_z = lax.axis_size("z")
    pts = area.shape[0]
    hid, lat = w_in.shape
    own = PAD // n_ens
    me = lax.axis_index(ENS)
    core = lax.axis_index("c")
    swap = [(0, 1), (1, 0)]
    features = latent[0]

    hidden, preact, decoded = forward(w_in, features, w_out)

    fields = exchange(decoded.reshape(n_ens, own, pts), ENS)
    features_late, preact_late, _ = lax.optimization_barrier((features, preact, decoded))
    far = lax.ppermute(features_late, "c", swap)
    slope = gelu_slope(preact_late)
    target_own = lax.dynamic_slice_in_dim(
        jnp.pad(target, ((0, PAD - VARS), (0, 0))), me * own, own
    )
    weight_own = lax.dynamic_slice_in_dim(
        jnp.pad(var_weight, (0, PAD - VARS)), me * own, own
    )
    dout, sums = pairs(fields, target_own, area[None, :], weight_own[:, None], n_core)

    dout_got = exchange(dout, ENS + ("c",))
    sums_far = lax.ppermute(sums, "c", swap)
    far_late, _ = lax.optimization_barrier((far, dout))
    preact_far = dot(w_in, far_late)
    hidden_far = gelu_value(preact_far).astype(bf16)
    slope_far = gelu_slope(preact_far)
    w_out_t = jnp.pad(w_out, ((0, PAD - VARS), (0, 0))).T

    groups = lambda value: value.reshape(n_plane, 2 * n_core, 16, pts)
    terms, dpre = backward(
        core.astype(jnp.int32)[None],
        dout_got.reshape(n_ens, n_core, own, pts),
        sums, sums_far, w_out_t, slope, slope_far,
        groups(features), groups(far_late), groups(hidden), groups(hidden_far),
    )

    got = exchange(terms, CHIP_X)
    grad = lax.dot_general(
        w_in, dpre, (((0,), (0,)), ((), ())), preferred_element_type=f32
    )
    got = exchange(add_x(got, hid).reshape(n_z, 16, hid + 2 * PAD), "z")
    got = exchange(add_z(got, hid), "y")
    loss, grad_lat, grad_in, grad_out = finish(
        lax.axis_index("xh").astype(jnp.int32)[None],
        got, grad, float(n_ens), float(n_plane * n_core * pts),
    )
    return loss[0, 0], grad_lat[None], grad_in.T, grad_out.T


def solution(mesh):
    ens, grid_all = mesh.devices.shape
    split = (ens // 2, 2, 2, grid_all // 4, 2)
    fine = Mesh(mesh.devices.reshape(split), ENS + PLANE + ("c",))
    grid = PLANE + ("c",)
    in_specs = (P(ENS, None, grid), P(), P(), P(None, grid), P(grid), P())
    out_specs = (P(), P(ENS, None, grid), P(ENS, grid), P(None, grid))
    return jax.shard_map(
        per_device, mesh=fine, in_specs=in_specs, out_specs=out_specs, check_vma=False
    )
```

time: 741 us -> 112 us (0.15)
  the two profiles are of different devices: /device:TPU:12 before, /device:TPU:2 now
where the time goes in v2:
time: 112 us; the launch traced here: 111 us
  blocking collectives  43.9 us (39%)
  starting transfers between devices  20.1 us (18%)
  waiting for transfers between devices  18.7 us (17%)
  Pallas kernels  10.7 us (10%)
  local copies, waits for them, and re-layouts  9.38 us (8%)
  matrix products  5.38 us (5%)
  other arithmetic  1.84 us (2%)
    all_to_all x2, blocking collectives, exchange(): return lax.all_to_all(pieces, axes, split_axis=0, concat_axis=0, tiled=True)  43.9 us
    all_to_all x3, waiting for transfers between devices, exchange(): return lax.all_to_all(pieces, axes, split_axis=0, concat_axis=0, tiled=True)  18.7 us
    all_to_all x3, starting transfers between devices, exchange(): return lax.all_to_all(pieces, axes, split_axis=0, concat_axis=0, tiled=True)  16.1 us
    unnamed x29, local copies, waits for them, and re-layouts  9.16 us
    pallas_call x1, Pallas kernels, forward(): pl.pallas_call(forward_kernel, grid=(hid // BLOCK,), in_specs=[pl.BlockSp...  3.85 us
    pallas_call x1, Pallas kernels, backward(): pl.pallas_call(functools.partial(backward_kernel, steps), grid=(steps + 1...  3.7 us
    dot_general x1, matrix products, dot(): return jnp.dot(a, b, preferred_element_type=f32)  3.41 us
  transfers between devices with their start and end apart: 5, of which 3 were waited for; matrix products, arithmetic and copies ran while one was open for 7% of the time, Pallas kernels for 0%

profile of v2, /device:TPU:2, one launch (start us, length us, event | category | flops | bytes accessed | tf_op | source)
XLA Modules:
  0.0 110.8 jit_solution(12947940607815264248)
XLA Ops:
  0.7 1.6 %copy-done = bf16[1024,1024]{1,0:T(8,128)(2,1)S(1)} copy-done((bf16[1024,1024]{1,0:T(8,128)(2,1)S(1)}, bf16[1024,1024]{1,0:T(8,128)(2,1)}, u32[]{:S(2)}) %copy-start) | copy-done | bytes 2097176
  2.2 0.9 copy-done.4
  3.2 3.9 %forward.1 = (bf16[1024,256]{1,0:T(8,128)(2,1)S(1)}, f32[1024,256]{1,0:T(8,128)S(1)}, f32[128,256]{1,0:T(8,128)}) custom-call(bf16[1024,1024]{1,0:T(8,128)(2,1)S(1)} %copy-done, bf16[1024,256]{1,0:T(8,128)(2,1)} %bitcast.2.latent, bf16[99,1024]{1,0:T(8,128)(2,1)S(1)} %copy-done.4), custom_call_target="tpu_custom_call" | custom-call | tf_op jit(solution)/shard_map/forward/pallas_call | solution.py:84
  7.0 1.0 copy-done.3
  8.1 0.8 copy-done.6
  8.8 8.9 %all-to-all-start = ((f32[16,8,256]{2,1,0:T(8,128)}), f32[16,8,256]{2,1,0:T(8,128)S(1)}, u32[]{:S(2)}, u32[]{:S(2)}) async-start(f32[16,8,256]{2,1,0:T(8,128)} %bitcast.3), calls=%async_computation | async-start | bytes 262144 | tf_op jit(solution)/shard_map/all_to_all | solution.py:40
  17.8 1.9 %collective-permute-start.1 = (bf16[1024,256]{1,0:T(8,128)(2,1)}, bf16[1024,256]{1,0:T(8,128)(2,1)}, u32[]{:S(2)}, u32[]{:S(2)}) collective-permute-start(bf16[1024,256]{1,0:T(8,128)(2,1)} %bitcast.2.latent), channel_id=1, source_target_pairs={{0,1},{1,0},{2,3},{3,2},{4,5},{5,4},{6,7},{7,6},{8,9},{9,8},{10,11... | collective-permute-start | bytes 1572872 | tf_op jit(solution)/shard_map/ppermute | solution.py:396
  20.1 1.8 %fusion.4.slope = f32[1024,256]{1,0:T(8,128)S(1)} fusion(f32[1024,256]{1,0:T(8,128)} %copy-done.3), kind=kLoop, calls=%fused_computation.10 | loop fusion | flops 4456448 | bytes 2097152 | tf_op jit(solution)/shard_map/add | solution.py:34
  22.0 6.9 %all-to-all-done.fields = f32[16,8,256]{2,1,0:T(8,128)S(1)} async-done(((f32[16,8,256]{2,1,0:T(8,128)}), f32[16,8,256]{2,1,0:T(8,128)S(1)}, u32[]{:S(2)}, u32[]{:S(2)}) %all-to-all-start) | async-done | bytes 131104 | tf_op jit(solution)/shard_map/all_to_all | solution.py:40
  30.6 3.8 %all-to-all-start.1 = ((bf16[32,8,256]{2,1,0:T(8,128)(2,1)}), bf16[32,8,256]{2,1,0:T(8,128)(2,1)S(1)}, u32[]{:S(2)}, u32[]{:S(2)}) async-start(bf16[32,8,256]{2,1,0:T(8,128)(2,1)} %copy-done.10), calls=%async_computation.1 | async-start | bytes 262144 | tf_op jit(solution)/shard_map/all_to_all | solution.py:40
  34.5 2.1 %collective-permute-start = (f32[8,128]{1,0:T(8,128)S(1)}, f32[8,128]{1,0:T(8,128)S(1)}, u32[]{:S(2)}, u32[]{:S(2)}) collective-permute-start(f32[8,128]{1,0:T(8,128)S(1)} %get-tuple-element.20.sums), channel_id=1, source_target_pairs={{0,1},{1,0},{2,3},{3,2},{4,5},{5,4},{6,7},{7,6},{8,9},{9,8},{10,11... | collective-permute-start | bytes 12296 | tf_op jit(solution)/shard_map/ppermute | solution.py:407
  36.6 3.4 %multiply_convert_fusion = (bf16[1024,256]{1,0:T(8,128)(2,1)}, f32[1024,256]{1,0:T(8,128)}) fusion(bf16[1024,1024]{1,0:T(8,128)(2,1)S(1)} %copy-done.1, bf16[1024,256]{1,0:T(8,128)(2,1)} %collective-permute-done.1), kind=kOutput, calls=%fused_computation.16 | convolution fusion | flops 541851648 | bytes 4194304 | tf_op jit(solution)/shard_map/dot_general | solution.py:44
  40.0 5.1 %all-to-all-done.1 = bf16[32,8,256]{2,1,0:T(8,128)(2,1)S(1)} async-done(((bf16[32,8,256]{2,1,0:T(8,128)(2,1)}), bf16[32,8,256]{2,1,0:T(8,128)(2,1)S(1)}, u32[]{:S(2)}, u32[]{:S(2)}) %all-to-all-start.1) | async-done | bytes 131104 | tf_op jit(solution)/shard_map/all_to_all | solution.py:40
  45.1 1.2 %copy-done.2 = f32[1024,256]{1,0:T(8,128)S(1)} copy-done((f32[1024,256]{1,0:T(8,128)S(1)}, f32[1024,256]{1,0:T(8,128)}, u32[]{:S(2)}) %copy-start.2) | copy-done | bytes 1048600
  46.4 1.0 copy-done.7
  47.4 1.0 copy-done.9
  48.4 3.7 %backward.1 = (bf16[4,128,1280]{2,1,0:T(8,128)(2,1)S(1)}, bf16[1024,256]{1,0:T(8,128)(2,1)S(1)}) custom-call(s32[1]{0:T(128)} %bitcast.1.core, bf16[16,2,8,256]{3,2,1,0:T(8,128)(2,1)S(1)} %bitcast.30, f32[8,128]{1,0:T(8,128)S(1)} %get-tuple-element.20.sums, f32[8,128]{1,0:T(8,128)S(1)} %collective-permute-done.sums_far, ...), custom_call_target="tpu_custom_call" | custom-call | tf_op jit(solution)/shard_map/backward/pallas_call | solution.py:236
  52.1 21.2 %all_to_all.25.got = bf16[4,128,1280]{2,1,0:T(8,128)(2,1)S(1)} all-to-all(bf16[4,128,1280]{2,1,0:T(8,128)(2,1)S(1)} %get-tuple-element.26), channel_id=1, replica_groups=mesh['y'=8,'xh'=2,'xl'=2,'z'=8,'c'=2] {'xh','xl'}, dimensions={0} | all-to-all | bytes 2621440 | tf_op jit(solution)/shard_map/all_to_all | solution.py:40
  73.7 22.7 %all_to_all.26.got = bf16[8,16,1280]{2,1,0:T(8,128)(2,1)S(1)} all-to-all(bf16[8,16,1280]{2,1,0:T(8,128)(2,1)S(1)} %bitcast.27), channel_id=1, replica_groups=mesh['y'=8,'xh'=2,'xl'=2,'z'=8,'c'=2] {'z'}, dimensions={0} | all-to-all | bytes 655360 | tf_op jit(solution)/shard_map/all_to_all | solution.py:40
  96.3 0.8 add_z.1
  97.1 3.4 %all-to-all-start.4 = ((bf16[8,16,384]{2,1,0:T(8,128)(2,1)}), bf16[8,16,384]{2,1,0:T(8,128)(2,1)S(1)}, u32[]{:S(2)}, u32[]{:S(2)}) async-start(bf16[8,16,384]{2,1,0:T(8,128)(2,1)} %add_z.1), calls=%async_computation.4 | async-start | bytes 196608 | tf_op jit(solution)/shard_map/all_to_all | solution.py:40
  100.5 2.0 %convolution_bitcast_fusion.1.grad = f32[1024,256]{1,0:T(8,128)S(1)} fusion(bf16[1024,256]{1,0:T(8,128)(2,1)} %copy-done.8, bf16[1024,1024]{1,0:T(8,128)(2,1)S(1)} %copy-done.1), kind=kOutput, calls=%fused_computation.5 | convolution fusion | flops 536870912 | bytes 3670016 | tf_op jit(solution)/shard_map/dot_general | solution.py:423
  102.5 6.7 %all-to-all-done.4.got = bf16[8,16,384]{2,1,0:T(8,128)(2,1)S(1)} async-done(((bf16[8,16,384]{2,1,0:T(8,128)(2,1)}), bf16[8,16,384]{2,1,0:T(8,128)(2,1)S(1)}, u32[]{:S(2)}, u32[]{:S(2)}) %all-to-all-start.4) | async-done | bytes 98336 | tf_op jit(solution)/shard_map/all_to_all | solution.py:40
  109.1 1.7 %finish.1 = (f32[1,1]{1,0:T(1,128)}, bf16[1024,256]{1,0:T(8,128)(2,1)}, f32[32,64]{1,0:T(8,128)}, f32[32,99]{1,0:T(8,128)}) custom-call(s32[1]{0:T(128)} %bitcast.turn, bf16[8,16,384]{2,1,0:T(8,128)(2,1)S(1)} %all-to-all-done.4.got, f32[1024,256]{1,0:T(8,128)S(1)} %convolution_bitcast_fusion.1.grad), custom_call_target="tpu_custom_call" | custom-call | tf_op jit(solution)/shard_map/finish/pallas_call | solution.py:353
  (30 shorter events, 2.5 us)
Async XLA Ops:
  0.6 19.1 %copy-start.13 = (f32[99]{0:T(128)S(1)}, f32[99]{0:T(128)}, u32[]{:S(2)}) copy-start(f32[99]{0:T(128)} %param.11) | copy-start | bytes 1192
  0.6 1.6 %copy-start = (bf16[1024,1024]{1,0:T(8,128)(2,1)S(1)}, bf16[1024,1024]{1,0:T(8,128)(2,1)}, u32[]{:S(2)}) copy-start(bf16[1024,1024]{1,0:T(8,128)(2,1)} %w_in.1) | copy-start | bytes 6291460
  2.2 0.9 copy-start.4
  3.2 16.6 %copy-start.5 = (bf16[99,1024]{1,0:T(8,128)(2,1)S(1)}, bf16[99,1024]{1,0:T(8,128)(2,1)}, u32[]{:S(2)}) copy-start(bf16[99,1024]{1,0:T(8,128)(2,1)} %w_out.1) | copy-start | bytes 608260
  3.2 16.9 %copy-start.12 = (f32[99,256]{1,0:T(8,128)S(1)}, f32[99,256]{1,0:T(8,128)}, u32[]{:S(2)}) copy-start(f32[99,256]{1,0:T(8,128)} %param.9) | copy-start | bytes 304132
  7.0 1.0 copy-start.3
  8.0 0.8 copy-start.6
  8.8 27.7 %copy-start.1 = (bf16[1024,1024]{1,0:T(8,128)(2,1)S(1)}, bf16[1024,1024]{1,0:T(8,128)(2,1)}, u32[]{:S(2)}) copy-start(bf16[1024,1024]{1,0:T(8,128)(2,1)} %w_in.1) | copy-start | bytes 6291460
  8.8 20.0 %all-to-all-start = ((f32[16,8,256]{2,1,0:T(8,128)}), f32[16,8,256]{2,1,0:T(8,128)S(1)}, u32[]{:S(2)}, u32[]{:S(2)}) async-start(f32[16,8,256]{2,1,0:T(8,128)} %bitcast.3), calls=%async_computation | async-start | bytes 262144 | tf_op jit(solution)/shard_map/all_to_all | solution.py:40
  17.8 18.8 %collective-permute-start.1 = (bf16[1024,256]{1,0:T(8,128)(2,1)}, bf16[1024,256]{1,0:T(8,128)(2,1)}, u32[]{:S(2)}, u32[]{:S(2)}) collective-permute-start(bf16[1024,256]{1,0:T(8,128)(2,1)} %bitcast.2.latent), channel_id=1, source_target_pairs={{0,1},{1,0},{2,3},{3,2},{4,5},{5,4},{6,7},{7,6},{8,9},{9,8},{10,11... | collective-permute-start | bytes 1572872 | tf_op jit(solution)/shard_map/ppermute | solution.py:396
  28.9 0.7 copy-start.11
  30.0 0.7 copy-start.10
  30.6 14.5 %all-to-all-start.1 = ((bf16[32,8,256]{2,1,0:T(8,128)(2,1)}), bf16[32,8,256]{2,1,0:T(8,128)(2,1)S(1)}, u32[]{:S(2)}, u32[]{:S(2)}) async-start(bf16[32,8,256]{2,1,0:T(8,128)(2,1)} %copy-done.10), calls=%async_computation.1 | async-start | bytes 262144 | tf_op jit(solution)/shard_map/all_to_all | solution.py:40
  34.5 5.5 %collective-permute-start = (f32[8,128]{1,0:T(8,128)S(1)}, f32[8,128]{1,0:T(8,128)S(1)}, u32[]{:S(2)}, u32[]{:S(2)}) collective-permute-start(f32[8,128]{1,0:T(8,128)S(1)} %get-tuple-element.20.sums), channel_id=1, source_target_pairs={{0,1},{1,0},{2,3},{3,2},{4,5},{5,4},{6,7},{7,6},{8,9},{9,8},{10,11... | collective-permute-start | bytes 12296 | tf_op jit(solution)/shard_map/ppermute | solution.py:407
  45.1 1.2 %copy-start.2 = (f32[1024,256]{1,0:T(8,128)S(1)}, f32[1024,256]{1,0:T(8,128)}, u32[]{:S(2)}) copy-start(f32[1024,256]{1,0:T(8,128)} %get-tuple-element.33.slope_far) | copy-start | bytes 3145732
  46.3 1.0 copy-start.7
  47.4 1.0 copy-start.9
  52.1 21.5 %copy-start.8 = (bf16[1024,256]{1,0:T(8,128)(2,1)}, bf16[1024,256]{1,0:T(8,128)(2,1)S(1)}, u32[]{:S(2)}) copy-start(bf16[1024,256]{1,0:T(8,128)(2,1)S(1)} %get-tuple-element.27) | copy-start | bytes 1572868
  97.1 12.0 %all-to-all-start.4 = ((bf16[8,16,384]{2,1,0:T(8,128)(2,1)}), bf16[8,16,384]{2,1,0:T(8,128)(2,1)S(1)}, u32[]{:S(2)}, u32[]{:S(2)}) async-start(bf16[8,16,384]{2,1,0:T(8,128)(2,1)} %add_z.1), calls=%async_computation.4 | async-start | bytes 196608 | tf_op jit(solution)/shard_map/all_to_all | solution.py:40

commit v3 on v2

v3 whole, which is shorter than its diff:
```python
import functools

import jax
import jax.numpy as jnp
from jax import lax
from jax.experimental import pallas as pl
from jax.experimental.pallas import tpu as pltpu
from jax.sharding import Mesh, PartitionSpec as P

VARS = 99
PAD = 128
HALF = PAD // 2
OWN = 8
ENS = ("y", "xh")
PLANE = ("xl", "z")
CHIP_X = ("xh", "xl")
BLOCK = 256

smooth_sq = 0.01
gelu_c = 0.7978845608
gelu_k = 0.044715
f32 = jnp.float32
bf16 = jnp.bfloat16
NT = (((1,), (1,)), ((), ()))


def gelu_value(value):
    inner = jnp.tanh(gelu_c * (value + gelu_k * value * value * value))
    return 0.5 * value * (1.0 + inner)


def gelu_slope(value):
    inner = jnp.tanh(gelu_c * (value + gelu_k * value * value * value))
    return 0.5 * (1.0 + inner) + 0.5 * value * (1.0 - inner * inner) * gelu_c * (
        1.0 + 3.0 * gelu_k * value * value
    )


def exchange(pieces, axes):
    return lax.all_to_all(pieces, axes, split_axis=0, concat_axis=0, tiled=True)


def dot(a, b):
    return jnp.dot(a, b, preferred_element_type=f32)


def dot_nt(a, b):
    return lax.dot_general(a, b, NT, preferred_element_type=f32)


def whole():
    return pl.BlockSpec(memory_space=pltpu.VMEM)


def smem():
    return pl.BlockSpec(memory_space=pltpu.SMEM)


def hbm():
    return pl.BlockSpec(memory_space=pltpu.HBM)


def in_hbm(*arrays):
    return [pltpu.with_memory_space_constraint(array, pltpu.HBM) for array in arrays]


def params(mib):
    return pltpu.CompilerParams(vmem_limit_bytes=mib << 20)


class Copies:
    def __init__(self, sems):
        self.sems = sems
        self.used = 0
        self.open = []

    def start(self, source, target):
        copy = pltpu.make_async_copy(source, target, self.sems.at[self.used])
        self.used += 1
        copy.start()
        self.open.append(copy)
        return copy

    def wait(self, copy):
        copy.wait()
        self.open = [other for other in self.open if other is not copy]

    def finish(self):
        for copy in self.open:
            self.wait(copy)


def scratch(*shapes, copies):
    return [pltpu.VMEM(shape, kind) for shape, kind in shapes] + [
        pltpu.SemaphoreType.DMA((copies,))
    ]


def blocks(size):
    return [slice(at, at + BLOCK) for at in range(0, size, BLOCK)]


def spare(k):
    return OWN * (k + 1) - 1


def row_table():
    row = lax.broadcasted_iota(jnp.int32, (PAD, VARS), 0)
    held = lax.rem(row, OWN) < OWN - 1
    variable = lax.div(row, OWN) * (OWN - 1) + lax.rem(row, OWN)
    return held & (variable == lanes((PAD, VARS)))


def lanes(shape):
    return lax.broadcasted_iota(jnp.int32, shape, len(shape) - 1)


def forward_kernel(
    w_in, latent, w_out, hidden, preact, decoded,
    w_in_v, latent_v, w_out_v, hidden_v, preact_v, decoded_v, sems,
):
    copies = Copies(sems)
    parts = blocks(w_in.shape[0])
    first = [copies.start(latent, latent_v)]
    weights = [copies.start(w_in.at[here], w_in_v.at[here]) for here in parts[:1]]
    first.append(copies.start(w_out, w_out_v))
    weights += [copies.start(w_in.at[here], w_in_v.at[here]) for here in parts[1:]]
    for copy in first:
        copies.wait(copy)
    w_out_rows = dot(row_table().astype(bf16), w_out_v[...]).astype(bf16)
    total = None
    for here, weight in zip(parts, weights):
        copies.wait(weight)
        value = dot(w_in_v[here, :], latent_v[...])
        preact_v[here, :] = value
        copies.start(preact_v.at[here], preact.at[here])
        rounded = gelu_value(value).astype(bf16)
        hidden_v[here, :] = rounded
        copies.start(hidden_v.at[here], hidden.at[here])
        part = dot(w_out_rows[:, here], rounded)
        total = part if total is None else total + part
    decoded_v[...] = total
    copies.start(decoded_v, decoded)
    copies.finish()


def forward(w_in, latent, w_out):
    hid, lat = w_in.shape
    pts = latent.shape[1]
    count = len(blocks(hid))
    return pl.pallas_call(
        forward_kernel,
        in_specs=[hbm()] * 3,
        out_specs=[hbm()] * 3,
        out_shape=[
            pltpu.HBM((hid, pts), bf16),
            pltpu.HBM((hid, pts), f32),
            pltpu.HBM((PAD, pts), f32),
        ],
        scratch_shapes=scratch(
            ((hid, lat), bf16), ((lat, pts), bf16), ((VARS, hid), bf16),
            ((hid, pts), bf16), ((hid, pts), f32), ((PAD, pts), f32),
            copies=3 * count + 3,
        ),
        compiler_params=params(16),
        name="forward",
    )(*in_hbm(w_in, latent, w_out))


def far_kernel(w_in, latent, hidden, slope, w_in_v, latent_v, hidden_v, slope_v, sems):
    copies = Copies(sems)
    parts = blocks(w_in.shape[0])
    first = copies.start(latent, latent_v)
    weights = [copies.start(w_in.at[here], w_in_v.at[here]) for here in parts]
    copies.wait(first)
    for here, weight in zip(parts, weights):
        copies.wait(weight)
        value = dot(w_in_v[here, :], latent_v[...])
        hidden_v[here, :] = gelu_value(value).astype(bf16)
        copies.start(hidden_v.at[here], hidden.at[here])
        slope_v[here, :] = gelu_slope(value)
        copies.start(slope_v.at[here], slope.at[here])
    copies.finish()


def far_forward(w_in, latent):
    hid, lat = w_in.shape
    pts = latent.shape[1]
    return pl.pallas_call(
        far_kernel,
        in_specs=[hbm()] * 2,
        out_specs=[hbm()] * 2,
        out_shape=[
            pltpu.HBM((hid, pts), bf16),
            pltpu.HBM((hid, pts), f32),
        ],
        scratch_shapes=scratch(
            ((hid, lat), bf16), ((lat, pts), bf16), ((hid, pts), bf16), ((hid, pts), f32),
            copies=3 * len(blocks(hid)) + 1,
        ),
        compiler_params=params(16),
        cost_estimate=pl.CostEstimate(
            flops=2 * hid * lat * pts, bytes_accessed=4 << 20, transcendentals=hid * pts
        ),
        name="far_forward",
    )(*in_hbm(w_in), latent)


def slope_kernel(preact, w_out, slope, w_out_t, preact_v, w_out_v, slope_v, w_out_t_v, sems):
    copies = Copies(sems)
    parts = blocks(preact.shape[0])
    first = copies.start(w_out, w_out_v)
    inputs = [copies.start(preact.at[here], preact_v.at[here]) for here in parts]
    copies.wait(first)
    w_out_t_v[...] = lax.dot_general(
        w_out_v[...], row_table().astype(bf16), (((0,), (1,)), ((), ())), preferred_element_type=f32
    ).astype(bf16)
    copies.start(w_out_t_v, w_out_t)
    for here, copy in zip(parts, inputs):
        copies.wait(copy)
        slope_v[here, :] = gelu_slope(preact_v[here, :])
        copies.start(slope_v.at[here], slope.at[here])
    copies.finish()


def slopes(preact, w_out):
    hid, pts = preact.shape
    return pl.pallas_call(
        slope_kernel,
        in_specs=[hbm()] * 2,
        out_specs=[hbm()] * 2,
        out_shape=[
            pltpu.HBM((hid, pts), f32),
            pltpu.HBM((hid, PAD), bf16),
        ],
        scratch_shapes=scratch(
            ((hid, pts), f32), ((VARS, hid), bf16), ((hid, pts), f32), ((hid, PAD), bf16),
            copies=2 * len(blocks(hid)) + 2,
        ),
        compiler_params=params(16),
        cost_estimate=pl.CostEstimate(
            flops=20 * hid * pts, bytes_accessed=4 << 20, transcendentals=hid * pts
        ),
        name="slopes",
    )(*in_hbm(preact, w_out))


def grad_kernel(w_in, dpre, grad, w_in_v, dpre_v, grad_v, sems):
    copies = Copies(sems)
    inputs = [copies.start(dpre, dpre_v), copies.start(w_in, w_in_v)]
    for copy in inputs:
        copies.wait(copy)
    for here in blocks(w_in.shape[1]):
        grad_v[here, :] = lax.dot_general(
            w_in_v[:, here], dpre_v[...], (((0,), (0,)), ((), ())), preferred_element_type=f32
        )
    copies.start(grad_v, grad)
    copies.finish()


def grad_latent(w_in, dpre):
    hid, lat = w_in.shape
    pts = dpre.shape[1]
    return pl.pallas_call(
        grad_kernel,
        in_specs=[hbm()] * 2,
        out_specs=hbm(),
        out_shape=pltpu.HBM((lat, pts), f32),
        scratch_shapes=scratch(
            ((hid, lat), bf16), ((hid, pts), bf16), ((lat, pts), f32), copies=3
        ),
        compiler_params=params(16),
        cost_estimate=pl.CostEstimate(
            flops=2 * hid * lat * pts, bytes_accessed=4 << 20, transcendentals=0
        ),
        name="grad_latent",
    )(*in_hbm(w_in, dpre))


def pairs_kernel(
    members, cores, owner, fields, target_all, area_h, var_weight_h, dout,
    target_v, area_v, var_weight_v, dout_v, sems,
):
    copies = Copies(sems)
    inputs = [
        copies.start(area_h, area_v),
        copies.start(var_weight_h, var_weight_v),
        copies.start(target_all, target_v),
    ]
    count = float(members)
    own, pts = fields.shape[1:]
    slopes = [None] * members
    total = None
    for m in range(1, members):
        for k in range(m):
            diff = fields[m] - fields[k]
            square = diff * diff + smooth_sq
            inverse = lax.rsqrt(square)
            slope = diff * inverse
            apart = square * inverse
            total = apart if total is None else total + apart
            slopes[m] = slope if slopes[m] is None else slopes[m] + slope
            slopes[k] = -slope if slopes[k] is None else slopes[k] - slope
    total = 2.0 * total + count * smooth_sq**0.5
    local = total * (-1.0 / (2.0 * count * (count - 1.0)))
    for copy in inputs:
        copies.wait(copy)
    row = lax.broadcasted_iota(jnp.int32, (own, VARS), 0)
    held = (row < own - 1) & (lanes((own, VARS)) == owner[0] * (own - 1) + row)
    weight = jnp.sum(jnp.where(held, var_weight_v[...], 0.0), axis=1, keepdims=True)
    weight = area_v[...] * weight
    target = lax.dot_general(
        held.astype(f32), target_v[...], (((1,), (0,)), ((), ())),
        precision=lax.Precision.HIGHEST, preferred_element_type=f32,
    )
    values = []
    for m in range(members):
        miss = fields[m] - target
        square = miss * miss + smooth_sq
        inverse = lax.rsqrt(square)
        local = local + square * inverse * (1.0 / count)
        values.append(
            weight
            * (miss * inverse * (1.0 / count) - slopes[m] * (1.0 / (count * (count - 1.0))))
        )
    loss = jnp.sum(weight * local, keepdims=True)
    here = jnp.sum(area_v[...], keepdims=True)
    lane = lanes((own, pts))
    last = lax.broadcasted_iota(jnp.int32, (own, pts), 0) == own - 1
    ride = jnp.zeros((own, pts), f32)
    for k, value in enumerate((loss, here)):
        high = value.astype(bf16).astype(f32)
        ride = jnp.where(lane == 2 * k, high, jnp.where(lane == 2 * k + 1, value - high, ride))
    for m in range(members):
        value = jnp.where(last, ride, values[m]).astype(bf16)
        for c in range(cores):
            dout_v[m * cores + c] = value
    copies.start(dout_v, dout)
    copies.finish()


def pairs(owner, fields, target, area, var_weight, cores):
    members, own, pts = fields.shape
    return pl.pallas_call(
        functools.partial(pairs_kernel, members, cores),
        in_specs=[smem(), whole()] + [hbm()] * 3,
        out_specs=hbm(),
        out_shape=pltpu.HBM((members * cores, own, pts), bf16),
        scratch_shapes=scratch(
            (target.shape, f32), (area.shape, f32), (var_weight.shape, f32),
            ((members * cores, own, pts), bf16),
            copies=4,
        ),
        compiler_params=params(8),
        name="pairs",
    )(owner, fields, *in_hbm(target, area, var_weight))


def backward_kernel(
    core, dout, w_out_t, slope, slope_far, latent, latent_far, hidden, hidden_far,
    terms, dpre_out,
    w_out_t_v, slope_v, slope_far_v, latent_v, latent_far_v, hidden_v, hidden_far_v,
    terms_v, dpre_v, sems,
):
    copies = Copies(sems)
    me = core[0]
    rows = terms.shape[1]
    hid, pts = slope.shape
    parts = blocks(hid)

    def fetch(source, target, here):
        return copies.start(source.at[here], target.at[here])

    mine = (slice(None), pl.ds(2 * me, 2))
    fetched = [copies.start(w_out_t, w_out_t_v)]
    halves = [[fetch(slope, slope_v, parts[0]), fetch(slope_far, slope_far_v, parts[0])]]
    fetched.append(copies.start(latent.at[mine], latent_v))
    fetched.append(copies.start(latent_far.at[mine], latent_far_v))
    for here in parts[1:]:
        halves.append([fetch(slope, slope_v, here), fetch(slope_far, slope_far_v, here)])
    late = [
        copies.start(hidden.at[mine], hidden_v),
        copies.start(hidden_far.at[mine], hidden_far_v),
    ]

    row = lax.broadcasted_iota(jnp.int32, (PAD, pts), 0)
    last = lax.rem(row, OWN) == OWN - 1
    seeds = []
    ride = jnp.zeros((1, pts), f32)
    for which in (me, 1 - me):
        value = dout[:, pl.ds(which, 1)].astype(f32).reshape(PAD, pts)
        ride = ride + jnp.sum(jnp.where(last, value, 0.0), axis=0, keepdims=True)
        seeds.append(jnp.where(last, 0.0, value).astype(bf16))

    for copy in fetched:
        copies.wait(copy)
    features = [
        [ref[:, k].reshape(-1, pts) for k in range(2)] for ref in (latent_v, latent_far_v)
    ]
    for here, half in zip(parts, halves):
        first = second = None
        for copy in half:
            copies.wait(copy)
        for k, ref in enumerate((slope_v, slope_far_v)):
            dh = dot(w_out_t_v[here, :], seeds[k])
            dpre = (dh * ref[here, :]).astype(bf16)
            if k == 0:
                dpre_v[here, :] = dpre
                copies.start(dpre_v.at[here], dpre_out.at[here])
            swapped = jnp.concatenate(
                [
                    dpre[base + off : base + off + HALF]
                    for base in range(0, BLOCK, PAD)
                    for off in (HALF, 0)
                ],
                0,
            )
            a = dot_nt(features[k][0], dpre)
            b = dot_nt(features[k][1], swapped)
            first = a if first is None else first + a
            second = b if second is None else second + b
        low = lax.rem(lanes(first.shape), PAD) < HALF
        for xh, value in enumerate(
            (jnp.where(low, first, second), jnp.where(low, second, first))
        ):
            for xl in range(2):
                terms_v[2 * xh + xl, :, here] = value[xl * rows : (xl + 1) * rows].astype(bf16)
        copies.start(terms_v.at[:, :, here], terms.at[:, :, here])

    for copy in late:
        copies.wait(copy)
    out = dot_nt(hidden_v[...].reshape(-1, pts), seeds[0])
    out += dot_nt(hidden_far_v[...].reshape(-1, pts), seeds[1])
    out = out.reshape(-1, 2, 16, PAD)
    left = out[:, 0].reshape(-1, PAD)
    right = out[:, 1].reshape(-1, PAD)
    lane = lanes((1, PAD))
    parts = jnp.zeros((1, PAD), f32)
    for k in range(2):
        mine = lax.div(lanes((1, pts)), 2) == k
        value = jnp.sum(jnp.where(mine, ride, 0.0), axis=1, keepdims=True)
        high = value.astype(bf16).astype(f32)
        parts = jnp.where(lane == spare(2 * k), high, parts)
        parts = jnp.where(lane == spare(2 * k + 1), value - high, parts)
    row = lax.rem(lax.broadcasted_iota(jnp.int32, left.shape, 0), 16)
    unused = lax.rem(lanes(left.shape), OWN) == OWN - 1
    left = jnp.where(unused, jnp.where(row == 0, parts, 0.0), left)
    for xh in range(2):
        for xl in range(2):
            piece = slice(xl * rows, (xl + 1) * rows)
            terms_v[2 * xh + xl, :, hid : hid + PAD] = left[piece].astype(bf16)
            terms_v[2 * xh + xl, :, hid + PAD :] = right[piece].astype(bf16)
    tail = (slice(None), slice(None), slice(hid, hid + 2 * PAD))
    copies.start(terms_v.at[tail], terms.at[tail])
    copies.finish()


def backward(core, dout, w_out_t, slope, slope_far, latent, latent_far, hidden, hidden_far):
    hid, pts = slope.shape
    plane = latent.shape[0]
    shape = (4, plane * 16 // 2, hid + 2 * PAD)
    half = ((plane, 2, 16, pts), bf16)
    return pl.pallas_call(
        backward_kernel,
        in_specs=[smem(), whole()] + [hbm()] * 7,
        out_specs=[hbm()] * 2,
        out_shape=[
            pltpu.HBM(shape, bf16),
            pltpu.HBM((hid, pts), bf16),
        ],
        scratch_shapes=scratch(
            ((hid, PAD), bf16), ((hid, pts), f32), ((hid, pts), f32), half, half, half, half,
            (shape, bf16), ((hid, pts), bf16),
            copies=4 * len(blocks(hid)) + 6,
        ),
        compiler_params=params(24),
        name="backward",
    )(core, dout, *in_hbm(w_out_t, slope, slope_far, latent), latent_far, *in_hbm(hidden, hidden_far))


def split_again(tile):
    lane = lanes(tile.shape)
    value = tile + pltpu.roll(tile, PAD - OWN, 1)
    high = value.astype(bf16).astype(f32)
    low = pltpu.roll(value - high, OWN, 1)
    even = (lane == spare(0)) | (lane == spare(2))
    odd = (lane == spare(1)) | (lane == spare(3))
    return jnp.where(even, high, jnp.where(odd, low, tile))


def add_x_kernel(hid, got, out):
    value = got[0].astype(f32)
    for k in range(1, got.shape[0]):
        value = value + got[k].astype(f32)
    out[:, 0:hid] = value[:, 0:hid].astype(bf16)
    out[:, hid : hid + PAD] = split_again(value[:, hid : hid + PAD]).astype(bf16)
    out[:, hid + PAD :] = value[:, hid + PAD :].astype(bf16)


def add_x(got, hid):
    return pl.pallas_call(
        functools.partial(add_x_kernel, hid),
        in_specs=[whole()],
        out_specs=whole(),
        out_shape=jax.ShapeDtypeStruct(got.shape[1:], bf16),
        compiler_params=params(8),
        name="add_x",
    )(got)


def add_z_kernel(hid, got, out):
    value = got[0].astype(f32)
    for k in range(1, got.shape[0]):
        value = value + got[k].astype(f32)
    left = split_again(value[:, hid : hid + PAD]).astype(bf16)
    right = value[:, hid + PAD :].astype(bf16)
    for y in range(out.shape[0]):
        out[y, :, 0:PAD] = value[:, y * PAD : (y + 1) * PAD].astype(bf16)
        out[y, :, PAD : 2 * PAD] = left
        out[y, :, 2 * PAD :] = right


def add_z(got, hid):
    return pl.pallas_call(
        functools.partial(add_z_kernel, hid),
        in_specs=[whole()],
        out_specs=whole(),
        out_shape=jax.ShapeDtypeStruct((hid // PAD, got.shape[1], 3 * PAD), bf16),
        compiler_params=params(4),
        name="add_z",
    )(got)


def finish_kernel(
    count, points_all, turn, got, grad, loss, grad_lat, grad_in, grad_out, grad_lat_v, sems
):
    copies = Copies(sems)
    value = got[0].astype(f32)
    for k in range(1, got.shape[0]):
        value = value + got[k].astype(f32)
    left = value[:, PAD : 2 * PAD]
    head = left[0:1, :]
    lane = lanes(head.shape)

    def pick(k):
        mine = (lane == spare(2 * k)) | (lane == spare(2 * k + 1))
        return jnp.sum(jnp.where(mine, head, 0.0), axis=1, keepdims=True)

    weight_total = pick(1) * (1.0 / (count * count))
    scale = 1.0 / (weight_total * VARS)
    loss[...] = pick(0) * (1.0 / count) * scale
    scale = points_all * scale
    for here in blocks(grad.shape[0]):
        grad_lat_v[here, :] = (grad[here, :] * scale).astype(bf16)
        copies.start(grad_lat_v.at[here], grad_lat.at[here])
    ratio = scale * (1.0 / (points_all * count) ** 0.5)
    tile = value[:, 0:PAD] * ratio
    other = pltpu.roll(tile, HALF, 1)
    even = turn[0] == 0
    grad_in[0:16, :] = jnp.where(even, tile, other)[:, 0:HALF]
    grad_in[16:32, :] = jnp.where(even, other, tile)[:, 0:HALF]
    both = jnp.concatenate([left, value[:, 2 * PAD :]], 0) * ratio
    grad_out[...] = lax.dot_general(
        both, row_table().astype(f32), (((1,), (0,)), ((), ())),
        precision=lax.Precision.HIGHEST, preferred_element_type=f32,
    )
    copies.finish()


def finish(turn, got, grad, count, points_all):
    lat, pts = grad.shape
    return pl.pallas_call(
        functools.partial(finish_kernel, count, points_all),
        in_specs=[smem(), whole(), whole()],
        out_specs=[whole(), hbm(), whole(), whole()],
        out_shape=[
            jax.ShapeDtypeStruct((1, 1), f32),
            jax.ShapeDtypeStruct((lat, pts), bf16),
            jax.ShapeDtypeStruct((32, HALF), f32),
            jax.ShapeDtypeStruct((32, VARS), f32),
        ],
        scratch_shapes=scratch(((lat, pts), bf16), copies=len(blocks(lat))),
        compiler_params=params(8),
        name="finish",
    )(turn, got, grad)


def per_device(latent, w_in, w_out, target, area, var_weight):
    n_ens = lax.axis_size(ENS)
    n_plane = lax.axis_size(PLANE)
    n_core = lax.axis_size("c")
    n_z = lax.axis_size("z")
    pts = area.shape[0]
    hid, _ = w_in.shape
    own = PAD // n_ens
    assert own == OWN
    me = lax.axis_index(ENS)
    core = lax.axis_index("c")
    swap = [(0, 1), (1, 0)]
    features = latent[0]

    hidden, preact, decoded = forward(w_in, features, w_out)

    fields = exchange(decoded.reshape(n_ens, own, pts), ENS)
    late = lax.optimization_barrier((features, preact, w_out, decoded))
    far = lax.ppermute(late[0], "c", swap)
    slope, w_out_t = slopes(late[1], late[2])
    dout = pairs(
        me.astype(jnp.int32)[None], fields, target, area[None, :], var_weight[None, :], n_core
    )

    dout_got = exchange(dout, ENS + ("c",))
    far, _ = lax.optimization_barrier((far, dout))
    hidden_far, slope_far = far_forward(w_in, far)

    groups = lambda value: value.reshape(n_plane, 2 * n_core, 16, pts)
    terms, dpre = backward(
        core.astype(jnp.int32)[None],
        dout_got.reshape(n_ens, n_core, own, pts),
        w_out_t, slope, slope_far,
        groups(features), groups(far), groups(hidden), groups(hidden_far),
    )

    got = exchange(terms, CHIP_X)
    grad = grad_latent(w_in, dpre)
    got, grad = lax.optimization_barrier((got, grad))
    got = exchange(add_x(got, hid).reshape(n_z, 16, hid + 2 * PAD), "z")
    got = exchange(add_z(got, hid), "y")
    loss, grad_lat, part_in, part_out = finish(
        lax.axis_index("xh").astype(jnp.int32)[None],
        got, grad, float(n_ens), float(n_plane * n_core * pts),
    )
    return loss[0, 0], grad_lat[None], part_in.T, part_out.T


def solution(mesh):
    ens, grid_all = mesh.devices.shape
    split = (ens // 2, 2, 2, grid_all // 4, 2)
    fine = Mesh(mesh.devices.reshape(split), ENS + PLANE + ("c",))
    grid = PLANE + ("c",)
    in_specs = (P(ENS, None, grid), P(), P(), P(None, grid), P(grid), P())
    out_specs = (P(), P(ENS, None, grid), P(ENS, grid), P(None, grid))
    return jax.shard_map(
        per_device, mesh=fine, in_specs=in_specs, out_specs=out_specs, check_vma=False
    )
```

time: 112 us -> 107 us (0.955)
  Pallas kernels: 10.7 us -> 22.8 us
  waiting for transfers between devices: 18.7 us -> 29.5 us
  blocking collectives: 43.9 us -> 34.2 us
  local copies, waits for them, and re-layouts: 9.38 us -> 0.01 us
  matrix products: 5.38 us -> 0 us
  other arithmetic: 1.84 us -> 0 us
    pallas_call x3 -> x6, Pallas kernels: 9.21 us -> 20.4 us  [the longest x1 4.42 us: backward(): pl.pallas_call(backward_kernel, in_specs=[smem(), whole()] + [hbm()] * 7,...]
    all_to_all x3, waiting for transfers between devices: 18.7 us -> 29.5 us  [exchange(): return lax.all_to_all(pieces, axes, split_axis=0, concat_axis=0, tiled=True)]
    all_to_all x2, blocking collectives: 43.9 us -> 34.2 us  [exchange(): return lax.all_to_all(pieces, axes, split_axis=0, concat_axis=0, tiled=True)]
    unnamed x29 -> x4, local copies, waits for them, and re-layouts: 9.16 us -> 0.01 us
    dot_general x2 -> x0, matrix products: 5.38 us -> none  [the longest x1 3.41 us: dot(): return jnp.dot(a, b, preferred_element_type=f32)]
    ppermute x2 -> x1, starting transfers between devices: 3.99 us -> 1.92 us  [per_device(): far = lax.ppermute(late[0], 'c', swap)]
    add x1 -> x0, other arithmetic: 1.84 us -> none  [gelu_slope(): 0.5 * (1.0 + inner)]
    pallas_call x1, Pallas kernels: 0.41 us -> 1.95 us  [pairs(): pl.pallas_call(functools.partial(pairs_kernel, members, cores), in_specs=...]
  transfers between devices with their start and end apart: 5 -> 4, of which waited for: 3 -> 3; matrix products, arithmetic and copies ran while one was open for 7% -> 0% of each run, Pallas kernels for 0% -> 11%
where the time goes in v3:
time: 107 us
  blocking collectives  34.2 us (32%)
  waiting for transfers between devices  29.5 us (28%)
  Pallas kernels  22.8 us (21%)
  starting transfers between devices  19.5 us (18%)
    all_to_all x2, blocking collectives, exchange(): return lax.all_to_all(pieces, axes, split_axis=0, concat_axis=0, tiled=True)  34.2 us
    all_to_all x3, waiting for transfers between devices, exchange(): return lax.all_to_all(pieces, axes, split_axis=0, concat_axis=0, tiled=True)  29.5 us
    all_to_all x3, starting transfers between devices, exchange(): return lax.all_to_all(pieces, axes, split_axis=0, concat_axis=0, tiled=True)  17.6 us
    pallas_call x1, Pallas kernels, backward(): pl.pallas_call(backward_kernel, in_specs=[smem(), whole()] + [hbm()] * 7,...  4.42 us
    pallas_call x1, Pallas kernels, forward(): pl.pallas_call(forward_kernel, in_specs=[hbm()] * 3, out_specs=[hbm()] *...  4.27 us
    pallas_call x1, Pallas kernels, far_forward(): pl.pallas_call(far_kernel, in_specs=[hbm()] * 2, out_specs=[hbm()] * 2, o...  4.04 us
    pallas_call x1, Pallas kernels, grad_latent(): pl.pallas_call(grad_kernel, in_specs=[hbm()] * 2, out_specs=hbm(), out_sh...  3.51 us
    pallas_call x1, Pallas kernels, slopes(): pl.pallas_call(slope_kernel, in_specs=[hbm()] * 2, out_specs=[hbm()] * 2,...  2.63 us
  transfers between devices with their start and end apart: 4, of which 3 were waited for; matrix products, arithmetic and copies ran while one was open for 0% of the time, Pallas kernels for 11%

profile of v3, /device:TPU:2, one launch (start us, length us, event | category | flops | bytes accessed | tf_op | source)
XLA Modules:
  0.0 106.9 jit_solution(5513521768097593235)
XLA Ops:
  0.6 0.0 copy-start.1
  0.6 4.3 %forward.1 = (bf16[1024,256]{1,0:T(8,128)(2,1)}, f32[1024,256]{1,0:T(8,128)}, f32[128,256]{1,0:T(8,128)}) custom-call(bf16[1024,1024]{1,0:T(8,128)(2,1)} %w_in.5, bf16[1024,256]{1,0:T(8,128)(2,1)} %bitcast.20, bf16[99,1024]{1,0:T(8,128)(2,1)} %w_out.2), custom_call_target="tpu_custom_call" | custom-call | tf_op jit(solution)/shard_map/forward/pallas_call | solution.py:151
  4.9 0.0 copy-done.1
  4.9 1.9 %collective-permute-start = (bf16[1024,256]{1,0:T(8,128)(2,1)S(1)}, bf16[1024,256]{1,0:T(8,128)(2,1)S(1)}, u32[]{:S(2)}, u32[]{:S(2)}) collective-permute-start(bf16[1024,256]{1,0:T(8,128)(2,1)S(1)} %bitcast.22), channel_id=1, source_target_pairs={{0,1},{1,0},{2,3},{3,2},{4,5},{5,4},{6,7},{7,6},{8,9},{9,8},{10,11... | collective-permute-start | bytes 1572872 | tf_op jit(solution)/shard_map/ppermute | solution.py:606
  6.9 8.8 %all-to-all-start = ((f32[16,8,256]{2,1,0:T(8,128)}), f32[16,8,256]{2,1,0:T(8,128)S(1)}, u32[]{:S(2)}, u32[]{:S(2)}) async-start(f32[16,8,256]{2,1,0:T(8,128)} %bitcast.25), calls=%async_computation | async-start | bytes 262144 | tf_op jit(solution)/shard_map/all_to_all | solution.py:40
  15.7 11.7 %all-to-all-done.fields = f32[16,8,256]{2,1,0:T(8,128)S(1)} async-done(((f32[16,8,256]{2,1,0:T(8,128)}), f32[16,8,256]{2,1,0:T(8,128)S(1)}, u32[]{:S(2)}, u32[]{:S(2)}) %all-to-all-start) | async-done | bytes 131104 | tf_op jit(solution)/shard_map/all_to_all | solution.py:40
  27.4 2.0 %pairs.1 = bf16[32,8,256]{2,1,0:T(8,128)(2,1)} custom-call(s32[1]{0:T(128)} %bitcast.2.owner, f32[16,8,256]{2,1,0:T(8,128)S(1)} %all-to-all-done.fields, f32[99,256]{1,0:T(8,128)} %target_all.1, f32[1,256]{1,0:T(1,128)} %bitcast.26, f32[1,99]{1,0:T(1,128)} %bitcast.27), custom_call_target="tpu_custom_call" | custom-call | tf_op jit(solution)/shard_map/pairs/pallas_call | solution.py:344
  29.3 3.9 %all-to-all-start.1 = ((bf16[32,8,256]{2,1,0:T(8,128)(2,1)}), bf16[32,8,256]{2,1,0:T(8,128)(2,1)S(1)}, u32[]{:S(2)}, u32[]{:S(2)}) async-start(bf16[32,8,256]{2,1,0:T(8,128)(2,1)} %pairs.1), calls=%async_computation.1 | async-start | bytes 262144 | tf_op jit(solution)/shard_map/all_to_all | solution.py:40
  33.2 2.6 %slopes.1 = (f32[1024,256]{1,0:T(8,128)}, bf16[1024,128]{1,0:T(8,128)(2,1)}) custom-call(f32[1024,256]{1,0:T(8,128)} %get-tuple-element.25.preact, bf16[99,1024]{1,0:T(8,128)(2,1)} %w_out.2), custom_call_target="tpu_custom_call" | custom-call | flops 5242880 | bytes 4194304 | tf_op jit(solution)/shard_map/slopes/pallas_call | solution.py:228
  35.8 0.0 collective-permute-done.latent
  35.9 4.0 %far_forward.1 = (bf16[1024,256]{1,0:T(8,128)(2,1)}, f32[1024,256]{1,0:T(8,128)}) custom-call(bf16[1024,1024]{1,0:T(8,128)(2,1)} %w_in.5, bf16[1024,256]{1,0:T(8,128)(2,1)S(1)} %collective-permute-done.latent), custom_call_target="tpu_custom_call" | custom-call | flops 536870912 | bytes 4194304 | tf_op jit(solution)/shard_map/far_forward/pallas_call | solution.py:189
  39.9 4.0 %all-to-all-done.1 = bf16[32,8,256]{2,1,0:T(8,128)(2,1)S(1)} async-done(((bf16[32,8,256]{2,1,0:T(8,128)(2,1)}), bf16[32,8,256]{2,1,0:T(8,128)(2,1)S(1)}, u32[]{:S(2)}, u32[]{:S(2)}) %all-to-all-start.1) | async-done | bytes 131104 | tf_op jit(solution)/shard_map/all_to_all | solution.py:40
  43.9 4.4 %backward.1 = (bf16[4,128,1280]{2,1,0:T(8,128)(2,1)}, bf16[1024,256]{1,0:T(8,128)(2,1)}) custom-call(s32[1]{0:T(128)} %bitcast.1.core, bf16[16,2,8,256]{3,2,1,0:T(8,128)(2,1)S(1)} %bitcast.19, bf16[1024,128]{1,0:T(8,128)(2,1)} %get-tuple-element.27.w_out_t, f32[1024,256]{1,0:T(8,128)} %get-tuple-element.28.slope, f32[1024,256]{1,0:T(8,128)} %get-tuple-element.31.slope_far, ...), custom_call_target="tpu_custom_call" | custom-call | tf_op jit(solution)/shard_map/backward/pallas_call | solution.py:463
  48.3 5.0 %all-to-all-start.2 = ((bf16[4,128,1280]{2,1,0:T(8,128)(2,1)}), bf16[4,128,1280]{2,1,0:T(8,128)(2,1)S(1)}, u32[]{:S(2)}, u32[]{:S(2)}) async-start(bf16[4,128,1280]{2,1,0:T(8,128)(2,1)} %get-tuple-element.34), calls=%async_computation.2 | async-start | bytes 2621440 | tf_op jit(solution)/shard_map/all_to_all | solution.py:40
  53.2 3.5 %grad_latent.1.grad = f32[1024,256]{1,0:T(8,128)} custom-call(bf16[1024,1024]{1,0:T(8,128)(2,1)} %w_in.5, bf16[1024,256]{1,0:T(8,128)(2,1)} %get-tuple-element.35.dpre), custom_call_target="tpu_custom_call" | custom-call | flops 536870912 | bytes 4194304 | tf_op jit(solution)/shard_map/grad_latent/pallas_call | solution.py:264
  56.8 0.0 copy-start
  56.8 13.8 %all-to-all-done.2.got = bf16[4,128,1280]{2,1,0:T(8,128)(2,1)S(1)} async-done(((bf16[4,128,1280]{2,1,0:T(8,128)(2,1)}), bf16[4,128,1280]{2,1,0:T(8,128)(2,1)S(1)}, u32[]{:S(2)}, u32[]{:S(2)}) %all-to-all-start.2) | async-done | bytes 1310752 | tf_op jit(solution)/shard_map/all_to_all | solution.py:40
  70.6 0.3 add_x.1
  70.9 23.2 %all_to_all.25.got = bf16[8,16,1280]{2,1,0:T(8,128)(2,1)S(1)} all-to-all(bf16[8,16,1280]{2,1,0:T(8,128)(2,1)S(1)} %bitcast.18), channel_id=1, replica_groups=mesh['y'=8,'xh'=2,'xl'=2,'z'=8,'c'=2] {'z'}, dimensions={0} | all-to-all | bytes 655360 | tf_op jit(solution)/shard_map/all_to_all | solution.py:40
  94.1 0.2 add_z.1
  94.2 11.1 %all_to_all.26.got = bf16[8,16,384]{2,1,0:T(8,128)(2,1)S(1)} all-to-all(bf16[8,16,384]{2,1,0:T(8,128)(2,1)S(1)} %add_z.1), channel_id=1, replica_groups=mesh['y'=8,'xh'=2,'xl'=2,'z'=8,'c'=2] {'y'}, dimensions={0} | all-to-all | bytes 196608 | tf_op jit(solution)/shard_map/all_to_all | solution.py:40
  105.3 0.0 copy-done
  105.3 1.5 %finish.1 = (f32[1,1]{1,0:T(1,128)}, bf16[1024,256]{1,0:T(8,128)(2,1)}, f32[32,64]{1,0:T(8,128)}, f32[32,99]{1,0:T(8,128)}) custom-call(s32[1]{0:T(128)} %bitcast.turn, bf16[8,16,384]{2,1,0:T(8,128)(2,1)S(1)} %all_to_all.26.got, f32[1024,256]{1,0:T(8,128)S(1)} %copy-done), custom_call_target="tpu_custom_call" | custom-call | tf_op jit(solution)/shard_map/finish/pallas_call | solution.py:572
Async XLA Ops:
  0.6 4.3 %copy-start.1 = (bf16[1,1024,256]{2,1,0:T(8,128)(2,1)S(1)}, bf16[1,1024,256]{2,1,0:T(8,128)(2,1)}, u32[]{:S(2)}) copy-start(bf16[1,1024,256]{2,1,0:T(8,128)(2,1)} %param.6) | copy-start | bytes 1572868
  4.9 30.9 %collective-permute-start = (bf16[1024,256]{1,0:T(8,128)(2,1)S(1)}, bf16[1024,256]{1,0:T(8,128)(2,1)S(1)}, u32[]{:S(2)}, u32[]{:S(2)}) collective-permute-start(bf16[1024,256]{1,0:T(8,128)(2,1)S(1)} %bitcast.22), channel_id=1, source_target_pairs={{0,1},{1,0},{2,3},{3,2},{4,5},{5,4},{6,7},{7,6},{8,9},{9,8},{10,11... | collective-permute-start | bytes 1572872 | tf_op jit(solution)/shard_map/ppermute | solution.py:606
  6.9 20.5 %all-to-all-start = ((f32[16,8,256]{2,1,0:T(8,128)}), f32[16,8,256]{2,1,0:T(8,128)S(1)}, u32[]{:S(2)}, u32[]{:S(2)}) async-start(f32[16,8,256]{2,1,0:T(8,128)} %bitcast.25), calls=%async_computation | async-start | bytes 262144 | tf_op jit(solution)/shard_map/all_to_all | solution.py:40
  29.3 14.5 %all-to-all-start.1 = ((bf16[32,8,256]{2,1,0:T(8,128)(2,1)}), bf16[32,8,256]{2,1,0:T(8,128)(2,1)S(1)}, u32[]{:S(2)}, u32[]{:S(2)}) async-start(bf16[32,8,256]{2,1,0:T(8,128)(2,1)} %pairs.1), calls=%async_computation.1 | async-start | bytes 262144 | tf_op jit(solution)/shard_map/all_to_all | solution.py:40
  48.3 22.3 %all-to-all-start.2 = ((bf16[4,128,1280]{2,1,0:T(8,128)(2,1)}), bf16[4,128,1280]{2,1,0:T(8,128)(2,1)S(1)}, u32[]{:S(2)}, u32[]{:S(2)}) async-start(bf16[4,128,1280]{2,1,0:T(8,128)(2,1)} %get-tuple-element.34), calls=%async_computation.2 | async-start | bytes 2621440 | tf_op jit(solution)/shard_map/all_to_all | solution.py:40
  56.8 48.6 %copy-start = (f32[1024,256]{1,0:T(8,128)S(1)}, f32[1024,256]{1,0:T(8,128)}, u32[]{:S(2)}) copy-start(f32[1024,256]{1,0:T(8,128)} %grad_latent.1.grad) | copy-start | bytes 3145732

commit v4 on v3

v4 whole, which is shorter than its diff:
```python
import functools

import jax
import jax.numpy as jnp
from jax import lax
from jax.experimental import pallas as pl
from jax.experimental.pallas import tpu as pltpu
from jax.sharding import Mesh, PartitionSpec as P

VARS = 99
PAD = 128
HALF = PAD // 2
OWN = 8
ENS = ("y", "xh")
PLANE = ("xl", "z")
CHIP_X = ("xh", "xl")
BLOCK = 256

smooth_sq = 0.01
gelu_c = 0.7978845608
gelu_k = 0.044715
f32 = jnp.float32
bf16 = jnp.bfloat16
NT = (((1,), (1,)), ((), ()))


def gelu(value):
    square = value * value
    inner = jnp.tanh(gelu_c * (value + gelu_k * square * value))
    both = 0.5 * (1.0 + inner)
    slope = both + 0.5 * value * (1.0 - inner * inner) * (
        gelu_c * (1.0 + 3.0 * gelu_k * square)
    )
    return value * both, slope


def exchange(pieces, axes):
    return lax.all_to_all(pieces, axes, split_axis=0, concat_axis=0, tiled=True)


def dot(a, b):
    return jnp.dot(a, b, preferred_element_type=f32)


def dot_nt(a, b):
    return lax.dot_general(a, b, NT, preferred_element_type=f32)


def whole():
    return pl.BlockSpec(memory_space=pltpu.VMEM)


def smem():
    return pl.BlockSpec(memory_space=pltpu.SMEM)


def hbm():
    return pl.BlockSpec(memory_space=pltpu.HBM)


def in_hbm(*arrays):
    return [pltpu.with_memory_space_constraint(array, pltpu.HBM) for array in arrays]


def params(mib):
    return pltpu.CompilerParams(vmem_limit_bytes=mib << 20)


class Copies:
    def __init__(self, sems):
        self.sems = sems
        self.used = 0
        self.open = []

    def start(self, source, target):
        copy = pltpu.make_async_copy(source, target, self.sems.at[self.used])
        self.used += 1
        copy.start()
        self.open.append(copy)
        return copy

    def wait(self, copy):
        copy.wait()
        self.open = [other for other in self.open if other is not copy]

    def finish(self):
        for copy in self.open:
            self.wait(copy)


def scratch(*shapes, copies):
    return [pltpu.VMEM(shape, kind) for shape, kind in shapes] + [
        pltpu.SemaphoreType.DMA((copies,))
    ]


def blocks(size):
    return [slice(at, at + BLOCK) for at in range(0, size, BLOCK)]


def spare(k):
    return OWN * (k + 1) - 1


def row_table():
    row = lax.broadcasted_iota(jnp.int32, (PAD, VARS), 0)
    held = lax.rem(row, OWN) < OWN - 1
    variable = lax.div(row, OWN) * (OWN - 1) + lax.rem(row, OWN)
    return held & (variable == lanes((PAD, VARS)))


def lanes(shape):
    return lax.broadcasted_iota(jnp.int32, shape, len(shape) - 1)


def load_weights(copies, w_in, w_in_v):
    loads = []
    for here in blocks(w_in.shape[0]):
        middle = (here.start + here.stop) // 2
        loads.append(
            [
                copies.start(w_in.at[part], w_in_v.at[part])
                for part in (slice(here.start, middle), slice(middle, here.stop))
            ]
        )
    return loads


def forward_kernel(
    w_in, latent, w_out, hidden, slope, decoded,
    w_in_v, latent_v, w_out_v, hidden_v, slope_v, decoded_v, sems,
):
    copies = Copies(sems)
    first = copies.start(latent, latent_v)
    loads = load_weights(copies, w_in, w_in_v)
    rows = copies.start(w_out, w_out_v)
    copies.wait(first)
    for here, load in zip(blocks(w_in.shape[0]), loads):
        for copy in load:
            copies.wait(copy)
        value, bend = gelu(dot(w_in_v[here, :], latent_v[...]))
        hidden_v[here, :] = value.astype(bf16)
        copies.start(hidden_v.at[here], hidden.at[here])
        slope_v[here, :] = bend.astype(bf16)
        copies.start(slope_v.at[here], slope.at[here])
    copies.wait(rows)
    w_out_rows = dot(row_table().astype(bf16), w_out_v[...]).astype(bf16)
    decoded_v[...] = dot(w_out_rows, hidden_v[...])
    copies.start(decoded_v, decoded)
    copies.finish()


def forward(w_in, latent, w_out):
    hid, lat = w_in.shape
    pts = latent.shape[1]
    return pl.pallas_call(
        forward_kernel,
        in_specs=[hbm()] * 3,
        out_specs=[hbm()] * 3,
        out_shape=[
            pltpu.HBM((hid, pts), bf16),
            pltpu.HBM((hid, pts), bf16),
            pltpu.HBM((PAD, pts), f32),
        ],
        scratch_shapes=scratch(
            ((hid, lat), bf16), ((lat, pts), bf16), ((VARS, hid), bf16),
            ((hid, pts), bf16), ((hid, pts), bf16), ((PAD, pts), f32),
            copies=4 * len(blocks(hid)) + 3,
        ),
        compiler_params=params(16),
        name="forward",
    )(*in_hbm(w_in, latent, w_out))


def far_kernel(w_in, latent, hidden, slope, w_in_v, hidden_v, slope_v, sems):
    copies = Copies(sems)
    loads = load_weights(copies, w_in, w_in_v)
    for here, load in zip(blocks(w_in.shape[0]), loads):
        for copy in load:
            copies.wait(copy)
        value, bend = gelu(dot(w_in_v[here, :], latent[...]))
        hidden_v[here, :] = value.astype(bf16)
        copies.start(hidden_v.at[here], hidden.at[here])
        slope_v[here, :] = bend.astype(bf16)
        copies.start(slope_v.at[here], slope.at[here])
    copies.finish()


def far_forward(w_in, latent):
    hid, lat = w_in.shape
    pts = latent.shape[1]
    return pl.pallas_call(
        far_kernel,
        in_specs=[hbm(), whole()],
        out_specs=[hbm()] * 2,
        out_shape=[pltpu.HBM((hid, pts), bf16), pltpu.HBM((hid, pts), bf16)],
        scratch_shapes=scratch(
            ((hid, lat), bf16), ((hid, pts), bf16), ((hid, pts), bf16),
            copies=4 * len(blocks(hid)),
        ),
        compiler_params=params(16),
        cost_estimate=pl.CostEstimate(
            flops=2 * hid * lat * pts, bytes_accessed=4 << 20, transcendentals=hid * pts
        ),
        name="far_forward",
    )(*in_hbm(w_in), latent)


def prepare_kernel(
    owner, w_out_h, target_h, area_h, var_weight_h, w_out_t_h, target, weight, area_sum,
    w_out_v, w_out_t_v, target_v, area_v, var_weight_v, sems,
):
    copies = Copies(sems)
    inputs = [
        copies.start(w_out_h, w_out_v),
        copies.start(target_h, target_v),
        copies.start(area_h, area_v),
        copies.start(var_weight_h, var_weight_v),
    ]
    copies.wait(inputs[0])
    w_out_t_v[...] = lax.dot_general(
        w_out_v[...], row_table().astype(bf16), (((0,), (1,)), ((), ())),
        preferred_element_type=f32,
    ).astype(bf16)
    copies.start(w_out_t_v, w_out_t_h)
    for copy in inputs[1:]:
        copies.wait(copy)
    row = lax.broadcasted_iota(jnp.int32, (OWN, VARS), 0)
    held = (row < OWN - 1) & (lanes((OWN, VARS)) == owner[0] * (OWN - 1) + row)
    scale = jnp.sum(jnp.where(held, var_weight_v[...], 0.0), axis=1, keepdims=True)
    weight[...] = area_v[...] * scale
    target[...] = lax.dot_general(
        held.astype(f32), target_v[...], (((1,), (0,)), ((), ())),
        precision=lax.Precision.HIGHEST, preferred_element_type=f32,
    )
    area_sum[...] = jnp.broadcast_to(jnp.sum(area_v[...], keepdims=True), area_sum.shape)
    copies.finish()


def prepare(owner, w_out, target, area, var_weight):
    hid = w_out.shape[1]
    pts = target.shape[1]
    return pl.pallas_call(
        prepare_kernel,
        in_specs=[smem()] + [hbm()] * 4,
        out_specs=[hbm()] + [whole()] * 3,
        out_shape=[
            pltpu.HBM((hid, PAD), bf16),
            jax.ShapeDtypeStruct((OWN, pts), f32),
            jax.ShapeDtypeStruct((OWN, pts), f32),
            jax.ShapeDtypeStruct((8, PAD), f32),
        ],
        scratch_shapes=scratch(
            (w_out.shape, bf16), ((hid, PAD), bf16), (target.shape, f32),
            (area.shape, f32), (var_weight.shape, f32),
            copies=5,
        ),
        compiler_params=params(16),
        cost_estimate=pl.CostEstimate(flops=1 << 28, bytes_accessed=1 << 20, transcendentals=0),
        name="prepare",
    )(owner, *in_hbm(w_out, target, area, var_weight))


def grad_kernel(w_in, dpre, scale, grad, w_in_v, grad_v, sems):
    copies = Copies(sems)
    copies.start(w_in, w_in_v)
    copies.finish()
    factor = scale[0:1, 0:1]
    for here in blocks(w_in.shape[1]):
        value = lax.dot_general(
            w_in_v[:, here], dpre[...], (((0,), (0,)), ((), ())), preferred_element_type=f32
        )
        grad_v[here, :] = (value * factor).astype(bf16)
        copies.start(grad_v.at[here], grad.at[here])
    copies.finish()


def grad_latent(w_in, dpre, scale):
    hid, lat = w_in.shape
    pts = dpre.shape[1]
    return pl.pallas_call(
        grad_kernel,
        in_specs=[hbm(), whole(), whole()],
        out_specs=hbm(),
        out_shape=pltpu.HBM((lat, pts), bf16),
        scratch_shapes=scratch(
            ((hid, lat), bf16), ((lat, pts), bf16), copies=1 + len(blocks(lat))
        ),
        compiler_params=params(16),
        cost_estimate=pl.CostEstimate(
            flops=2 * hid * lat * pts, bytes_accessed=4 << 20, transcendentals=0
        ),
        name="grad_latent",
    )(*in_hbm(w_in), dpre, scale)


def pairs_kernel(members, cores, fields, target, weight, area_sum, dout, dout_v, sems):
    copies = Copies(sems)
    count = float(members)
    own, pts = fields.shape[1:]
    slopes = [None] * members
    total = None
    for m in range(1, members):
        for k in range(m):
            diff = fields[m] - fields[k]
            square = diff * diff + smooth_sq
            inverse = lax.rsqrt(square)
            slope = diff * inverse
            apart = square * inverse
            total = apart if total is None else total + apart
            slopes[m] = slope if slopes[m] is None else slopes[m] + slope
            slopes[k] = -slope if slopes[k] is None else slopes[k] - slope
    total = 2.0 * total + count * smooth_sq**0.5
    local = total * (-1.0 / (2.0 * count * (count - 1.0)))
    values = []
    for m in range(members):
        miss = fields[m] - target[...]
        square = miss * miss + smooth_sq
        inverse = lax.rsqrt(square)
        local = local + square * inverse * (1.0 / count)
        values.append(
            weight[...]
            * (miss * inverse * (1.0 / count) - slopes[m] * (1.0 / (count * (count - 1.0))))
        )
    loss = jnp.sum(weight[...] * local, keepdims=True)
    lane = lanes((own, pts))
    last = lax.broadcasted_iota(jnp.int32, (own, pts), 0) == own - 1
    ride = jnp.zeros((own, pts), f32)
    for k, value in enumerate((loss, area_sum[0:1, 0:1])):
        high = value.astype(bf16).astype(f32)
        ride = jnp.where(lane == 2 * k, high, jnp.where(lane == 2 * k + 1, value - high, ride))
    for m in range(members):
        value = jnp.where(last, ride, values[m]).astype(bf16)
        for c in range(cores):
            dout_v[m * cores + c] = value
    copies.start(dout_v, dout)
    copies.finish()


def pairs(fields, target, weight, area_sum, cores):
    members, own, pts = fields.shape
    shape = (members * cores, own, pts)
    return pl.pallas_call(
        functools.partial(pairs_kernel, members, cores),
        in_specs=[whole()] * 4,
        out_specs=hbm(),
        out_shape=pltpu.HBM(shape, bf16),
        scratch_shapes=scratch((shape, bf16), copies=1),
        compiler_params=params(8),
        name="pairs",
    )(fields, target, weight, area_sum)


def backward_kernel(
    core, dout, w_out_t, slope, slope_far, latent, latent_far, hidden, hidden_far,
    terms_v, dpre_v,
    w_out_t_v, slope_v, slope_far_v, latent_v, latent_far_v, hidden_v, hidden_far_v, sems,
):
    copies = Copies(sems)
    me = core[0]
    rows = terms_v.shape[1]
    hid, pts = slope.shape
    parts = blocks(hid)

    def fetch(source, target, here):
        return copies.start(source.at[here], target.at[here])

    mine = (slice(None), pl.ds(2 * me, 2))
    fetched = [copies.start(w_out_t, w_out_t_v)]
    halves = [[fetch(slope, slope_v, parts[0]), fetch(slope_far, slope_far_v, parts[0])]]
    fetched.append(copies.start(latent.at[mine], latent_v))
    fetched.append(copies.start(latent_far.at[mine], latent_far_v))
    for here in parts[1:]:
        halves.append([fetch(slope, slope_v, here), fetch(slope_far, slope_far_v, here)])
    late = [
        copies.start(hidden.at[mine], hidden_v),
        copies.start(hidden_far.at[mine], hidden_far_v),
    ]

    row = lax.broadcasted_iota(jnp.int32, (PAD, pts), 0)
    last = lax.rem(row, OWN) == OWN - 1
    seeds = []
    ride = jnp.zeros((1, pts), f32)
    for which in (me, 1 - me):
        value = dout[:, pl.ds(which, 1)].astype(f32).reshape(PAD, pts)
        ride = ride + jnp.sum(jnp.where(last, value, 0.0), axis=0, keepdims=True)
        seeds.append(jnp.where(last, 0.0, value).astype(bf16))

    for copy in fetched:
        copies.wait(copy)
    features = [
        [ref[:, k].reshape(-1, pts) for k in range(2)] for ref in (latent_v, latent_far_v)
    ]
    for here, half in zip(parts, halves):
        first = second = None
        for copy in half:
            copies.wait(copy)
        for k, ref in enumerate((slope_v, slope_far_v)):
            dh = dot(w_out_t_v[here, :], seeds[k])
            dpre = (dh * ref[here, :].astype(f32)).astype(bf16)
            if k == 0:
                dpre_v[here, :] = dpre
            swapped = jnp.concatenate(
                [
                    dpre[base + off : base + off + HALF]
                    for base in range(0, BLOCK, PAD)
                    for off in (HALF, 0)
                ],
                0,
            )
            a = dot_nt(features[k][0], dpre)
            b = dot_nt(features[k][1], swapped)
            first = a if first is None else first + a
            second = b if second is None else second + b
        low = lax.rem(lanes(first.shape), PAD) < HALF
        for xh, value in enumerate(
            (jnp.where(low, first, second), jnp.where(low, second, first))
        ):
            for xl in range(2):
                terms_v[2 * xh + xl, :, here] = value[xl * rows : (xl + 1) * rows].astype(bf16)

    for copy in late:
        copies.wait(copy)
    out = dot_nt(hidden_v[...].reshape(-1, pts), seeds[0])
    out += dot_nt(hidden_far_v[...].reshape(-1, pts), seeds[1])
    out = out.reshape(-1, 2, 16, PAD)
    left = out[:, 0].reshape(-1, PAD)
    right = out[:, 1].reshape(-1, PAD)
    lane = lanes((1, PAD))
    parts = jnp.zeros((1, PAD), f32)
    for k in range(2):
        mine = lax.div(lanes((1, pts)), 2) == k
        value = jnp.sum(jnp.where(mine, ride, 0.0), axis=1, keepdims=True)
        high = value.astype(bf16).astype(f32)
        parts = jnp.where(lane == spare(2 * k), high, parts)
        parts = jnp.where(lane == spare(2 * k + 1), value - high, parts)
    row = lax.rem(lax.broadcasted_iota(jnp.int32, left.shape, 0), 16)
    unused = lax.rem(lanes(left.shape), OWN) == OWN - 1
    left = jnp.where(unused, jnp.where(row == 0, parts, 0.0), left)
    for xh in range(2):
        for xl in range(2):
            piece = slice(xl * rows, (xl + 1) * rows)
            terms_v[2 * xh + xl, :, hid : hid + PAD] = left[piece].astype(bf16)
            terms_v[2 * xh + xl, :, hid + PAD :] = right[piece].astype(bf16)


def backward(core, dout, w_out_t, slope, slope_far, latent, latent_far, hidden, hidden_far):
    hid, pts = slope.shape
    plane = latent.shape[0]
    shape = (4, plane * 16 // 2, hid + 2 * PAD)
    half = ((plane, 2, 16, pts), bf16)
    return pl.pallas_call(
        backward_kernel,
        in_specs=[smem(), whole()] + [hbm()] * 7,
        out_specs=[whole()] * 2,
        out_shape=[
            jax.ShapeDtypeStruct(shape, bf16),
            jax.ShapeDtypeStruct((hid, pts), bf16),
        ],
        scratch_shapes=scratch(
            ((hid, PAD), bf16), ((hid, pts), bf16), ((hid, pts), bf16), half, half, half, half,
            copies=2 * len(blocks(hid)) + 5,
        ),
        compiler_params=params(24),
        name="backward",
    )(core, dout, *in_hbm(w_out_t, slope, slope_far, latent), latent_far, *in_hbm(hidden, hidden_far))


def split_again(tile):
    lane = lanes(tile.shape)
    value = tile + pltpu.roll(tile, PAD - OWN, 1)
    high = value.astype(bf16).astype(f32)
    low = pltpu.roll(value - high, OWN, 1)
    even = (lane == spare(0)) | (lane == spare(2))
    odd = (lane == spare(1)) | (lane == spare(3))
    return jnp.where(even, high, jnp.where(odd, low, tile))


def add_x_kernel(hid, got, out):
    value = got[0].astype(f32)
    for k in range(1, got.shape[0]):
        value = value + got[k].astype(f32)
    out[:, 0:hid] = value[:, 0:hid].astype(bf16)
    out[:, hid : hid + PAD] = split_again(value[:, hid : hid + PAD]).astype(bf16)
    out[:, hid + PAD :] = value[:, hid + PAD :].astype(bf16)


def add_x(got, hid):
    return pl.pallas_call(
        functools.partial(add_x_kernel, hid),
        in_specs=[whole()],
        out_specs=whole(),
        out_shape=jax.ShapeDtypeStruct(got.shape[1:], bf16),
        compiler_params=params(8),
        name="add_x",
    )(got)


def pick(head, k):
    lane = lanes(head.shape)
    mine = (lane == spare(2 * k)) | (lane == spare(2 * k + 1))
    return jnp.sum(jnp.where(mine, head, 0.0), axis=1, keepdims=True)


def add_z_kernel(hid, copied, points_all, got, out, scale, out_v, sems):
    copies = Copies(sems)
    value = got[0].astype(f32)
    for k in range(1, got.shape[0]):
        value = value + got[k].astype(f32)
    left = value[:, hid : hid + PAD]
    keep = split_again(left).astype(bf16)
    right = value[:, hid + PAD :].astype(bf16)
    for y in range(out.shape[0]):
        out_v[y, :, 0:PAD] = value[:, y * PAD : (y + 1) * PAD].astype(bf16)
        out_v[y, :, PAD : 2 * PAD] = keep
        out_v[y, :, 2 * PAD :] = right
    copies.start(out_v, out)
    weight_total = pick(left[0:1, :], 1) * (1.0 / copied)
    scale[...] = jnp.broadcast_to(points_all / (weight_total * VARS), scale.shape)
    copies.finish()


def add_z(got, hid, copied, points_all):
    shape = (hid // PAD, got.shape[1], 3 * PAD)
    return pl.pallas_call(
        functools.partial(add_z_kernel, hid, copied, points_all),
        in_specs=[whole()],
        out_specs=[hbm(), whole()],
        out_shape=[pltpu.HBM(shape, bf16), jax.ShapeDtypeStruct((8, PAD), f32)],
        scratch_shapes=scratch((shape, bf16), copies=1),
        compiler_params=params(4),
        name="add_z",
    )(got)


def finish_kernel(copied, points_all, count, turn, got, loss, grad_in, grad_out):
    value = got[0].astype(f32)
    for k in range(1, got.shape[0]):
        value = value + got[k].astype(f32)
    left = value[:, PAD : 2 * PAD]
    head = left[0:1, :]
    weight_total = pick(head, 1) * (1.0 / (copied * count))
    scale = 1.0 / (weight_total * VARS)
    loss[...] = pick(head, 0) * (1.0 / copied) * scale
    ratio = scale * (points_all / (points_all * count) ** 0.5)
    tile = value[:, 0:PAD] * ratio
    other = pltpu.roll(tile, HALF, 1)
    even = turn[0] == 0
    grad_in[0:16, :] = jnp.where(even, tile, other)[:, 0:HALF]
    grad_in[16:32, :] = jnp.where(even, other, tile)[:, 0:HALF]
    both = jnp.concatenate([left, value[:, 2 * PAD :]], 0) * ratio
    grad_out[...] = lax.dot_general(
        both, row_table().astype(f32), (((1,), (0,)), ((), ())),
        precision=lax.Precision.HIGHEST, preferred_element_type=f32,
    )


def finish(turn, got, copied, points_all, count):
    return pl.pallas_call(
        functools.partial(finish_kernel, copied, points_all, count),
        in_specs=[smem(), whole()],
        out_specs=[whole()] * 3,
        out_shape=[
            jax.ShapeDtypeStruct((1, 1), f32),
            jax.ShapeDtypeStruct((32, HALF), f32),
            jax.ShapeDtypeStruct((32, VARS), f32),
        ],
        compiler_params=params(4),
        name="finish",
    )(turn, got)


def per_device(latent, w_in, w_out, target, area, var_weight):
    n_ens = lax.axis_size(ENS)
    n_plane = lax.axis_size(PLANE)
    n_core = lax.axis_size("c")
    n_z = lax.axis_size("z")
    pts = area.shape[0]
    hid, _ = w_in.shape
    own = PAD // n_ens
    assert own == OWN
    me = lax.axis_index(ENS)
    core = lax.axis_index("c")
    swap = [(0, 1), (1, 0)]
    features = latent[0]

    count = float(n_ens)
    points_all = float(n_plane * n_core * pts)
    hidden, slope, decoded = forward(w_in, features, w_out)

    fields = exchange(decoded.reshape(n_ens, own, pts), ENS)
    late = lax.optimization_barrier((features, w_out, decoded))
    far = lax.ppermute(late[0], "c", swap)
    w_out_t, target_own, weight_own, area_sum = prepare(
        me.astype(jnp.int32)[None], late[1], target, area[None, :], var_weight[None, :]
    )
    dout = pairs(fields, target_own, weight_own, area_sum, n_core)

    dout_got = exchange(dout, ENS + ("c",))
    far, _ = lax.optimization_barrier((far, dout))
    hidden_far, slope_far = far_forward(w_in, far)

    groups = lambda value: value.reshape(n_plane, 2 * n_core, 16, pts)
    terms, dpre = backward(
        core.astype(jnp.int32)[None],
        dout_got.reshape(n_ens, n_core, own, pts),
        w_out_t, slope, slope_far,
        groups(features), groups(far), groups(hidden), groups(hidden_far),
    )

    got = exchange(terms, CHIP_X)
    got = exchange(add_x(got, hid).reshape(n_z, 16, hid + 2 * PAD), "z")
    got, scale = add_z(got, hid, count * lax.axis_size("xh"), points_all)
    got = exchange(got, "y")
    grad_lat = grad_latent(w_in, dpre, scale)
    loss, part_in, part_out = finish(
        lax.axis_index("xh").astype(jnp.int32)[None], got, count, points_all, count
    )
    return loss[0, 0], grad_lat[None], part_in.T, part_out.T


def solution(mesh):
    ens, grid_all = mesh.devices.shape
    split = (ens // 2, 2, 2, grid_all // 4, 2)
    fine = Mesh(mesh.devices.reshape(split), ENS + PLANE + ("c",))
    grid = PLANE + ("c",)
    in_specs = (P(ENS, None, grid), P(), P(), P(None, grid), P(grid), P())
    out_specs = (P(), P(ENS, None, grid), P(ENS, grid), P(None, grid))
    return jax.shard_map(
        per_device, mesh=fine, in_specs=in_specs, out_specs=out_specs, check_vma=False
    )
```

time: 107 us -> 105 us (0.981)
  blocking collectives: 34.2 us -> 43.9 us
  waiting for transfers between devices: 29.5 us -> 21.9 us
  Pallas kernels: 22.8 us -> 20.3 us
  starting transfers between devices: 19.5 us -> 17.9 us
    all_to_all x2, blocking collectives: 34.2 us -> 43.9 us  [exchange(): return lax.all_to_all(pieces, axes, split_axis=0, concat_axis=0, tiled=True)]
    all_to_all x3, waiting for transfers between devices: 29.5 us -> 21.9 us  [exchange(): return lax.all_to_all(pieces, axes, split_axis=0, concat_axis=0, tiled=True)]
    all_to_all x3, starting transfers between devices: 17.6 us -> 16 us  [exchange(): return lax.all_to_all(pieces, axes, split_axis=0, concat_axis=0, tiled=True)]
    pallas_call x5, Pallas kernels: 11.9 us -> 10.7 us  [the longest x1 3.96 us: far_forward(): pl.pallas_call(far_kernel, in_specs=[hbm(), whole()], out_specs=[hbm()] *...]
  transfers between devices with their start and end apart: 4 -> 4, of which waited for: 3 -> 3; matrix products, arithmetic and copies ran while one was open for 0% -> 0% of each run, Pallas kernels for 11% -> 10%
where the time goes in v4:
time: 105 us
  blocking collectives  43.9 us (42%)
  waiting for transfers between devices  21.9 us (21%)
  Pallas kernels  20.3 us (19%)
  starting transfers between devices  17.9 us (17%)
    all_to_all x2, blocking collectives, exchange(): return lax.all_to_all(pieces, axes, split_axis=0, concat_axis=0, tiled=True)  43.9 us
    all_to_all x3, waiting for transfers between devices, exchange(): return lax.all_to_all(pieces, axes, split_axis=0, concat_axis=0, tiled=True)  21.9 us
    all_to_all x3, starting transfers between devices, exchange(): return lax.all_to_all(pieces, axes, split_axis=0, concat_axis=0, tiled=True)  16 us
    pallas_call x1, Pallas kernels, forward(): pl.pallas_call(forward_kernel, in_specs=[hbm()] * 3, out_specs=[hbm()] *...  4.51 us
    pallas_call x1, Pallas kernels, far_forward(): pl.pallas_call(far_kernel, in_specs=[hbm(), whole()], out_specs=[hbm()] *...  3.96 us
    pallas_call x1, Pallas kernels, backward(): pl.pallas_call(backward_kernel, in_specs=[smem(), whole()] + [hbm()] * 7,...  3.59 us
    pallas_call x1, Pallas kernels, grad_latent(): pl.pallas_call(grad_kernel, in_specs=[hbm(), whole(), whole()], out_specs...  3.1 us
  transfers between devices with their start and end apart: 4, of which 3 were waited for; matrix products, arithmetic and copies ran while one was open for 0% of the time, Pallas kernels for 10%

profile of v4, /device:TPU:2, one launch (start us, length us, event | category | flops | bytes accessed | tf_op | source)
XLA Modules:
  0.0 104.8 jit_solution(672813737885669060)
XLA Ops:
  0.6 0.0 copy-start
  0.6 4.5 %forward.1 = (bf16[1024,256]{1,0:T(8,128)(2,1)}, bf16[1024,256]{1,0:T(8,128)(2,1)}, f32[128,256]{1,0:T(8,128)}) custom-call(bf16[1024,1024]{1,0:T(8,128)(2,1)} %w_in.5, bf16[1024,256]{1,0:T(8,128)(2,1)} %bitcast.20, bf16[99,1024]{1,0:T(8,128)(2,1)} %w_out_h), custom_call_target="tpu_custom_call" | custom-call | tf_op jit(solution)/shard_map/forward/pallas_call | solution.py:156
  5.2 0.0 copy-done
  5.2 1.9 %collective-permute-start = (bf16[1024,256]{1,0:T(8,128)(2,1)S(1)}, bf16[1024,256]{1,0:T(8,128)(2,1)S(1)}, u32[]{:S(2)}, u32[]{:S(2)}) collective-permute-start(bf16[1024,256]{1,0:T(8,128)(2,1)S(1)} %bitcast.22), channel_id=1, source_target_pairs={{0,1},{1,0},{2,3},{3,2},{4,5},{5,4},{6,7},{7,6},{8,9},{9,8},{10,11... | collective-permute-start | bytes 1572872 | tf_op jit(solution)/shard_map/ppermute | solution.py:593
  7.1 8.8 %all-to-all-start = ((f32[16,8,256]{2,1,0:T(8,128)}), f32[16,8,256]{2,1,0:T(8,128)S(1)}, u32[]{:S(2)}, u32[]{:S(2)}) async-start(f32[16,8,256]{2,1,0:T(8,128)} %bitcast.26), calls=%async_computation | async-start | bytes 262144 | tf_op jit(solution)/shard_map/all_to_all | solution.py:38
  15.9 2.0 %prepare.1 = (bf16[1024,128]{1,0:T(8,128)(2,1)}, f32[8,256]{1,0:T(8,128)S(1)}, f32[8,256]{1,0:T(8,128)S(1)}, f32[8,128]{1,0:T(8,128)S(1)}) custom-call(s32[1]{0:T(128)} %bitcast.4.owner, bf16[99,1024]{1,0:T(8,128)(2,1)} %w_out_h, f32[99,256]{1,0:T(8,128)} %target_h.1, f32[1,256]{1,0:T(1,128)} %bitcast.29, f32[1,99]{1,0:T(1,128)} %bitcast.30), custom_call_target="tpu_custom_call" | custom-call | flops 268435456 | bytes 1048576 | tf_op jit(solution)/shard_map/prepare/pallas_call | solution.py:243
  17.9 9.7 %all-to-all-done.fields = f32[16,8,256]{2,1,0:T(8,128)S(1)} async-done(((f32[16,8,256]{2,1,0:T(8,128)}), f32[16,8,256]{2,1,0:T(8,128)S(1)}, u32[]{:S(2)}, u32[]{:S(2)}) %all-to-all-start) | async-done | bytes 131104 | tf_op jit(solution)/shard_map/all_to_all | solution.py:38
  27.6 1.2 %pairs.1 = bf16[32,8,256]{2,1,0:T(8,128)(2,1)} custom-call(f32[16,8,256]{2,1,0:T(8,128)S(1)} %all-to-all-done.fields, f32[8,256]{1,0:T(8,128)S(1)} %get-tuple-element.25.target, f32[8,256]{1,0:T(8,128)S(1)} %get-tuple-element.26.weight, f32[8,128]{1,0:T(8,128)S(1)} %get-tuple-element.27.area_sum), custom_call_target="tpu_custom_call" | custom-call | tf_op jit(solution)/shard_map/pairs/pallas_call | solution.py:343
  28.8 3.9 %all-to-all-start.1 = ((bf16[32,8,256]{2,1,0:T(8,128)(2,1)}), bf16[32,8,256]{2,1,0:T(8,128)(2,1)S(1)}, u32[]{:S(2)}, u32[]{:S(2)}) async-start(bf16[32,8,256]{2,1,0:T(8,128)(2,1)} %pairs.1), calls=%async_computation.1 | async-start | bytes 262144 | tf_op jit(solution)/shard_map/all_to_all | solution.py:38
  32.7 0.0 collective-permute-done.latent
  32.7 4.0 %far_forward.1 = (bf16[1024,256]{1,0:T(8,128)(2,1)}, bf16[1024,256]{1,0:T(8,128)(2,1)}) custom-call(bf16[1024,1024]{1,0:T(8,128)(2,1)} %w_in.5, bf16[1024,256]{1,0:T(8,128)(2,1)S(1)} %collective-permute-done.latent), custom_call_target="tpu_custom_call" | custom-call | flops 536870912 | bytes 4194304 | tf_op jit(solution)/shard_map/far_forward/pallas_call | solution.py:192
  36.6 6.7 %all-to-all-done.1 = bf16[32,8,256]{2,1,0:T(8,128)(2,1)S(1)} async-done(((bf16[32,8,256]{2,1,0:T(8,128)(2,1)}), bf16[32,8,256]{2,1,0:T(8,128)(2,1)S(1)}, u32[]{:S(2)}, u32[]{:S(2)}) %all-to-all-start.1) | async-done | bytes 131104 | tf_op jit(solution)/shard_map/all_to_all | solution.py:38
  43.3 3.6 %backward.1 = (bf16[4,128,1280]{2,1,0:T(8,128)(2,1)S(1)}, bf16[1024,256]{1,0:T(8,128)(2,1)S(1)}) custom-call(s32[1]{0:T(128)} %bitcast.1.core, bf16[16,2,8,256]{3,2,1,0:T(8,128)(2,1)S(1)} %bitcast.19, bf16[1024,128]{1,0:T(8,128)(2,1)} %get-tuple-element.28.w_out_t, bf16[1024,256]{1,0:T(8,128)(2,1)} %get-tuple-element.29.slope, ...), custom_call_target="tpu_custom_call" | custom-call | tf_op jit(solution)/shard_map/backward/pallas_call | solution.py:452
  46.9 21.2 %all_to_all.25.got = bf16[4,128,1280]{2,1,0:T(8,128)(2,1)S(1)} all-to-all(bf16[4,128,1280]{2,1,0:T(8,128)(2,1)S(1)} %get-tuple-element.35), channel_id=1, replica_groups=mesh['y'=8,'xh'=2,'xl'=2,'z'=8,'c'=2] {'xh','xl'}, dimensions={0} | all-to-all | bytes 2621440 | tf_op jit(solution)/shard_map/all_to_all | solution.py:38
  68.1 0.3 add_x.1
  68.4 22.7 %all_to_all.26.got = bf16[8,16,1280]{2,1,0:T(8,128)(2,1)S(1)} all-to-all(bf16[8,16,1280]{2,1,0:T(8,128)(2,1)S(1)} %bitcast.18), channel_id=1, replica_groups=mesh['y'=8,'xh'=2,'xl'=2,'z'=8,'c'=2] {'z'}, dimensions={0} | all-to-all | bytes 655360 | tf_op jit(solution)/shard_map/all_to_all | solution.py:38
  91.1 0.8 add_z.1
  91.9 3.4 %all-to-all-start.4 = ((bf16[8,16,384]{2,1,0:T(8,128)(2,1)}), bf16[8,16,384]{2,1,0:T(8,128)(2,1)S(1)}, u32[]{:S(2)}, u32[]{:S(2)}) async-start(bf16[8,16,384]{2,1,0:T(8,128)(2,1)} %get-tuple-element.36), calls=%async_computation.4 | async-start | bytes 196608 | tf_op jit(solution)/shard_map/all_to_all | solution.py:38
  95.3 3.1 %grad_latent.1 = bf16[1024,256]{1,0:T(8,128)(2,1)} custom-call(bf16[1024,1024]{1,0:T(8,128)(2,1)} %w_in.5, bf16[1024,256]{1,0:T(8,128)(2,1)S(1)} %get-tuple-element.38.dpre, f32[8,128]{1,0:T(8,128)S(1)} %get-tuple-element.39.scale), custom_call_target="tpu_custom_call" | custom-call | flops 536870912 | bytes 4194304 | tf_op jit(solution)/shard_map/grad_latent/pallas_call | solution.py:281
  98.4 5.5 %all-to-all-done.4.got = bf16[8,16,384]{2,1,0:T(8,128)(2,1)S(1)} async-done(((bf16[8,16,384]{2,1,0:T(8,128)(2,1)}), bf16[8,16,384]{2,1,0:T(8,128)(2,1)S(1)}, u32[]{:S(2)}, u32[]{:S(2)}) %all-to-all-start.4) | async-done | bytes 98336 | tf_op jit(solution)/shard_map/all_to_all | solution.py:38
  103.9 0.9 finish.1
Async XLA Ops:
  0.6 4.5 %copy-start = (bf16[1,1024,256]{2,1,0:T(8,128)(2,1)S(1)}, bf16[1,1024,256]{2,1,0:T(8,128)(2,1)}, u32[]{:S(2)}) copy-start(bf16[1,1024,256]{2,1,0:T(8,128)(2,1)} %param.6) | copy-start | bytes 1572868
  5.2 27.5 %collective-permute-start = (bf16[1024,256]{1,0:T(8,128)(2,1)S(1)}, bf16[1024,256]{1,0:T(8,128)(2,1)S(1)}, u32[]{:S(2)}, u32[]{:S(2)}) collective-permute-start(bf16[1024,256]{1,0:T(8,128)(2,1)S(1)} %bitcast.22), channel_id=1, source_target_pairs={{0,1},{1,0},{2,3},{3,2},{4,5},{5,4},{6,7},{7,6},{8,9},{9,8},{10,11... | collective-permute-start | bytes 1572872 | tf_op jit(solution)/shard_map/ppermute | solution.py:593
  7.1 20.5 %all-to-all-start = ((f32[16,8,256]{2,1,0:T(8,128)}), f32[16,8,256]{2,1,0:T(8,128)S(1)}, u32[]{:S(2)}, u32[]{:S(2)}) async-start(f32[16,8,256]{2,1,0:T(8,128)} %bitcast.26), calls=%async_computation | async-start | bytes 262144 | tf_op jit(solution)/shard_map/all_to_all | solution.py:38
  28.8 14.5 %all-to-all-start.1 = ((bf16[32,8,256]{2,1,0:T(8,128)(2,1)}), bf16[32,8,256]{2,1,0:T(8,128)(2,1)S(1)}, u32[]{:S(2)}, u32[]{:S(2)}) async-start(bf16[32,8,256]{2,1,0:T(8,128)(2,1)} %pairs.1), calls=%async_computation.1 | async-start | bytes 262144 | tf_op jit(solution)/shard_map/all_to_all | solution.py:38
  91.9 12.0 %all-to-all-start.4 = ((bf16[8,16,384]{2,1,0:T(8,128)(2,1)}), bf16[8,16,384]{2,1,0:T(8,128)(2,1)S(1)}, u32[]{:S(2)}, u32[]{:S(2)}) async-start(bf16[8,16,384]{2,1,0:T(8,128)(2,1)} %get-tuple-element.36), calls=%async_computation.4 | async-start | bytes 196608 | tf_op jit(solution)/shard_map/all_to_all | solution.py:38

commit v5 on v4

--- a/solution.py
+++ b/solution.py
@@ -26,12 +26,9 @@
 
 def gelu(value):
     square = value * value
-    inner = jnp.tanh(gelu_c * (value + gelu_k * square * value))
-    both = 0.5 * (1.0 + inner)
-    slope = both + 0.5 * value * (1.0 - inner * inner) * (
-        gelu_c * (1.0 + 3.0 * gelu_k * square)
-    )
-    return value * both, slope
+    share = 0.5 + 0.5 * jnp.tanh(value * (gelu_c + gelu_c * gelu_k * square))
+    bend = value * (2.0 * gelu_c + 6.0 * gelu_c * gelu_k * square)
+    return value * share, share + share * ((1.0 - share) * bend)
 
 
 def exchange(pieces, axes):
@@ -127,25 +124,27 @@
 
 
 def forward_kernel(
-    w_in, latent, w_out, hidden, slope, decoded,
-    w_in_v, latent_v, w_out_v, hidden_v, slope_v, decoded_v, sems,
+    w_in, latent, w_out, hidden, slope, decoded, w_in_v, latent_v, w_out_v, decoded_v, sems
 ):
     copies = Copies(sems)
     first = copies.start(latent, latent_v)
     loads = load_weights(copies, w_in, w_in_v)
     rows = copies.start(w_out, w_out_v)
     copies.wait(first)
+    total = None
     for here, load in zip(blocks(w_in.shape[0]), loads):
         for copy in load:
             copies.wait(copy)
         value, bend = gelu(dot(w_in_v[here, :], latent_v[...]))
-        hidden_v[here, :] = value.astype(bf16)
-        copies.start(hidden_v.at[here], hidden.at[here])
-        slope_v[here, :] = bend.astype(bf16)
-        copies.start(slope_v.at[here], slope.at[here])
-    copies.wait(rows)
-    w_out_rows = dot(row_table().astype(bf16), w_out_v[...]).astype(bf16)
-    decoded_v[...] = dot(w_out_rows, hidden_v[...])
+        value = value.astype(bf16)
+        hidden[here, :] = value
+        slope[here, :] = bend.astype(bf16)
+        if total is None:
+            copies.wait(rows)
+            w_out_rows = dot(row_table().astype(bf16), w_out_v[...]).astype(bf16)
+        part = dot(w_out_rows[:, here], value)
+        total = part if total is None else total + part
+    decoded_v[...] = total
     copies.start(decoded_v, decoded)
     copies.finish()
 
@@ -156,16 +155,15 @@
     return pl.pallas_call(
         forward_kernel,
         in_specs=[hbm()] * 3,
-        out_specs=[hbm()] * 3,
+        out_specs=[whole(), whole(), hbm()],
         out_shape=[
-            pltpu.HBM((hid, pts), bf16),
-            pltpu.HBM((hid, pts), bf16),
+            jax.ShapeDtypeStruct((hid, pts), bf16),
+            jax.ShapeDtypeStruct((hid, pts), bf16),
             pltpu.HBM((PAD, pts), f32),
         ],
         scratch_shapes=scratch(
-            ((hid, lat), bf16), ((lat, pts), bf16), ((VARS, hid), bf16),
-            ((hid, pts), bf16), ((hid, pts), bf16), ((PAD, pts), f32),
-            copies=4 * len(blocks(hid)) + 3,
+            ((hid, lat), bf16), ((lat, pts), bf16), ((VARS, hid), bf16), ((PAD, pts), f32),
+            copies=2 * len(blocks(hid)) + 3,
         ),
         compiler_params=params(16),
         name="forward",
@@ -207,8 +205,8 @@
 
 
 def prepare_kernel(
-    owner, w_out_h, target_h, area_h, var_weight_h, w_out_t_h, target, weight, area_sum,
-    w_out_v, w_out_t_v, target_v, area_v, var_weight_v, sems,
+    owner, w_out_h, target_h, area_h, var_weight_h, w_out_t, target, weight, area_sum,
+    w_out_v, target_v, area_v, var_weight_v, sems,
 ):
     copies = Copies(sems)
     inputs = [
@@ -218,11 +216,10 @@
         copies.start(var_weight_h, var_weight_v),
     ]
     copies.wait(inputs[0])
-    w_out_t_v[...] = lax.dot_general(
+    w_out_t[...] = lax.dot_general(
         w_out_v[...], row_table().astype(bf16), (((0,), (1,)), ((), ())),
         preferred_element_type=f32,
     ).astype(bf16)
-    copies.start(w_out_t_v, w_out_t_h)
     for copy in inputs[1:]:
         copies.wait(copy)
     row = lax.broadcasted_iota(jnp.int32, (OWN, VARS), 0)
@@ -243,17 +240,16 @@
     return pl.pallas_call(
         prepare_kernel,
         in_specs=[smem()] + [hbm()] * 4,
-        out_specs=[hbm()] + [whole()] * 3,
+        out_specs=[whole()] * 4,
         out_shape=[
-            pltpu.HBM((hid, PAD), bf16),
+            jax.ShapeDtypeStruct((hid, PAD), bf16),
             jax.ShapeDtypeStruct((OWN, pts), f32),
             jax.ShapeDtypeStruct((OWN, pts), f32),
             jax.ShapeDtypeStruct((8, PAD), f32),
         ],
         scratch_shapes=scratch(
-            (w_out.shape, bf16), ((hid, PAD), bf16), (target.shape, f32),
-            (area.shape, f32), (var_weight.shape, f32),
-            copies=5,
+            (w_out.shape, bf16), (target.shape, f32), (area.shape, f32), (var_weight.shape, f32),
+            copies=4,
         ),
         compiler_params=params(16),
         cost_estimate=pl.CostEstimate(flops=1 << 28, bytes_accessed=1 << 20, transcendentals=0),
@@ -352,30 +348,25 @@
 
 
 def backward_kernel(
-    core, dout, w_out_t, slope, slope_far, latent, latent_far, hidden, hidden_far,
-    terms_v, dpre_v,
-    w_out_t_v, slope_v, slope_far_v, latent_v, latent_far_v, hidden_v, hidden_far_v, sems,
+    place, dout, w_out_t, slope_v, slope_far, latent, latent_far, hidden, hidden_far,
+    own_out, right_out, across_out, left_out, dpre_v,
+    terms_v, slope_far_v, latent_v, hidden_far_v, sems,
 ):
     copies = Copies(sems)
-    me = core[0]
+    me = place[0]
     rows = terms_v.shape[1]
-    hid, pts = slope.shape
+    hid, pts = slope_v.shape
     parts = blocks(hid)
 
     def fetch(source, target, here):
         return copies.start(source.at[here], target.at[here])
 
     mine = (slice(None), pl.ds(2 * me, 2))
-    fetched = [copies.start(w_out_t, w_out_t_v)]
-    halves = [[fetch(slope, slope_v, parts[0]), fetch(slope_far, slope_far_v, parts[0])]]
-    fetched.append(copies.start(latent.at[mine], latent_v))
-    fetched.append(copies.start(latent_far.at[mine], latent_far_v))
+    near = copies.start(latent.at[mine], latent_v)
+    halves = [fetch(slope_far, slope_far_v, parts[0])]
     for here in parts[1:]:
-        halves.append([fetch(slope, slope_v, here), fetch(slope_far, slope_far_v, here)])
-    late = [
-        copies.start(hidden.at[mine], hidden_v),
-        copies.start(hidden_far.at[mine], hidden_far_v),
-    ]
+        halves.append(fetch(slope_far, slope_far_v, here))
+    late = copies.start(hidden_far.at[mine], hidden_far_v)
 
     row = lax.broadcasted_iota(jnp.int32, (PAD, pts), 0)
     last = lax.rem(row, OWN) == OWN - 1
@@ -386,17 +377,16 @@
         ride = ride + jnp.sum(jnp.where(last, value, 0.0), axis=0, keepdims=True)
         seeds.append(jnp.where(last, 0.0, value).astype(bf16))
 
-    for copy in fetched:
-        copies.wait(copy)
+    copies.wait(near)
     features = [
-        [ref[:, k].reshape(-1, pts) for k in range(2)] for ref in (latent_v, latent_far_v)
+        [latent_v[:, k].reshape(-1, pts) for k in range(2)],
+        [latent_far[:, pl.ds(2 * me + k, 1)].reshape(-1, pts) for k in range(2)],
     ]
     for here, half in zip(parts, halves):
         first = second = None
-        for copy in half:
-            copies.wait(copy)
+        copies.wait(half)
         for k, ref in enumerate((slope_v, slope_far_v)):
-            dh = dot(w_out_t_v[here, :], seeds[k])
+            dh = dot(w_out_t[here, :], seeds[k])
             dpre = (dh * ref[here, :].astype(f32)).astype(bf16)
             if k == 0:
                 dpre_v[here, :] = dpre
@@ -419,9 +409,8 @@
             for xl in range(2):
                 terms_v[2 * xh + xl, :, here] = value[xl * rows : (xl + 1) * rows].astype(bf16)
 
-    for copy in late:
-        copies.wait(copy)
-    out = dot_nt(hidden_v[...].reshape(-1, pts), seeds[0])
+    copies.wait(late)
+    out = dot_nt(hidden[:, pl.ds(2 * me, 2)].reshape(-1, pts), seeds[0])
     out += dot_nt(hidden_far_v[...].reshape(-1, pts), seeds[1])
     out = out.reshape(-1, 2, 16, PAD)
     left = out[:, 0].reshape(-1, PAD)
@@ -442,28 +431,31 @@
             piece = slice(xl * rows, (xl + 1) * rows)
             terms_v[2 * xh + xl, :, hid : hid + PAD] = left[piece].astype(bf16)
             terms_v[2 * xh + xl, :, hid + PAD :] = right[piece].astype(bf16)
-
-
-def backward(core, dout, w_out_t, slope, slope_far, latent, latent_far, hidden, hidden_far):
+    for k, out in enumerate((own_out, right_out, across_out, left_out)):
+        out[...] = terms_v[lax.rem(place[1] + k, 4)]
+
+
+def backward(place, dout, w_out_t, slope, slope_far, latent, latent_far, hidden, hidden_far):
     hid, pts = slope.shape
     plane = latent.shape[0]
-    shape = (4, plane * 16 // 2, hid + 2 * PAD)
+    shape = (plane * 16 // 2, hid + 2 * PAD)
     half = ((plane, 2, 16, pts), bf16)
     return pl.pallas_call(
         backward_kernel,
-        in_specs=[smem(), whole()] + [hbm()] * 7,
-        out_specs=[whole()] * 2,
-        out_shape=[
-            jax.ShapeDtypeStruct(shape, bf16),
-            jax.ShapeDtypeStruct((hid, pts), bf16),
-        ],
+        in_specs=[smem()] + [whole()] * 3 + [hbm()] * 2 + [whole()] * 2 + [hbm()],
+        out_specs=[whole()] * 5,
+        out_shape=[jax.ShapeDtypeStruct(shape, bf16)] * 4
+        + [jax.ShapeDtypeStruct((hid, pts), bf16)],
         scratch_shapes=scratch(
-            ((hid, PAD), bf16), ((hid, pts), bf16), ((hid, pts), bf16), half, half, half, half,
-            copies=2 * len(blocks(hid)) + 5,
+            ((4, *shape), bf16), ((hid, pts), bf16), half, half,
+            copies=len(blocks(hid)) + 2,
         ),
         compiler_params=params(24),
         name="backward",
-    )(core, dout, *in_hbm(w_out_t, slope, slope_far, latent), latent_far, *in_hbm(hidden, hidden_far))
+    )(
+        place, dout, w_out_t, slope, *in_hbm(slope_far, latent), latent_far, hidden,
+        *in_hbm(hidden_far),
+    )
 
 
 def split_again(tile):
@@ -476,24 +468,24 @@
     return jnp.where(even, high, jnp.where(odd, low, tile))
 
 
-def add_x_kernel(hid, got, out):
-    value = got[0].astype(f32)
-    for k in range(1, got.shape[0]):
-        value = value + got[k].astype(f32)
+def add_x_kernel(hid, own, right, across, left, out):
+    value = own[...].astype(f32)
+    for ref in (right, across, left):
+        value = value + ref[...].astype(f32)
     out[:, 0:hid] = value[:, 0:hid].astype(bf16)
     out[:, hid : hid + PAD] = split_again(value[:, hid : hid + PAD]).astype(bf16)
     out[:, hid + PAD :] = value[:, hid + PAD :].astype(bf16)
 
 
-def add_x(got, hid):
+def add_x(hid, *parts):
     return pl.pallas_call(
         functools.partial(add_x_kernel, hid),
-        in_specs=[whole()],
+        in_specs=[whole()] * 4,
         out_specs=whole(),
-        out_shape=jax.ShapeDtypeStruct(got.shape[1:], bf16),
+        out_shape=jax.ShapeDtypeStruct(parts[0].shape, bf16),
         compiler_params=params(8),
         name="add_x",
-    )(got)
+    )(*parts)
 
 
 def pick(head, k):
@@ -601,15 +593,20 @@
     hidden_far, slope_far = far_forward(w_in, far)
 
     groups = lambda value: value.reshape(n_plane, 2 * n_core, 16, pts)
-    terms, dpre = backward(
-        core.astype(jnp.int32)[None],
+    own_part, right, across, left, dpre = backward(
+        jnp.stack([core, lax.axis_index(CHIP_X)]).astype(jnp.int32),
         dout_got.reshape(n_ens, n_core, own, pts),
         w_out_t, slope, slope_far,
         groups(features), groups(far), groups(hidden), groups(hidden_far),
     )
 
-    got = exchange(terms, CHIP_X)
-    got = exchange(add_x(got, hid).reshape(n_z, 16, hid + 2 * PAD), "z")
+    n_x = lax.axis_size(CHIP_X)
+    sent = []
+    for part, far_by in ((across, 2), (right, 1), (left, n_x - 1)):
+        sent.append(
+            lax.ppermute(part, CHIP_X, [(k, (k + far_by) % n_x) for k in range(n_x)])
+        )
+    got = exchange(add_x(hid, own_part, *sent).reshape(n_z, 16, hid + 2 * PAD), "z")
     got, scale = add_z(got, hid, count * lax.axis_size("xh"), points_all)
     got = exchange(got, "y")
     grad_lat = grad_latent(w_in, dpre, scale)

time: 105 us -> 106 us (level)
  blocking collectives: 43.9 us -> 23.6 us
  waiting for transfers between devices: 21.9 us -> 33.3 us
  starting transfers between devices: 17.9 us -> 27.5 us
    all_to_all x2 -> x1, blocking collectives: 43.9 us -> 23.6 us  [exchange(): return lax.all_to_all(pieces, axes, split_axis=0, concat_axis=0, tiled=True)]
    ppermute x0 -> x3, waiting for transfers between devices: none -> 10.8 us  [per_device(): lax.ppermute(part, CHIP_X, [(k, (k + far_by) % n_x) for k in range(n_x)])]
    ppermute x0 -> x3, starting transfers between devices: none -> 9.61 us  [per_device(): lax.ppermute(part, CHIP_X, [(k, (k + far_by) % n_x) for k in range(n_x)])]
  transfers between devices with their start and end apart: 4 -> 7, of which waited for: 3 -> 6; matrix products, arithmetic and copies ran while one was open for 0% -> 0% of each run, Pallas kernels for 10% -> 9%
where the time goes in v5:
time: 106 us
  waiting for transfers between devices  33.3 us (31%)
  starting transfers between devices  27.5 us (26%)
  blocking collectives  23.6 us (22%)
  Pallas kernels  20.3 us (19%)
    all_to_all x1, blocking collectives, exchange(): return lax.all_to_all(pieces, axes, split_axis=0, concat_axis=0, tiled=True)  23.6 us
    all_to_all x3, waiting for transfers between devices, exchange(): return lax.all_to_all(pieces, axes, split_axis=0, concat_axis=0, tiled=True)  22.5 us
    all_to_all x3, starting transfers between devices, exchange(): return lax.all_to_all(pieces, axes, split_axis=0, concat_axis=0, tiled=True)  16 us
    ppermute x3, waiting for transfers between devices, per_device(): lax.ppermute(part, CHIP_X, [(k, (k + far_by) % n_x) for k in range(n_x)])  10.8 us
    ppermute x3, starting transfers between devices, per_device(): lax.ppermute(part, CHIP_X, [(k, (k + far_by) % n_x) for k in range(n_x)])  9.61 us
    pallas_call x1, Pallas kernels, forward(): pl.pallas_call(forward_kernel, in_specs=[hbm()] * 3, out_specs=[whole(),...  4.66 us
    pallas_call x1, Pallas kernels, backward(): pl.pallas_call(backward_kernel, in_specs=[smem()] + [whole()] * 3 + [hbm(...  3.93 us
    pallas_call x1, Pallas kernels, far_forward(): pl.pallas_call(far_kernel, in_specs=[hbm(), whole()], out_specs=[hbm()] *...  3.86 us
  transfers between devices with their start and end apart: 7, of which 6 were waited for; matrix products, arithmetic and copies ran while one was open for 0% of the time, Pallas kernels for 9%

profile of v5, /device:TPU:2, one launch (start us, length us, event | category | flops | bytes accessed | tf_op | source)
XLA Modules:
  0.0 105.6 jit_solution(14534318744921248971)
XLA Ops:
  0.6 4.7 %forward.1 = (bf16[1024,256]{1,0:T(8,128)(2,1)S(1)}, bf16[1024,256]{1,0:T(8,128)(2,1)S(1)}, f32[128,256]{1,0:T(8,128)}) custom-call(bf16[1024,1024]{1,0:T(8,128)(2,1)} %w_in.5, bf16[1024,256]{1,0:T(8,128)(2,1)} %bitcast.22, bf16[99,1024]{1,0:T(8,128)(2,1)} %w_out_h), custom_call_target="tpu_custom_call" | custom-call | tf_op jit(solution)/shard_map/forward/pallas_call | solution.py:155
  5.3 1.9 %collective-permute-start = (bf16[1024,256]{1,0:T(8,128)(2,1)S(1)}, bf16[1024,256]{1,0:T(8,128)(2,1)S(1)}, u32[]{:S(2)}, u32[]{:S(2)}) collective-permute-start(bf16[1024,256]{1,0:T(8,128)(2,1)S(1)} %bitcast.24), channel_id=1, source_target_pairs={{0,1},{1,0},{2,3},{3,2},{4,5},{5,4},{6,7},{7,6},{8,9},{9,8},{10,11... | collective-permute-start | bytes 1572872 | tf_op jit(solution)/shard_map/ppermute | solution.py:585
  7.2 8.8 %all-to-all-start = ((f32[16,8,256]{2,1,0:T(8,128)}), f32[16,8,256]{2,1,0:T(8,128)S(1)}, u32[]{:S(2)}, u32[]{:S(2)}) async-start(f32[16,8,256]{2,1,0:T(8,128)} %bitcast.27), calls=%async_computation | async-start | bytes 262144 | tf_op jit(solution)/shard_map/all_to_all | solution.py:35
  16.0 1.5 %prepare.1 = (bf16[1024,128]{1,0:T(8,128)(2,1)S(1)}, f32[8,256]{1,0:T(8,128)S(1)}, f32[8,256]{1,0:T(8,128)S(1)}, f32[8,128]{1,0:T(8,128)S(1)}) custom-call(s32[1]{0:T(128)} %bitcast.5.owner, bf16[99,1024]{1,0:T(8,128)(2,1)} %w_out_h, f32[99,256]{1,0:T(8,128)} %target_h.1, f32[1,256]{1,0:T(1,128)} %bitcast.30, f32[1,99]{1,0:T(1,128)} %bitcast.31), custom_call_target="tpu_custom_call" | custom-call | flops 268435456 | bytes 1048576 | tf_op jit(solution)/shard_map/prepare/pallas_call | solution.py:240
  17.5 10.3 %all-to-all-done.fields = f32[16,8,256]{2,1,0:T(8,128)S(1)} async-done(((f32[16,8,256]{2,1,0:T(8,128)}), f32[16,8,256]{2,1,0:T(8,128)S(1)}, u32[]{:S(2)}, u32[]{:S(2)}) %all-to-all-start) | async-done | bytes 131104 | tf_op jit(solution)/shard_map/all_to_all | solution.py:35
  27.8 1.2 %pairs.1 = bf16[32,8,256]{2,1,0:T(8,128)(2,1)} custom-call(f32[16,8,256]{2,1,0:T(8,128)S(1)} %all-to-all-done.fields, f32[8,256]{1,0:T(8,128)S(1)} %get-tuple-element.28.target, f32[8,256]{1,0:T(8,128)S(1)} %get-tuple-element.29.weight, f32[8,128]{1,0:T(8,128)S(1)} %get-tuple-element.30.area_sum), custom_call_target="tpu_custom_call" | custom-call | tf_op jit(solution)/shard_map/pairs/pallas_call | solution.py:339
  28.9 3.9 %all-to-all-start.1 = ((bf16[32,8,256]{2,1,0:T(8,128)(2,1)}), bf16[32,8,256]{2,1,0:T(8,128)(2,1)S(1)}, u32[]{:S(2)}, u32[]{:S(2)}) async-start(bf16[32,8,256]{2,1,0:T(8,128)(2,1)} %pairs.1), calls=%async_computation.1 | async-start | bytes 262144 | tf_op jit(solution)/shard_map/all_to_all | solution.py:35
  32.8 0.1 pad_add_fusion.place
  32.9 3.9 %far_forward.1 = (bf16[1024,256]{1,0:T(8,128)(2,1)}, bf16[1024,256]{1,0:T(8,128)(2,1)}) custom-call(bf16[1024,1024]{1,0:T(8,128)(2,1)} %w_in.5, bf16[1024,256]{1,0:T(8,128)(2,1)S(1)} %collective-permute-done.latent), custom_call_target="tpu_custom_call" | custom-call | flops 536870912 | bytes 4194304 | tf_op jit(solution)/shard_map/far_forward/pallas_call | solution.py:190
  36.8 6.7 %all-to-all-done.1 = bf16[32,8,256]{2,1,0:T(8,128)(2,1)S(1)} async-done(((bf16[32,8,256]{2,1,0:T(8,128)(2,1)}), bf16[32,8,256]{2,1,0:T(8,128)(2,1)S(1)}, u32[]{:S(2)}, u32[]{:S(2)}) %all-to-all-start.1) | async-done | bytes 131104 | tf_op jit(solution)/shard_map/all_to_all | solution.py:35
  43.5 3.9 %backward.1 = (bf16[128,1280]{1,0:T(8,128)(2,1)S(1)}, bf16[128,1280]{1,0:T(8,128)(2,1)S(1)}, bf16[128,1280]{1,0:T(8,128)(2,1)S(1)}, bf16[128,1280]{1,0:T(8,128)(2,1)S(1)}, bf16[1024,256]{1,0:T(8,128)(2,1)S(1)}) custom-call(s32[2]{0:T(128)S(1)} %pad_add_fusion.place, bf16[16,2,8,256]{3,2,1,0:T(8,128)(2,1)S(1)} %bitcast.21, ...), custom_call_target="tpu_custom_call" | custom-call | tf_op jit(solution)/shard_map/backward/pallas_call | solution.py:443
  47.4 3.8 %collective-permute-start.1 = (bf16[128,1280]{1,0:T(8,128)(2,1)S(1)}, bf16[128,1280]{1,0:T(8,128)(2,1)S(1)}, u32[]{:S(2)}, u32[]{:S(2)}) collective-permute-start(bf16[128,1280]{1,0:T(8,128)(2,1)S(1)} %get-tuple-element.39), channel_id=1, source_target_pairs={{0,32},{16,48},{32,0},{48,16},{1,33},{17,49},{33,1},{49,17},{2,34}... | collective-permute-start | bytes 983048 | tf_op jit(solution)/shard_map/ppermute | solution.py:607
  51.2 2.9 %collective-permute-start.2 = (bf16[128,1280]{1,0:T(8,128)(2,1)S(1)}, bf16[128,1280]{1,0:T(8,128)(2,1)S(1)}, u32[]{:S(2)}, u32[]{:S(2)}) collective-permute-start(bf16[128,1280]{1,0:T(8,128)(2,1)S(1)} %get-tuple-element.40), channel_id=1, source_target_pairs={{0,16},{16,32},{32,48},{48,0},{1,17},{17,33},{33,49},{49,1},{2,18}... | collective-permute-start | bytes 983048 | tf_op jit(solution)/shard_map/ppermute | solution.py:607
  54.1 2.9 %collective-permute-start.3 = (bf16[128,1280]{1,0:T(8,128)(2,1)S(1)}, bf16[128,1280]{1,0:T(8,128)(2,1)S(1)}, u32[]{:S(2)}, u32[]{:S(2)}) collective-permute-start(bf16[128,1280]{1,0:T(8,128)(2,1)S(1)} %get-tuple-element.41), channel_id=1, source_target_pairs={{0,48},{16,0},{32,16},{48,32},{1,49},{17,1},{33,17},{49,33},{2,50}... | collective-permute-start | bytes 983048 | tf_op jit(solution)/shard_map/ppermute | solution.py:607
  57.0 4.4 %collective-permute-done.1.right = bf16[128,1280]{1,0:T(8,128)(2,1)S(1)} collective-permute-done((bf16[128,1280]{1,0:T(8,128)(2,1)S(1)}, bf16[128,1280]{1,0:T(8,128)(2,1)S(1)}, u32[]{:S(2)}, u32[]{:S(2)}) %collective-permute-start.1) | collective-permute-done | bytes 327712 | tf_op jit(solution)/shard_map/ppermute | solution.py:607
  61.4 5.1 %collective-permute-done.2.across = bf16[128,1280]{1,0:T(8,128)(2,1)S(1)} collective-permute-done((bf16[128,1280]{1,0:T(8,128)(2,1)S(1)}, bf16[128,1280]{1,0:T(8,128)(2,1)S(1)}, u32[]{:S(2)}, u32[]{:S(2)}) %collective-permute-start.2) | collective-permute-done | bytes 327712 | tf_op jit(solution)/shard_map/ppermute | solution.py:607
  66.5 1.4 %collective-permute-done.3.left = bf16[128,1280]{1,0:T(8,128)(2,1)S(1)} collective-permute-done((bf16[128,1280]{1,0:T(8,128)(2,1)S(1)}, bf16[128,1280]{1,0:T(8,128)(2,1)S(1)}, u32[]{:S(2)}, u32[]{:S(2)}) %collective-permute-start.3) | collective-permute-done | bytes 327712 | tf_op jit(solution)/shard_map/ppermute | solution.py:607
  67.9 0.4 add_x.1
  68.3 23.6 %all_to_all.20.got = bf16[8,16,1280]{2,1,0:T(8,128)(2,1)S(1)} all-to-all(bf16[8,16,1280]{2,1,0:T(8,128)(2,1)S(1)} %bitcast.19), channel_id=1, replica_groups=mesh['y'=8,'xh'=2,'xl'=2,'z'=8,'c'=2] {'z'}, dimensions={0} | all-to-all | bytes 655360 | tf_op jit(solution)/shard_map/all_to_all | solution.py:35
  91.8 0.8 add_z.1
  92.7 3.4 %all-to-all-start.3 = ((bf16[8,16,384]{2,1,0:T(8,128)(2,1)}), bf16[8,16,384]{2,1,0:T(8,128)(2,1)S(1)}, u32[]{:S(2)}, u32[]{:S(2)}) async-start(bf16[8,16,384]{2,1,0:T(8,128)(2,1)} %get-tuple-element.42), calls=%async_computation.3 | async-start | bytes 196608 | tf_op jit(solution)/shard_map/all_to_all | solution.py:35
  96.1 3.1 %grad_latent.1 = bf16[1024,256]{1,0:T(8,128)(2,1)} custom-call(bf16[1024,1024]{1,0:T(8,128)(2,1)} %w_in.5, bf16[1024,256]{1,0:T(8,128)(2,1)S(1)} %get-tuple-element.44.dpre, f32[8,128]{1,0:T(8,128)S(1)} %get-tuple-element.45.scale), custom_call_target="tpu_custom_call" | custom-call | flops 536870912 | bytes 4194304 | tf_op jit(solution)/shard_map/grad_latent/pallas_call | solution.py:277
  99.2 5.5 %all-to-all-done.3.got = bf16[8,16,384]{2,1,0:T(8,128)(2,1)S(1)} async-done(((bf16[8,16,384]{2,1,0:T(8,128)(2,1)}), bf16[8,16,384]{2,1,0:T(8,128)(2,1)S(1)}, u32[]{:S(2)}, u32[]{:S(2)}) %all-to-all-start.3) | async-done | bytes 98336 | tf_op jit(solution)/shard_map/all_to_all | solution.py:35
  104.7 0.9 finish.1
  (3 shorter events, 0.0 us)
Async XLA Ops:
  0.6 4.7 %copy-start = (bf16[1,1024,256]{2,1,0:T(8,128)(2,1)S(1)}, bf16[1,1024,256]{2,1,0:T(8,128)(2,1)}, u32[]{:S(2)}) copy-start(bf16[1,1024,256]{2,1,0:T(8,128)(2,1)} %param.6) | copy-start | bytes 1572868
  5.3 27.6 %collective-permute-start = (bf16[1024,256]{1,0:T(8,128)(2,1)S(1)}, bf16[1024,256]{1,0:T(8,128)(2,1)S(1)}, u32[]{:S(2)}, u32[]{:S(2)}) collective-permute-start(bf16[1024,256]{1,0:T(8,128)(2,1)S(1)} %bitcast.24), channel_id=1, source_target_pairs={{0,1},{1,0},{2,3},{3,2},{4,5},{5,4},{6,7},{7,6},{8,9},{9,8},{10,11... | collective-permute-start | bytes 1572872 | tf_op jit(solution)/shard_map/ppermute | solution.py:585
  7.2 20.5 %all-to-all-start = ((f32[16,8,256]{2,1,0:T(8,128)}), f32[16,8,256]{2,1,0:T(8,128)S(1)}, u32[]{:S(2)}, u32[]{:S(2)}) async-start(f32[16,8,256]{2,1,0:T(8,128)} %bitcast.27), calls=%async_computation | async-start | bytes 262144 | tf_op jit(solution)/shard_map/all_to_all | solution.py:35
  28.9 14.5 %all-to-all-start.1 = ((bf16[32,8,256]{2,1,0:T(8,128)(2,1)}), bf16[32,8,256]{2,1,0:T(8,128)(2,1)S(1)}, u32[]{:S(2)}, u32[]{:S(2)}) async-start(bf16[32,8,256]{2,1,0:T(8,128)(2,1)} %pairs.1), calls=%async_computation.1 | async-start | bytes 262144 | tf_op jit(solution)/shard_map/all_to_all | solution.py:35
  47.4 14.0 %collective-permute-start.1 = (bf16[128,1280]{1,0:T(8,128)(2,1)S(1)}, bf16[128,1280]{1,0:T(8,128)(2,1)S(1)}, u32[]{:S(2)}, u32[]{:S(2)}) collective-permute-start(bf16[128,1280]{1,0:T(8,128)(2,1)S(1)} %get-tuple-element.39), channel_id=1, source_target_pairs={{0,32},{16,48},{32,0},{48,16},{1,33},{17,49},{33,1},{49,17},{2,34}... | collective-permute-start | bytes 983048 | tf_op jit(solution)/shard_map/ppermute | solution.py:607
  51.2 15.3 %collective-permute-start.2 = (bf16[128,1280]{1,0:T(8,128)(2,1)S(1)}, bf16[128,1280]{1,0:T(8,128)(2,1)S(1)}, u32[]{:S(2)}, u32[]{:S(2)}) collective-permute-start(bf16[128,1280]{1,0:T(8,128)(2,1)S(1)} %get-tuple-element.40), channel_id=1, source_target_pairs={{0,16},{16,32},{32,48},{48,0},{1,17},{17,33},{33,49},{49,1},{2,18}... | collective-permute-start | bytes 983048 | tf_op jit(solution)/shard_map/ppermute | solution.py:607
  54.1 13.8 %collective-permute-start.3 = (bf16[128,1280]{1,0:T(8,128)(2,1)S(1)}, bf16[128,1280]{1,0:T(8,128)(2,1)S(1)}, u32[]{:S(2)}, u32[]{:S(2)}) collective-permute-start(bf16[128,1280]{1,0:T(8,128)(2,1)S(1)} %get-tuple-element.41), channel_id=1, source_target_pairs={{0,48},{16,0},{32,16},{48,32},{1,49},{17,1},{33,17},{49,33},{2,50}... | collective-permute-start | bytes 983048 | tf_op jit(solution)/shard_map/ppermute | solution.py:607
  92.7 12.0 %all-to-all-start.3 = ((bf16[8,16,384]{2,1,0:T(8,128)(2,1)}), bf16[8,16,384]{2,1,0:T(8,128)(2,1)S(1)}, u32[]{:S(2)}, u32[]{:S(2)}) async-start(bf16[8,16,384]{2,1,0:T(8,128)(2,1)} %get-tuple-element.42), calls=%async_computation.3 | async-start | bytes 196608 | tf_op jit(solution)/shard_map/all_to_all | solution.py:35

commit v6 on v5

--- a/solution.py
+++ b/solution.py
@@ -14,7 +14,7 @@
 ENS = ("y", "xh")
 PLANE = ("xl", "z")
 CHIP_X = ("xh", "xl")
-BLOCK = 256
+BLOCK = 1024
 
 smooth_sq = 0.01
 gelu_c = 0.7978845608
@@ -92,7 +92,8 @@
 
 
 def blocks(size):
-    return [slice(at, at + BLOCK) for at in range(0, size, BLOCK)]
+    step = min(size, BLOCK)
+    return [slice(at, at + step) for at in range(0, size, step)]
 
 
 def spare(k):
@@ -110,17 +111,36 @@
     return lax.broadcasted_iota(jnp.int32, shape, len(shape) - 1)
 
 
-def load_weights(copies, w_in, w_in_v):
-    loads = []
-    for here in blocks(w_in.shape[0]):
-        middle = (here.start + here.stop) // 2
-        loads.append(
-            [
-                copies.start(w_in.at[part], w_in_v.at[part])
-                for part in (slice(here.start, middle), slice(middle, here.stop))
-            ]
-        )
-    return loads
+class Stream:
+    def __init__(self, copies, source, target):
+        self.copies = copies
+        self.started = []
+        for here in blocks(source.shape[0]):
+            middle = (here.start + here.stop) // 2
+            self.started.append(
+                [
+                    copies.start(source.at[part], target.at[part])
+                    for part in (slice(here.start, middle), slice(middle, here.stop))
+                ]
+            )
+
+    def wait(self, k):
+        for copy in self.started[k]:
+            self.copies.wait(copy)
+
+
+def products(weights, w_in_v, latent):
+    parts = blocks(w_in_v.shape[0])
+    ahead = None
+    for k, here in enumerate(parts):
+        if ahead is None:
+            weights.wait(k)
+            ahead = dot(w_in_v[here, :], latent[...])
+        now = ahead
+        if k + 1 < len(parts):
+            weights.wait(k + 1)
+            ahead = dot(w_in_v[parts[k + 1], :], latent[...])
+        yield here, now
 
 
 def forward_kernel(
@@ -128,20 +148,17 @@
 ):
     copies = Copies(sems)
     first = copies.start(latent, latent_v)
-    loads = load_weights(copies, w_in, w_in_v)
     rows = copies.start(w_out, w_out_v)
+    weights = Stream(copies, w_in, w_in_v)
     copies.wait(first)
+    copies.wait(rows)
+    w_out_rows = dot(row_table().astype(bf16), w_out_v[...]).astype(bf16)
     total = None
-    for here, load in zip(blocks(w_in.shape[0]), loads):
-        for copy in load:
-            copies.wait(copy)
-        value, bend = gelu(dot(w_in_v[here, :], latent_v[...]))
+    for here, product in products(weights, w_in_v, latent_v):
+        value, bend = gelu(product)
         value = value.astype(bf16)
         hidden[here, :] = value
         slope[here, :] = bend.astype(bf16)
-        if total is None:
-            copies.wait(rows)
-            w_out_rows = dot(row_table().astype(bf16), w_out_v[...]).astype(bf16)
         part = dot(w_out_rows[:, here], value)
         total = part if total is None else total + part
     decoded_v[...] = total
@@ -163,7 +180,7 @@
         ],
         scratch_shapes=scratch(
             ((hid, lat), bf16), ((lat, pts), bf16), ((VARS, hid), bf16), ((PAD, pts), f32),
-            copies=2 * len(blocks(hid)) + 3,
+            copies=4 * len(blocks(hid)) + 3,
         ),
         compiler_params=params(16),
         name="forward",
@@ -172,11 +189,9 @@
 
 def far_kernel(w_in, latent, hidden, slope, w_in_v, hidden_v, slope_v, sems):
     copies = Copies(sems)
-    loads = load_weights(copies, w_in, w_in_v)
-    for here, load in zip(blocks(w_in.shape[0]), loads):
-        for copy in load:
-            copies.wait(copy)
-        value, bend = gelu(dot(w_in_v[here, :], latent[...]))
+    weights = Stream(copies, w_in, w_in_v)
+    for here, product in products(weights, w_in_v, latent):
+        value, bend = gelu(product)
         hidden_v[here, :] = value.astype(bf16)
         copies.start(hidden_v.at[here], hidden.at[here])
         slope_v[here, :] = bend.astype(bf16)
@@ -194,7 +209,7 @@
         out_shape=[pltpu.HBM((hid, pts), bf16), pltpu.HBM((hid, pts), bf16)],
         scratch_shapes=scratch(
             ((hid, lat), bf16), ((hid, pts), bf16), ((hid, pts), bf16),
-            copies=4 * len(blocks(hid)),
+            copies=6 * len(blocks(hid)),
         ),
         compiler_params=params(16),
         cost_estimate=pl.CostEstimate(
@@ -349,8 +364,7 @@
 
 def backward_kernel(
     place, dout, w_out_t, slope_v, slope_far, latent, latent_far, hidden, hidden_far,
-    own_out, right_out, across_out, left_out, dpre_v,
-    terms_v, slope_far_v, latent_v, hidden_far_v, sems,
+    terms_v, dpre_v, slope_far_v, latent_v, hidden_far_v, sems,
 ):
     copies = Copies(sems)
     me = place[0]
@@ -378,13 +392,15 @@
         seeds.append(jnp.where(last, 0.0, value).astype(bf16))
 
     copies.wait(near)
+    for half in halves:
+        copies.wait(half)
+    copies.wait(late)
     features = [
         [latent_v[:, k].reshape(-1, pts) for k in range(2)],
         [latent_far[:, pl.ds(2 * me + k, 1)].reshape(-1, pts) for k in range(2)],
     ]
     for here, half in zip(parts, halves):
         first = second = None
-        copies.wait(half)
         for k, ref in enumerate((slope_v, slope_far_v)):
             dh = dot(w_out_t[here, :], seeds[k])
             dpre = (dh * ref[here, :].astype(f32)).astype(bf16)
@@ -409,7 +425,6 @@
             for xl in range(2):
                 terms_v[2 * xh + xl, :, here] = value[xl * rows : (xl + 1) * rows].astype(bf16)
 
-    copies.wait(late)
     out = dot_nt(hidden[:, pl.ds(2 * me, 2)].reshape(-1, pts), seeds[0])
     out += dot_nt(hidden_far_v[...].reshape(-1, pts), seeds[1])
     out = out.reshape(-1, 2, 16, PAD)
@@ -431,23 +446,23 @@
             piece = slice(xl * rows, (xl + 1) * rows)
             terms_v[2 * xh + xl, :, hid : hid + PAD] = left[piece].astype(bf16)
             terms_v[2 * xh + xl, :, hid + PAD :] = right[piece].astype(bf16)
-    for k, out in enumerate((own_out, right_out, across_out, left_out)):
-        out[...] = terms_v[lax.rem(place[1] + k, 4)]
 
 
 def backward(place, dout, w_out_t, slope, slope_far, latent, latent_far, hidden, hidden_far):
     hid, pts = slope.shape
     plane = latent.shape[0]
-    shape = (plane * 16 // 2, hid + 2 * PAD)
+    shape = (4, plane * 16 // 2, hid + 2 * PAD)
     half = ((plane, 2, 16, pts), bf16)
     return pl.pallas_call(
         backward_kernel,
         in_specs=[smem()] + [whole()] * 3 + [hbm()] * 2 + [whole()] * 2 + [hbm()],
-        out_specs=[whole()] * 5,
-        out_shape=[jax.ShapeDtypeStruct(shape, bf16)] * 4
-        + [jax.ShapeDtypeStruct((hid, pts), bf16)],
+        out_specs=[whole()] * 2,
+        out_shape=[
+            jax.ShapeDtypeStruct(shape, bf16),
+            jax.ShapeDtypeStruct((hid, pts), bf16),
+        ],
         scratch_shapes=scratch(
-            ((4, *shape), bf16), ((hid, pts), bf16), half, half,
+            ((hid, pts), bf16), half, half,
             copies=len(blocks(hid)) + 2,
         ),
         compiler_params=params(24),
@@ -468,24 +483,24 @@
     return jnp.where(even, high, jnp.where(odd, low, tile))
 
 
-def add_x_kernel(hid, own, right, across, left, out):
-    value = own[...].astype(f32)
-    for ref in (right, across, left):
-        value = value + ref[...].astype(f32)
+def add_x_kernel(hid, got, out):
+    value = got[0].astype(f32)
+    for k in range(1, got.shape[0]):
+        value = value + got[k].astype(f32)
     out[:, 0:hid] = value[:, 0:hid].astype(bf16)
     out[:, hid : hid + PAD] = split_again(value[:, hid : hid + PAD]).astype(bf16)
     out[:, hid + PAD :] = value[:, hid + PAD :].astype(bf16)
 
 
-def add_x(hid, *parts):
+def add_x(got, hid):
     return pl.pallas_call(
         functools.partial(add_x_kernel, hid),
-        in_specs=[whole()] * 4,
+        in_specs=[whole()],
         out_specs=whole(),
-        out_shape=jax.ShapeDtypeStruct(parts[0].shape, bf16),
+        out_shape=jax.ShapeDtypeStruct(got.shape[1:], bf16),
         compiler_params=params(8),
         name="add_x",
-    )(*parts)
+    )(got)
 
 
 def pick(head, k):
@@ -593,20 +608,15 @@
     hidden_far, slope_far = far_forward(w_in, far)
 
     groups = lambda value: value.reshape(n_plane, 2 * n_core, 16, pts)
-    own_part, right, across, left, dpre = backward(
-        jnp.stack([core, lax.axis_index(CHIP_X)]).astype(jnp.int32),
+    terms, dpre = backward(
+        core.astype(jnp.int32)[None],
         dout_got.reshape(n_ens, n_core, own, pts),
         w_out_t, slope, slope_far,
         groups(features), groups(far), groups(hidden), groups(hidden_far),
     )
 
-    n_x = lax.axis_size(CHIP_X)
-    sent = []
-    for part, far_by in ((across, 2), (right, 1), (left, n_x - 1)):
-        sent.append(
-            lax.ppermute(part, CHIP_X, [(k, (k + far_by) % n_x) for k in range(n_x)])
-        )
-    got = exchange(add_x(hid, own_part, *sent).reshape(n_z, 16, hid + 2 * PAD), "z")
+    got = exchange(terms, CHIP_X)
+    got = exchange(add_x(got, hid).reshape(n_z, 16, hid + 2 * PAD), "z")
     got, scale = add_z(got, hid, count * lax.axis_size("xh"), points_all)
     got = exchange(got, "y")
     grad_lat = grad_latent(w_in, dpre, scale)

time: 106 us -> 104 us (0.981)
  blocking collectives: 23.6 us -> 43.9 us
  waiting for transfers between devices: 33.3 us -> 22.7 us
  starting transfers between devices: 27.5 us -> 17.9 us
  Pallas kernels: 20.3 us -> 17.8 us
    all_to_all x1 -> x2, blocking collectives: 23.6 us -> 43.9 us  [exchange(): return lax.all_to_all(pieces, axes, split_axis=0, concat_axis=0, tiled=True)]
    ppermute x3 -> x0, waiting for transfers between devices: 10.8 us -> none  [per_device(): lax.ppermute(part, CHIP_X, [(k, (k + far_by) % n_x) for k in range(n_x)])]
    ppermute x3 -> x0, starting transfers between devices: 9.61 us -> none  [per_device(): lax.ppermute(part, CHIP_X, [(k, (k + far_by) % n_x) for k in range(n_x)])]
    pallas_call x1, Pallas kernels: 3.93 us -> 2.55 us  [backward(): pl.pallas_call(backward_kernel, in_specs=[smem()] + [whole()] * 3 + [hbm(...]
  transfers between devices with their start and end apart: 7 -> 4, of which waited for: 6 -> 3; matrix products, arithmetic and copies ran while one was open for 0% -> 0% of each run, Pallas kernels for 9% -> 9%
where the time goes in v6:
time: 104 us; the launch traced here: 103 us
  blocking collectives  43.9 us (42%)
  waiting for transfers between devices  22.7 us (22%)
  starting transfers between devices  17.9 us (17%)
  Pallas kernels  17.8 us (17%)
    all_to_all x2, blocking collectives, exchange(): return lax.all_to_all(pieces, axes, split_axis=0, concat_axis=0, tiled=True)  43.9 us
    all_to_all x3, waiting for transfers between devices, exchange(): return lax.all_to_all(pieces, axes, split_axis=0, concat_axis=0, tiled=True)  22.7 us
    all_to_all x3, starting transfers between devices, exchange(): return lax.all_to_all(pieces, axes, split_axis=0, concat_axis=0, tiled=True)  16 us
    pallas_call x1, Pallas kernels, forward(): pl.pallas_call(forward_kernel, in_specs=[hbm()] * 3, out_specs=[whole(),...  3.81 us
    pallas_call x1, Pallas kernels, far_forward(): pl.pallas_call(far_kernel, in_specs=[hbm(), whole()], out_specs=[hbm()] *...  3.6 us
    pallas_call x1, Pallas kernels, grad_latent(): pl.pallas_call(grad_kernel, in_specs=[hbm(), whole(), whole()], out_specs...  3.2 us
    pallas_call x1, Pallas kernels, backward(): pl.pallas_call(backward_kernel, in_specs=[smem()] + [whole()] * 3 + [hbm(...  2.55 us
  transfers between devices with their start and end apart: 4, of which 3 were waited for; matrix products, arithmetic and copies ran while one was open for 0% of the time, Pallas kernels for 9%

profile of v6, /device:TPU:2, one launch (start us, length us, event | category | flops | bytes accessed | tf_op | source)
XLA Modules:
  0.0 103.0 jit_solution(1788992167416636310)
XLA Ops:
  0.6 0.0 copy-start
  0.6 3.8 %forward.1 = (bf16[1024,256]{1,0:T(8,128)(2,1)S(1)}, bf16[1024,256]{1,0:T(8,128)(2,1)S(1)}, f32[128,256]{1,0:T(8,128)}) custom-call(bf16[1024,1024]{1,0:T(8,128)(2,1)} %w_in.5, bf16[1024,256]{1,0:T(8,128)(2,1)} %bitcast.21, bf16[99,1024]{1,0:T(8,128)(2,1)} %w_out_h), custom_call_target="tpu_custom_call" | custom-call | tf_op jit(solution)/shard_map/forward/pallas_call | solution.py:172
  4.5 0.0 copy-done
  4.5 1.9 %collective-permute-start = (bf16[1024,256]{1,0:T(8,128)(2,1)S(1)}, bf16[1024,256]{1,0:T(8,128)(2,1)S(1)}, u32[]{:S(2)}, u32[]{:S(2)}) collective-permute-start(bf16[1024,256]{1,0:T(8,128)(2,1)S(1)} %bitcast.23), channel_id=1, source_target_pairs={{0,1},{1,0},{2,3},{3,2},{4,5},{5,4},{6,7},{7,6},{8,9},{9,8},{10,11... | collective-permute-start | bytes 1572872 | tf_op jit(solution)/shard_map/ppermute | solution.py:600
  6.4 8.8 %all-to-all-start = ((f32[16,8,256]{2,1,0:T(8,128)}), f32[16,8,256]{2,1,0:T(8,128)S(1)}, u32[]{:S(2)}, u32[]{:S(2)}) async-start(f32[16,8,256]{2,1,0:T(8,128)} %bitcast.26), calls=%async_computation | async-start | bytes 262144 | tf_op jit(solution)/shard_map/all_to_all | solution.py:35
  15.2 1.5 %prepare.1 = (bf16[1024,128]{1,0:T(8,128)(2,1)S(1)}, f32[8,256]{1,0:T(8,128)S(1)}, f32[8,256]{1,0:T(8,128)S(1)}, f32[8,128]{1,0:T(8,128)S(1)}) custom-call(s32[1]{0:T(128)} %bitcast.4.owner, bf16[99,1024]{1,0:T(8,128)(2,1)} %w_out_h, f32[99,256]{1,0:T(8,128)} %target_h.1, f32[1,256]{1,0:T(1,128)} %bitcast.29, f32[1,99]{1,0:T(1,128)} %bitcast.30), custom_call_target="tpu_custom_call" | custom-call | flops 268435456 | bytes 1048576 | tf_op jit(solution)/shard_map/prepare/pallas_call | solution.py:255
  16.7 10.3 %all-to-all-done.fields = f32[16,8,256]{2,1,0:T(8,128)S(1)} async-done(((f32[16,8,256]{2,1,0:T(8,128)}), f32[16,8,256]{2,1,0:T(8,128)S(1)}, u32[]{:S(2)}, u32[]{:S(2)}) %all-to-all-start) | async-done | bytes 131104 | tf_op jit(solution)/shard_map/all_to_all | solution.py:35
  26.9 1.1 %pairs.1 = bf16[32,8,256]{2,1,0:T(8,128)(2,1)} custom-call(f32[16,8,256]{2,1,0:T(8,128)S(1)} %all-to-all-done.fields, f32[8,256]{1,0:T(8,128)S(1)} %get-tuple-element.25.target, f32[8,256]{1,0:T(8,128)S(1)} %get-tuple-element.26.weight, f32[8,128]{1,0:T(8,128)S(1)} %get-tuple-element.27.area_sum), custom_call_target="tpu_custom_call" | custom-call | tf_op jit(solution)/shard_map/pairs/pallas_call | solution.py:354
  28.1 3.8 %all-to-all-start.1 = ((bf16[32,8,256]{2,1,0:T(8,128)(2,1)}), bf16[32,8,256]{2,1,0:T(8,128)(2,1)S(1)}, u32[]{:S(2)}, u32[]{:S(2)}) async-start(bf16[32,8,256]{2,1,0:T(8,128)(2,1)} %pairs.1), calls=%async_computation.1 | async-start | bytes 262144 | tf_op jit(solution)/shard_map/all_to_all | solution.py:35
  31.9 0.0 collective-permute-done.latent
  31.9 3.6 %far_forward.1 = (bf16[1024,256]{1,0:T(8,128)(2,1)}, bf16[1024,256]{1,0:T(8,128)(2,1)}) custom-call(bf16[1024,1024]{1,0:T(8,128)(2,1)} %w_in.5, bf16[1024,256]{1,0:T(8,128)(2,1)S(1)} %collective-permute-done.latent), custom_call_target="tpu_custom_call" | custom-call | flops 536870912 | bytes 4194304 | tf_op jit(solution)/shard_map/far_forward/pallas_call | solution.py:205
  35.5 7.0 %all-to-all-done.1 = bf16[32,8,256]{2,1,0:T(8,128)(2,1)S(1)} async-done(((bf16[32,8,256]{2,1,0:T(8,128)(2,1)}), bf16[32,8,256]{2,1,0:T(8,128)(2,1)S(1)}, u32[]{:S(2)}, u32[]{:S(2)}) %all-to-all-start.1) | async-done | bytes 131104 | tf_op jit(solution)/shard_map/all_to_all | solution.py:35
  42.6 2.6 %backward.1 = (bf16[4,128,1280]{2,1,0:T(8,128)(2,1)S(1)}, bf16[1024,256]{1,0:T(8,128)(2,1)S(1)}) custom-call(s32[1]{0:T(128)} %bitcast.1.place, bf16[16,2,8,256]{3,2,1,0:T(8,128)(2,1)S(1)} %bitcast.20, bf16[1024,128]{1,0:T(8,128)(2,1)S(1)} %get-tuple-element.28.w_out_t, bf16[1024,256]{1,0:T(8,128)(2,1)S(1)} %get-tuple-element.29.slope_v, ...), custom_call_target="tpu_custom_call" | custom-call | tf_op jit(solution)/shard_map/backward/pallas_call | solution.py:456
  45.1 21.2 %all_to_all.25.got = bf16[4,128,1280]{2,1,0:T(8,128)(2,1)S(1)} all-to-all(bf16[4,128,1280]{2,1,0:T(8,128)(2,1)S(1)} %get-tuple-element.35), channel_id=1, replica_groups=mesh['y'=8,'xh'=2,'xl'=2,'z'=8,'c'=2] {'xh','xl'}, dimensions={0} | all-to-all | bytes 2621440 | tf_op jit(solution)/shard_map/all_to_all | solution.py:35
  66.3 0.3 add_x.1
  66.7 22.7 %all_to_all.26.got = bf16[8,16,1280]{2,1,0:T(8,128)(2,1)S(1)} all-to-all(bf16[8,16,1280]{2,1,0:T(8,128)(2,1)S(1)} %bitcast.18), channel_id=1, replica_groups=mesh['y'=8,'xh'=2,'xl'=2,'z'=8,'c'=2] {'z'}, dimensions={0} | all-to-all | bytes 655360 | tf_op jit(solution)/shard_map/all_to_all | solution.py:35
  89.3 0.8 add_z.1
  90.1 3.4 %all-to-all-start.4 = ((bf16[8,16,384]{2,1,0:T(8,128)(2,1)}), bf16[8,16,384]{2,1,0:T(8,128)(2,1)S(1)}, u32[]{:S(2)}, u32[]{:S(2)}) async-start(bf16[8,16,384]{2,1,0:T(8,128)(2,1)} %get-tuple-element.36), calls=%async_computation.4 | async-start | bytes 196608 | tf_op jit(solution)/shard_map/all_to_all | solution.py:35
  93.5 3.2 %grad_latent.1 = bf16[1024,256]{1,0:T(8,128)(2,1)} custom-call(bf16[1024,1024]{1,0:T(8,128)(2,1)} %w_in.5, bf16[1024,256]{1,0:T(8,128)(2,1)S(1)} %get-tuple-element.38.dpre, f32[8,128]{1,0:T(8,128)S(1)} %get-tuple-element.39.scale), custom_call_target="tpu_custom_call" | custom-call | flops 536870912 | bytes 4194304 | tf_op jit(solution)/shard_map/grad_latent/pallas_call | solution.py:292
  96.7 5.4 %all-to-all-done.4.got = bf16[8,16,384]{2,1,0:T(8,128)(2,1)S(1)} async-done(((bf16[8,16,384]{2,1,0:T(8,128)(2,1)}), bf16[8,16,384]{2,1,0:T(8,128)(2,1)S(1)}, u32[]{:S(2)}, u32[]{:S(2)}) %all-to-all-start.4) | async-done | bytes 98336 | tf_op jit(solution)/shard_map/all_to_all | solution.py:35
  102.2 0.9 finish.1
Async XLA Ops:
  0.6 3.8 %copy-start = (bf16[1,1024,256]{2,1,0:T(8,128)(2,1)S(1)}, bf16[1,1024,256]{2,1,0:T(8,128)(2,1)}, u32[]{:S(2)}) copy-start(bf16[1,1024,256]{2,1,0:T(8,128)(2,1)} %param.6) | copy-start | bytes 1572868
  4.5 27.5 %collective-permute-start = (bf16[1024,256]{1,0:T(8,128)(2,1)S(1)}, bf16[1024,256]{1,0:T(8,128)(2,1)S(1)}, u32[]{:S(2)}, u32[]{:S(2)}) collective-permute-start(bf16[1024,256]{1,0:T(8,128)(2,1)S(1)} %bitcast.23), channel_id=1, source_target_pairs={{0,1},{1,0},{2,3},{3,2},{4,5},{5,4},{6,7},{7,6},{8,9},{9,8},{10,11... | collective-permute-start | bytes 1572872 | tf_op jit(solution)/shard_map/ppermute | solution.py:600
  6.4 20.5 %all-to-all-start = ((f32[16,8,256]{2,1,0:T(8,128)}), f32[16,8,256]{2,1,0:T(8,128)S(1)}, u32[]{:S(2)}, u32[]{:S(2)}) async-start(f32[16,8,256]{2,1,0:T(8,128)} %bitcast.26), calls=%async_computation | async-start | bytes 262144 | tf_op jit(solution)/shard_map/all_to_all | solution.py:35
  28.1 14.5 %all-to-all-start.1 = ((bf16[32,8,256]{2,1,0:T(8,128)(2,1)}), bf16[32,8,256]{2,1,0:T(8,128)(2,1)S(1)}, u32[]{:S(2)}, u32[]{:S(2)}) async-start(bf16[32,8,256]{2,1,0:T(8,128)(2,1)} %pairs.1), calls=%async_computation.1 | async-start | bytes 262144 | tf_op jit(solution)/shard_map/all_to_all | solution.py:35
  90.1 12.0 %all-to-all-start.4 = ((bf16[8,16,384]{2,1,0:T(8,128)(2,1)}), bf16[8,16,384]{2,1,0:T(8,128)(2,1)S(1)}, u32[]{:S(2)}, u32[]{:S(2)}) async-start(bf16[8,16,384]{2,1,0:T(8,128)(2,1)} %get-tuple-element.36), calls=%async_computation.4 | async-start | bytes 196608 | tf_op jit(solution)/shard_map/all_to_all | solution.py:35

commit v7 on v6

--- a/solution.py
+++ b/solution.py
@@ -13,7 +13,6 @@
 OWN = 8
 ENS = ("y", "xh")
 PLANE = ("xl", "z")
-CHIP_X = ("xh", "xl")
 BLOCK = 1024
 
 smooth_sq = 0.01
@@ -187,10 +186,12 @@
     )(*in_hbm(w_in, latent, w_out))
 
 
-def far_kernel(w_in, latent, hidden, slope, w_in_v, hidden_v, slope_v, sems):
+def far_kernel(w_in, latent, hidden, slope, w_in_v, latent_v, hidden_v, slope_v, sems):
     copies = Copies(sems)
+    first = copies.start(latent, latent_v)
     weights = Stream(copies, w_in, w_in_v)
-    for here, product in products(weights, w_in_v, latent):
+    copies.wait(first)
+    for here, product in products(weights, w_in_v, latent_v):
         value, bend = gelu(product)
         hidden_v[here, :] = value.astype(bf16)
         copies.start(hidden_v.at[here], hidden.at[here])
@@ -204,12 +205,12 @@
     pts = latent.shape[1]
     return pl.pallas_call(
         far_kernel,
-        in_specs=[hbm(), whole()],
+        in_specs=[hbm()] * 2,
         out_specs=[hbm()] * 2,
         out_shape=[pltpu.HBM((hid, pts), bf16), pltpu.HBM((hid, pts), bf16)],
         scratch_shapes=scratch(
-            ((hid, lat), bf16), ((hid, pts), bf16), ((hid, pts), bf16),
-            copies=6 * len(blocks(hid)),
+            ((hid, lat), bf16), ((lat, pts), bf16), ((hid, pts), bf16), ((hid, pts), bf16),
+            copies=4 * len(blocks(hid)) + 1,
         ),
         compiler_params=params(16),
         cost_estimate=pl.CostEstimate(
@@ -220,8 +221,8 @@
 
 
 def prepare_kernel(
-    owner, w_out_h, target_h, area_h, var_weight_h, w_out_t, target, weight, area_sum,
-    w_out_v, target_v, area_v, var_weight_v, sems,
+    owner, w_out_h, target_h, area_h, var_weight_h, w_out_t_h, target, weight, area_sum,
+    w_out_v, w_out_t, target_v, area_v, var_weight_v, sems,
 ):
     copies = Copies(sems)
     inputs = [
@@ -235,6 +236,7 @@
         w_out_v[...], row_table().astype(bf16), (((0,), (1,)), ((), ())),
         preferred_element_type=f32,
     ).astype(bf16)
+    copies.start(w_out_t, w_out_t_h)
     for copy in inputs[1:]:
         copies.wait(copy)
     row = lax.broadcasted_iota(jnp.int32, (OWN, VARS), 0)
@@ -255,16 +257,17 @@
     return pl.pallas_call(
         prepare_kernel,
         in_specs=[smem()] + [hbm()] * 4,
-        out_specs=[whole()] * 4,
+        out_specs=[hbm()] + [whole()] * 3,
         out_shape=[
-            jax.ShapeDtypeStruct((hid, PAD), bf16),
+            pltpu.HBM((hid, PAD), bf16),
             jax.ShapeDtypeStruct((OWN, pts), f32),
             jax.ShapeDtypeStruct((OWN, pts), f32),
             jax.ShapeDtypeStruct((8, PAD), f32),
         ],
         scratch_shapes=scratch(
-            (w_out.shape, bf16), (target.shape, f32), (area.shape, f32), (var_weight.shape, f32),
-            copies=4,
+            (w_out.shape, bf16), ((hid, PAD), bf16), (target.shape, f32),
+            (area.shape, f32), (var_weight.shape, f32),
+            copies=5,
         ),
         compiler_params=params(16),
         cost_estimate=pl.CostEstimate(flops=1 << 28, bytes_accessed=1 << 20, transcendentals=0),
@@ -363,113 +366,102 @@
 
 
 def backward_kernel(
-    place, dout, w_out_t, slope_v, slope_far, latent, latent_far, hidden, hidden_far,
-    terms_v, dpre_v, slope_far_v, latent_v, hidden_far_v, sems,
+    place, dout, w_out_t_h, slope, hidden, latent, *refs
 ):
+    sides = 4
+    far_latents, far_hiddens, far_slopes = refs[0:3], refs[3:6], refs[6:9]
+    terms, dpre_out = refs[9:11]
+    w_out_t, latents_v, hiddens_v, slopes_v, sems = refs[11:16]
     copies = Copies(sems)
-    me = place[0]
-    rows = terms_v.shape[1]
-    hid, pts = slope_v.shape
-    parts = blocks(hid)
-
-    def fetch(source, target, here):
-        return copies.start(source.at[here], target.at[here])
-
-    mine = (slice(None), pl.ds(2 * me, 2))
-    near = copies.start(latent.at[mine], latent_v)
-    halves = [fetch(slope_far, slope_far_v, parts[0])]
-    for here in parts[1:]:
-        halves.append(fetch(slope_far, slope_far_v, here))
-    late = copies.start(hidden_far.at[mine], hidden_far_v)
+    xl, core = place[0], place[1]
+    hid, pts = slope.shape
+
+    mine = (pl.ds(xl, 1), slice(None), pl.ds(core, 1))
+    copies.start(w_out_t_h, w_out_t)
+    copies.start(latent.at[mine], latents_v.at[0])
+    for k in range(sides - 1):
+        copies.start(far_latents[k].at[mine], latents_v.at[k + 1])
+        copies.start(far_slopes[k], slopes_v.at[k])
+        copies.start(far_hiddens[k].at[mine], hiddens_v.at[k])
 
     row = lax.broadcasted_iota(jnp.int32, (PAD, pts), 0)
     last = lax.rem(row, OWN) == OWN - 1
     seeds = []
     ride = jnp.zeros((1, pts), f32)
-    for which in (me, 1 - me):
-        value = dout[:, pl.ds(which, 1)].astype(f32).reshape(PAD, pts)
+    for at_x, at_c in ((xl, core), (xl, 1 - core), (1 - xl, core), (1 - xl, 1 - core)):
+        value = dout[:, pl.ds(2 * at_x + at_c, 1)].astype(f32).reshape(PAD, pts)
         ride = ride + jnp.sum(jnp.where(last, value, 0.0), axis=0, keepdims=True)
         seeds.append(jnp.where(last, 0.0, value).astype(bf16))
-
-    copies.wait(near)
-    for half in halves:
-        copies.wait(half)
-    copies.wait(late)
-    features = [
-        [latent_v[:, k].reshape(-1, pts) for k in range(2)],
-        [latent_far[:, pl.ds(2 * me + k, 1)].reshape(-1, pts) for k in range(2)],
-    ]
-    for here, half in zip(parts, halves):
-        first = second = None
-        for k, ref in enumerate((slope_v, slope_far_v)):
-            dh = dot(w_out_t[here, :], seeds[k])
-            dpre = (dh * ref[here, :].astype(f32)).astype(bf16)
-            if k == 0:
-                dpre_v[here, :] = dpre
-            swapped = jnp.concatenate(
-                [
-                    dpre[base + off : base + off + HALF]
-                    for base in range(0, BLOCK, PAD)
-                    for off in (HALF, 0)
-                ],
-                0,
-            )
-            a = dot_nt(features[k][0], dpre)
-            b = dot_nt(features[k][1], swapped)
-            first = a if first is None else first + a
-            second = b if second is None else second + b
-        low = lax.rem(lanes(first.shape), PAD) < HALF
-        for xh, value in enumerate(
-            (jnp.where(low, first, second), jnp.where(low, second, first))
-        ):
-            for xl in range(2):
-                terms_v[2 * xh + xl, :, here] = value[xl * rows : (xl + 1) * rows].astype(bf16)
-
-    out = dot_nt(hidden[:, pl.ds(2 * me, 2)].reshape(-1, pts), seeds[0])
-    out += dot_nt(hidden_far_v[...].reshape(-1, pts), seeds[1])
+    copies.finish()
+
+    first = second = out = None
+    for k in range(sides):
+        dh = dot(w_out_t[...], seeds[k])
+        bend = slope[...] if k == 0 else slopes_v[k - 1]
+        dpre = (dh * bend.astype(f32)).astype(bf16)
+        if k == 0:
+            dpre_out[...] = dpre
+        swapped = jnp.concatenate(
+            [
+                dpre[base + off : base + off + HALF]
+                for base in range(0, hid, PAD)
+                for off in (HALF, 0)
+            ],
+            0,
+        )
+        a = dot_nt(latents_v[k, 0, :, 0, 0].reshape(-1, pts), dpre)
+        b = dot_nt(latents_v[k, 0, :, 0, 1].reshape(-1, pts), swapped)
+        first = a if first is None else first + a
+        second = b if second is None else second + b
+        if k == 0:
+            rows = hidden[pl.ds(xl, 1), :, pl.ds(core, 1)]
+        else:
+            rows = hiddens_v[k - 1]
+        part = dot_nt(rows.reshape(-1, pts), seeds[k])
+        out = part if out is None else out + part
+    low = lax.rem(lanes(first.shape), PAD) < HALF
+    terms[:, 0:hid] = jnp.where(low, first, second).astype(bf16)
+    terms[:, hid : 2 * hid] = jnp.where(low, second, first).astype(bf16)
+
     out = out.reshape(-1, 2, 16, PAD)
     left = out[:, 0].reshape(-1, PAD)
     right = out[:, 1].reshape(-1, PAD)
     lane = lanes((1, PAD))
     parts = jnp.zeros((1, PAD), f32)
     for k in range(2):
-        mine = lax.div(lanes((1, pts)), 2) == k
-        value = jnp.sum(jnp.where(mine, ride, 0.0), axis=1, keepdims=True)
+        both = lax.div(lanes((1, pts)), 2) == k
+        value = jnp.sum(jnp.where(both, ride, 0.0), axis=1, keepdims=True)
         high = value.astype(bf16).astype(f32)
         parts = jnp.where(lane == spare(2 * k), high, parts)
         parts = jnp.where(lane == spare(2 * k + 1), value - high, parts)
     row = lax.rem(lax.broadcasted_iota(jnp.int32, left.shape, 0), 16)
     unused = lax.rem(lanes(left.shape), OWN) == OWN - 1
     left = jnp.where(unused, jnp.where(row == 0, parts, 0.0), left)
-    for xh in range(2):
-        for xl in range(2):
-            piece = slice(xl * rows, (xl + 1) * rows)
-            terms_v[2 * xh + xl, :, hid : hid + PAD] = left[piece].astype(bf16)
-            terms_v[2 * xh + xl, :, hid + PAD :] = right[piece].astype(bf16)
-
-
-def backward(place, dout, w_out_t, slope, slope_far, latent, latent_far, hidden, hidden_far):
+    terms[:, 2 * hid : 2 * hid + PAD] = left.astype(bf16)
+    terms[:, 2 * hid + PAD :] = right.astype(bf16)
+
+
+def backward(place, dout, w_out_t, slope, hidden, latent, far_latents, far_hiddens, far_slopes):
     hid, pts = slope.shape
-    plane = latent.shape[0]
-    shape = (4, plane * 16 // 2, hid + 2 * PAD)
-    half = ((plane, 2, 16, pts), bf16)
+    n_z = latent.shape[1]
+    quarter = (1, n_z, 1, 2, 16, pts)
     return pl.pallas_call(
         backward_kernel,
-        in_specs=[smem()] + [whole()] * 3 + [hbm()] * 2 + [whole()] * 2 + [hbm()],
+        in_specs=[smem(), whole(), hbm(), whole(), whole()] + [hbm()] * 10,
         out_specs=[whole()] * 2,
         out_shape=[
-            jax.ShapeDtypeStruct(shape, bf16),
+            jax.ShapeDtypeStruct((n_z * 16, 2 * hid + 2 * PAD), bf16),
             jax.ShapeDtypeStruct((hid, pts), bf16),
         ],
         scratch_shapes=scratch(
-            ((hid, pts), bf16), half, half,
-            copies=len(blocks(hid)) + 2,
+            ((hid, PAD), bf16), ((4, *quarter), bf16), ((3, *quarter), bf16),
+            ((3, hid, pts), bf16), copies=11
         ),
-        compiler_params=params(24),
+        compiler_params=params(28),
         name="backward",
     )(
-        place, dout, w_out_t, slope, *in_hbm(slope_far, latent), latent_far, hidden,
-        *in_hbm(hidden_far),
+        place, dout, *in_hbm(w_out_t), slope, hidden,
+        *in_hbm(latent), *far_latents, *in_hbm(*far_hiddens, *far_slopes),
     )
 
 
@@ -483,26 +475,6 @@
     return jnp.where(even, high, jnp.where(odd, low, tile))
 
 
-def add_x_kernel(hid, got, out):
-    value = got[0].astype(f32)
-    for k in range(1, got.shape[0]):
-        value = value + got[k].astype(f32)
-    out[:, 0:hid] = value[:, 0:hid].astype(bf16)
-    out[:, hid : hid + PAD] = split_again(value[:, hid : hid + PAD]).astype(bf16)
-    out[:, hid + PAD :] = value[:, hid + PAD :].astype(bf16)
-
-
-def add_x(got, hid):
-    return pl.pallas_call(
-        functools.partial(add_x_kernel, hid),
-        in_specs=[whole()],
-        out_specs=whole(),
-        out_shape=jax.ShapeDtypeStruct(got.shape[1:], bf16),
-        compiler_params=params(8),
-        name="add_x",
-    )(got)
-
-
 def pick(head, k):
     lane = lanes(head.shape)
     mine = (lane == spare(2 * k)) | (lane == spare(2 * k + 1))
@@ -514,13 +486,15 @@
     value = got[0].astype(f32)
     for k in range(1, got.shape[0]):
         value = value + got[k].astype(f32)
-    left = value[:, hid : hid + PAD]
+    left = value[:, 2 * hid : 2 * hid + PAD]
     keep = split_again(left).astype(bf16)
-    right = value[:, hid + PAD :].astype(bf16)
-    for y in range(out.shape[0]):
-        out_v[y, :, 0:PAD] = value[:, y * PAD : (y + 1) * PAD].astype(bf16)
-        out_v[y, :, PAD : 2 * PAD] = keep
-        out_v[y, :, 2 * PAD :] = right
+    right = value[:, 2 * hid + PAD :].astype(bf16)
+    for k in range(out.shape[0]):
+        y, xh = k // 2, k % 2
+        at = xh * hid + y * PAD
+        out_v[k, :, 0:PAD] = value[:, at : at + PAD].astype(bf16)
+        out_v[k, :, PAD : 2 * PAD] = keep
+        out_v[k, :, 2 * PAD :] = right
     copies.start(out_v, out)
     weight_total = pick(left[0:1, :], 1) * (1.0 / copied)
     scale[...] = jnp.broadcast_to(points_all / (weight_total * VARS), scale.shape)
@@ -528,7 +502,7 @@
 
 
 def add_z(got, hid, copied, points_all):
-    shape = (hid // PAD, got.shape[1], 3 * PAD)
+    shape = (2 * hid // PAD, got.shape[1], 3 * PAD)
     return pl.pallas_call(
         functools.partial(add_z_kernel, hid, copied, points_all),
         in_specs=[whole()],
@@ -582,6 +556,7 @@
     n_plane = lax.axis_size(PLANE)
     n_core = lax.axis_size("c")
     n_z = lax.axis_size("z")
+    n_xl = lax.axis_size("xl")
     pts = area.shape[0]
     hid, _ = w_in.shape
     own = PAD // n_ens
@@ -597,28 +572,33 @@
 
     fields = exchange(decoded.reshape(n_ens, own, pts), ENS)
     late = lax.optimization_barrier((features, w_out, decoded))
-    far = lax.ppermute(late[0], "c", swap)
+    below = lax.ppermute(late[0], "c", swap)
+    beside = lax.ppermute(late[0], "xl", swap)
     w_out_t, target_own, weight_own, area_sum = prepare(
         me.astype(jnp.int32)[None], late[1], target, area[None, :], var_weight[None, :]
     )
-    dout = pairs(fields, target_own, weight_own, area_sum, n_core)
-
-    dout_got = exchange(dout, ENS + ("c",))
-    far, _ = lax.optimization_barrier((far, dout))
-    hidden_far, slope_far = far_forward(w_in, far)
-
-    groups = lambda value: value.reshape(n_plane, 2 * n_core, 16, pts)
+    hidden_below, slope_below = far_forward(w_in, below)
+    dout = pairs(fields, target_own, weight_own, area_sum, n_xl * n_core)
+
+    dout_got = exchange(dout, ENS + ("xl", "c"))
+    beside, below, _ = lax.optimization_barrier((beside, below, dout))
+    across = lax.ppermute(beside, "c", swap)
+    hidden_beside, slope_beside = far_forward(w_in, beside)
+    hidden_across, slope_across = far_forward(w_in, across)
+
+    groups = lambda value: value.reshape(n_xl, n_z, n_core, 2, 16, pts)
     terms, dpre = backward(
-        core.astype(jnp.int32)[None],
-        dout_got.reshape(n_ens, n_core, own, pts),
-        w_out_t, slope, slope_far,
-        groups(features), groups(far), groups(hidden), groups(hidden_far),
+        jnp.stack([lax.axis_index("xl"), core]).astype(jnp.int32),
+        dout_got.reshape(n_ens, n_xl * n_core, own, pts),
+        w_out_t, slope, groups(hidden), groups(features),
+        [groups(value) for value in (below, beside, across)],
+        [groups(value) for value in (hidden_below, hidden_beside, hidden_across)],
+        [slope_below, slope_beside, slope_across],
     )
 
-    got = exchange(terms, CHIP_X)
-    got = exchange(add_x(got, hid).reshape(n_z, 16, hid + 2 * PAD), "z")
-    got, scale = add_z(got, hid, count * lax.axis_size("xh"), points_all)
-    got = exchange(got, "y")
+    got = exchange(terms.reshape(n_z, 16, 2 * hid + 2 * PAD), "z")
+    got, scale = add_z(got, hid, count, points_all)
+    got = exchange(got, ENS)
     grad_lat = grad_latent(w_in, dpre, scale)
     loss, part_in, part_out = finish(
         lax.axis_index("xh").astype(jnp.int32)[None], got, count, points_all, count

time: 104 us -> 106 us (1.019)
  blocking collectives: 43.9 us -> 29.4 us
  starting transfers between devices: 17.9 us -> 28.2 us
  Pallas kernels: 17.8 us -> 27.2 us
  waiting for transfers between devices: 22.7 us -> 19.7 us
    all_to_all x2 -> x1, blocking collectives: 43.9 us -> 29.4 us  [exchange(): return lax.all_to_all(pieces, axes, split_axis=0, concat_axis=0, tiled=True)]
    ppermute x1 -> x3, starting transfers between devices: 1.92 us -> 11.6 us  [the longest x1 7.79 us: per_device(): beside = lax.ppermute(late[0], 'xl', swap)]
    pallas_call x3 -> x4, Pallas kernels: 6.47 us -> 15.3 us  [the longest x3 10.9 us: far_forward(): pl.pallas_call(far_kernel, in_specs=[hbm()] * 2, out_specs=[hbm()] * 2, o...]
    all_to_all x3, waiting for transfers between devices: 22.7 us -> 19.7 us  [exchange(): return lax.all_to_all(pieces, axes, split_axis=0, concat_axis=0, tiled=True)]
  transfers between devices with their start and end apart: 4 -> 6, of which waited for: 3 -> 3; matrix products, arithmetic and copies ran while one was open for 0% -> 0% of each run, Pallas kernels for 9% -> 16%
where the time goes in v7:
time: 106 us; the launch traced here: 105 us
  blocking collectives  29.4 us (28%)
  starting transfers between devices  28.2 us (27%)
  Pallas kernels  27.2 us (26%)
  waiting for transfers between devices  19.7 us (19%)
    all_to_all x1, blocking collectives, exchange(): return lax.all_to_all(pieces, axes, split_axis=0, concat_axis=0, tiled=True)  29.4 us
    all_to_all x3, waiting for transfers between devices, exchange(): return lax.all_to_all(pieces, axes, split_axis=0, concat_axis=0, tiled=True)  19.7 us
    all_to_all x3, starting transfers between devices, exchange(): return lax.all_to_all(pieces, axes, split_axis=0, concat_axis=0, tiled=True)  16.6 us
    pallas_call x3, Pallas kernels, far_forward(): pl.pallas_call(far_kernel, in_specs=[hbm()] * 2, out_specs=[hbm()] * 2, o...  10.9 us
    ppermute x1, starting transfers between devices, per_device(): beside = lax.ppermute(late[0], 'xl', swap)  7.79 us
    pallas_call x1, Pallas kernels, backward(): pl.pallas_call(backward_kernel, in_specs=[smem(), whole(), hbm(), whole()...  4.38 us
    pallas_call x1, Pallas kernels, forward(): pl.pallas_call(forward_kernel, in_specs=[hbm()] * 3, out_specs=[whole(),...  3.81 us
    pallas_call x1, Pallas kernels, grad_latent(): pl.pallas_call(grad_kernel, in_specs=[hbm(), whole(), whole()], out_specs...  3.2 us
  transfers between devices with their start and end apart: 6, of which 3 were waited for; matrix products, arithmetic and copies ran while one was open for 0% of the time, Pallas kernels for 16%

profile of v7, /device:TPU:2, one launch (start us, length us, event | category | flops | bytes accessed | tf_op | source)
XLA Modules:
  0.0 105.4 jit_solution(14294976663469766245)
XLA Ops:
  0.6 0.0 copy-start
  0.6 3.8 %forward.1 = (bf16[1024,256]{1,0:T(8,128)(2,1)S(1)}, bf16[1024,256]{1,0:T(8,128)(2,1)S(1)}, f32[128,256]{1,0:T(8,128)}) custom-call(bf16[1024,1024]{1,0:T(8,128)(2,1)} %w_in.9, bf16[1024,256]{1,0:T(8,128)(2,1)} %bitcast.28, bf16[99,1024]{1,0:T(8,128)(2,1)} %w_out_h), custom_call_target="tpu_custom_call" | custom-call | tf_op jit(solution)/shard_map/forward/pallas_call | solution.py:171
  4.5 1.9 %collective-permute-start.1 = (bf16[1024,256]{1,0:T(8,128)(2,1)S(1)}, bf16[1024,256]{1,0:T(8,128)(2,1)S(1)}, u32[]{:S(2)}, u32[]{:S(2)}) collective-permute-start(bf16[1024,256]{1,0:T(8,128)(2,1)S(1)} %bitcast.30), channel_id=1, source_target_pairs={{0,1},{1,0},{2,3},{3,2},{4,5},{5,4},{6,7},{7,6},{8,9},{9,8},{10,11... | collective-permute-start | bytes 1572872 | tf_op jit(solution)/shard_map/ppermute | solution.py:575
  6.4 7.8 %collective-permute-start = (bf16[1024,256]{1,0:T(8,128)(2,1)S(1)}, bf16[1024,256]{1,0:T(8,128)(2,1)S(1)}, u32[]{:S(2)}, u32[]{:S(2)}) collective-permute-start(bf16[1024,256]{1,0:T(8,128)(2,1)S(1)} %bitcast.31), channel_id=1, source_target_pairs={{0,16},{16,0},{1,17},{17,1},{2,18},{18,2},{3,19},{19,3},{4,20},{20... | collective-permute-start | bytes 1572872 | tf_op jit(solution)/shard_map/ppermute | solution.py:576
  14.2 3.7 %all-to-all-start = ((f32[16,8,256]{2,1,0:T(8,128)}), f32[16,8,256]{2,1,0:T(8,128)S(1)}, u32[]{:S(2)}, u32[]{:S(2)}) async-start(f32[16,8,256]{2,1,0:T(8,128)} %bitcast.36), calls=%async_computation | async-start | bytes 262144 | tf_op jit(solution)/shard_map/all_to_all | solution.py:34
  17.9 2.0 %prepare.1 = (bf16[1024,128]{1,0:T(8,128)(2,1)}, f32[8,256]{1,0:T(8,128)S(1)}, f32[8,256]{1,0:T(8,128)S(1)}, f32[8,128]{1,0:T(8,128)S(1)}) custom-call(s32[1]{0:T(128)} %bitcast.5.owner, bf16[99,1024]{1,0:T(8,128)(2,1)} %w_out_h, f32[99,256]{1,0:T(8,128)} %target_h.1, f32[1,256]{1,0:T(1,128)} %bitcast.39, f32[1,99]{1,0:T(1,128)} %bitcast.40), custom_call_target="tpu_custom_call" | custom-call | flops 268435456 | bytes 1048576 | tf_op jit(solution)/shard_map/prepare/pallas_call | solution.py:257
  19.9 9.7 %all-to-all-done.fields = f32[16,8,256]{2,1,0:T(8,128)S(1)} async-done(((f32[16,8,256]{2,1,0:T(8,128)}), f32[16,8,256]{2,1,0:T(8,128)S(1)}, u32[]{:S(2)}, u32[]{:S(2)}) %all-to-all-start) | async-done | bytes 131104 | tf_op jit(solution)/shard_map/all_to_all | solution.py:34
  29.6 1.2 %pairs.1 = bf16[64,8,256]{2,1,0:T(8,128)(2,1)} custom-call(f32[16,8,256]{2,1,0:T(8,128)S(1)} %all-to-all-done.fields, f32[8,256]{1,0:T(8,128)S(1)} %get-tuple-element.30.target, f32[8,256]{1,0:T(8,128)S(1)} %get-tuple-element.31.weight, f32[8,128]{1,0:T(8,128)S(1)} %get-tuple-element.32.area_sum), custom_call_target="tpu_custom_call" | custom-call | tf_op jit(solution)/shard_map/pairs/pallas_call | solution.py:357
  30.8 0.0 collective-permute-done.1.latent
  30.8 0.0 collective-permute-done.latent
  30.9 1.9 %collective-permute-start.2 = (bf16[1024,256]{1,0:T(8,128)(2,1)S(1)}, bf16[1024,256]{1,0:T(8,128)(2,1)S(1)}, u32[]{:S(2)}, u32[]{:S(2)}) collective-permute-start(bf16[1024,256]{1,0:T(8,128)(2,1)S(1)} %collective-permute-done.latent), channel_id=1, source_target_pairs={{0,1},{1,0},{2,3},{3,2},{4,5},{5,4},{6,7},{7,6},{8,9},{9,8},{10,11... | collective-permute-start | bytes 1572872 | tf_op jit(solution)/shard_map/ppermute | solution.py:585
  32.8 5.7 %all-to-all-start.1 = ((bf16[64,8,256]{2,1,0:T(8,128)(2,1)}), bf16[64,8,256]{2,1,0:T(8,128)(2,1)S(1)}, u32[]{:S(2)}, u32[]{:S(2)}) async-start(bf16[64,8,256]{2,1,0:T(8,128)(2,1)} %pairs.1), calls=%async_computation.1 | async-start | bytes 524288 | tf_op jit(solution)/shard_map/all_to_all | solution.py:34
  38.5 0.1 pad_add_fusion.place
  38.6 3.7 %far_forward.4 = (bf16[1024,256]{1,0:T(8,128)(2,1)}, bf16[1024,256]{1,0:T(8,128)(2,1)}) custom-call(bf16[1024,1024]{1,0:T(8,128)(2,1)} %w_in.9, bf16[1024,256]{1,0:T(8,128)(2,1)S(1)} %collective-permute-done.latent), custom_call_target="tpu_custom_call" | custom-call | flops 536870912 | bytes 4194304 | tf_op jit(solution)/shard_map/far_forward/pallas_call | solution.py:206
  42.2 3.6 %far_forward.3 = (bf16[1024,256]{1,0:T(8,128)(2,1)}, bf16[1024,256]{1,0:T(8,128)(2,1)}) custom-call(bf16[1024,1024]{1,0:T(8,128)(2,1)} %w_in.9, bf16[1024,256]{1,0:T(8,128)(2,1)S(1)} %collective-permute-done.1.latent), custom_call_target="tpu_custom_call" | custom-call | flops 536870912 | bytes 4194304 | tf_op jit(solution)/shard_map/far_forward/pallas_call | solution.py:206
  45.9 3.7 %far_forward.5 = (bf16[1024,256]{1,0:T(8,128)(2,1)}, bf16[1024,256]{1,0:T(8,128)(2,1)}) custom-call(bf16[1024,1024]{1,0:T(8,128)(2,1)} %w_in.9, bf16[1024,256]{1,0:T(8,128)(2,1)S(1)} %collective-permute-done.2.latent), custom_call_target="tpu_custom_call" | custom-call | flops 536870912 | bytes 4194304 | tf_op jit(solution)/shard_map/far_forward/pallas_call | solution.py:206
  49.5 1.3 %all-to-all-done.1 = bf16[64,8,256]{2,1,0:T(8,128)(2,1)S(1)} async-done(((bf16[64,8,256]{2,1,0:T(8,128)(2,1)}), bf16[64,8,256]{2,1,0:T(8,128)(2,1)S(1)}, u32[]{:S(2)}, u32[]{:S(2)}) %all-to-all-start.1) | async-done | bytes 262176 | tf_op jit(solution)/shard_map/all_to_all | solution.py:34
  50.8 4.4 %backward.1 = (bf16[128,2304]{1,0:T(8,128)(2,1)S(1)}, bf16[1024,256]{1,0:T(8,128)(2,1)S(1)}) custom-call(s32[2]{0:T(128)S(1)} %pad_add_fusion.place, bf16[16,4,8,256]{3,2,1,0:T(8,128)(2,1)S(1)} %bitcast.25, bf16[1024,128]{1,0:T(8,128)(2,1)} %get-tuple-element.33.w_out_t_h, bf16[1024,256]{1,0:T(8,128)(2,1)S(1)} %get-tuple-element.34.slope, ...), custom_call_target="tpu_custom_call" | custom-call | tf_op jit(solution)/shard_map/backward/pallas_call | solution.py:448
  55.2 29.4 %all_to_all.20.got = bf16[8,16,2304]{2,1,0:T(8,128)(2,1)S(1)} all-to-all(bf16[8,16,2304]{2,1,0:T(8,128)(2,1)S(1)} %bitcast.26), channel_id=1, replica_groups=mesh['y'=8,'xh'=2,'xl'=2,'z'=8,'c'=2] {'z'}, dimensions={0} | all-to-all | bytes 1179648 | tf_op jit(solution)/shard_map/all_to_all | solution.py:34
  84.6 0.8 add_z.1
  85.4 7.2 %all-to-all-start.3 = ((bf16[16,16,384]{2,1,0:T(8,128)(2,1)}), bf16[16,16,384]{2,1,0:T(8,128)(2,1)S(1)}, u32[]{:S(2)}, u32[]{:S(2)}) async-start(bf16[16,16,384]{2,1,0:T(8,128)(2,1)} %get-tuple-element.46), calls=%async_computation.3 | async-start | bytes 393216 | tf_op jit(solution)/shard_map/all_to_all | solution.py:34
  92.6 3.2 %grad_latent.1 = bf16[1024,256]{1,0:T(8,128)(2,1)} custom-call(bf16[1024,1024]{1,0:T(8,128)(2,1)} %w_in.9, bf16[1024,256]{1,0:T(8,128)(2,1)S(1)} %get-tuple-element.48.dpre, f32[8,128]{1,0:T(8,128)S(1)} %get-tuple-element.49.scale), custom_call_target="tpu_custom_call" | custom-call | flops 536870912 | bytes 4194304 | tf_op jit(solution)/shard_map/grad_latent/pallas_call | solution.py:295
  95.8 8.7 %all-to-all-done.3.got = bf16[16,16,384]{2,1,0:T(8,128)(2,1)S(1)} async-done(((bf16[16,16,384]{2,1,0:T(8,128)(2,1)}), bf16[16,16,384]{2,1,0:T(8,128)(2,1)S(1)}, u32[]{:S(2)}, u32[]{:S(2)}) %all-to-all-start.3) | async-done | bytes 196640 | tf_op jit(solution)/shard_map/all_to_all | solution.py:34
  104.6 0.9 finish.1
  (2 shorter events, 0.0 us)
Async XLA Ops:
  0.6 3.8 %copy-start = (bf16[1,1024,256]{2,1,0:T(8,128)(2,1)S(1)}, bf16[1,1024,256]{2,1,0:T(8,128)(2,1)}, u32[]{:S(2)}) copy-start(bf16[1,1024,256]{2,1,0:T(8,128)(2,1)} %param.6) | copy-start | bytes 1572868
  4.5 26.4 %collective-permute-start.1 = (bf16[1024,256]{1,0:T(8,128)(2,1)S(1)}, bf16[1024,256]{1,0:T(8,128)(2,1)S(1)}, u32[]{:S(2)}, u32[]{:S(2)}) collective-permute-start(bf16[1024,256]{1,0:T(8,128)(2,1)S(1)} %bitcast.30), channel_id=1, source_target_pairs={{0,1},{1,0},{2,3},{3,2},{4,5},{5,4},{6,7},{7,6},{8,9},{9,8},{10,11... | collective-permute-start | bytes 1572872 | tf_op jit(solution)/shard_map/ppermute | solution.py:575
  6.4 24.4 %collective-permute-start = (bf16[1024,256]{1,0:T(8,128)(2,1)S(1)}, bf16[1024,256]{1,0:T(8,128)(2,1)S(1)}, u32[]{:S(2)}, u32[]{:S(2)}) collective-permute-start(bf16[1024,256]{1,0:T(8,128)(2,1)S(1)} %bitcast.31), channel_id=1, source_target_pairs={{0,16},{16,0},{1,17},{17,1},{2,18},{18,2},{3,19},{19,3},{4,20},{20... | collective-permute-start | bytes 1572872 | tf_op jit(solution)/shard_map/ppermute | solution.py:576
  14.2 15.4 %all-to-all-start = ((f32[16,8,256]{2,1,0:T(8,128)}), f32[16,8,256]{2,1,0:T(8,128)S(1)}, u32[]{:S(2)}, u32[]{:S(2)}) async-start(f32[16,8,256]{2,1,0:T(8,128)} %bitcast.36), calls=%async_computation | async-start | bytes 262144 | tf_op jit(solution)/shard_map/all_to_all | solution.py:34
  30.9 15.0 %collective-permute-start.2 = (bf16[1024,256]{1,0:T(8,128)(2,1)S(1)}, bf16[1024,256]{1,0:T(8,128)(2,1)S(1)}, u32[]{:S(2)}, u32[]{:S(2)}) collective-permute-start(bf16[1024,256]{1,0:T(8,128)(2,1)S(1)} %collective-permute-done.latent), channel_id=1, source_target_pairs={{0,1},{1,0},{2,3},{3,2},{4,5},{5,4},{6,7},{7,6},{8,9},{9,8},{10,11... | collective-permute-start | bytes 1572872 | tf_op jit(solution)/shard_map/ppermute | solution.py:585
  32.8 18.0 %all-to-all-start.1 = ((bf16[64,8,256]{2,1,0:T(8,128)(2,1)}), bf16[64,8,256]{2,1,0:T(8,128)(2,1)S(1)}, u32[]{:S(2)}, u32[]{:S(2)}) async-start(bf16[64,8,256]{2,1,0:T(8,128)(2,1)} %pairs.1), calls=%async_computation.1 | async-start | bytes 524288 | tf_op jit(solution)/shard_map/all_to_all | solution.py:34
  85.4 19.1 %all-to-all-start.3 = ((bf16[16,16,384]{2,1,0:T(8,128)(2,1)}), bf16[16,16,384]{2,1,0:T(8,128)(2,1)S(1)}, u32[]{:S(2)}, u32[]{:S(2)}) async-start(bf16[16,16,384]{2,1,0:T(8,128)(2,1)} %get-tuple-element.46), calls=%async_computation.3 | async-start | bytes 393216 | tf_op jit(solution)/shard_map/all_to_all | solution.py:34

commit v8 on v7

--- a/solution.py
+++ b/solution.py
@@ -365,65 +365,120 @@
     )(fields, target, weight, area_sum)
 
 
-def backward_kernel(
-    place, dout, w_out_t_h, slope, hidden, latent, *refs
+def seeds_of(dout, which):
+    value = dout[:, pl.ds(which, 1)].astype(f32).reshape(PAD, dout.shape[-1])
+    last = lax.rem(lax.broadcasted_iota(jnp.int32, value.shape, 0), OWN) == OWN - 1
+    ride = jnp.sum(jnp.where(last, value, 0.0), axis=0, keepdims=True)
+    return jnp.where(last, 0.0, value).astype(bf16), ride
+
+
+def side_terms(seeds, w_out_t, bend, features_a, features_b, rows):
+    dpre = (dot(w_out_t, seeds) * bend.astype(f32)).astype(bf16)
+    swapped = jnp.concatenate(
+        [
+            dpre[base + off : base + off + HALF]
+            for base in range(0, dpre.shape[0], PAD)
+            for off in (HALF, 0)
+        ],
+        0,
+    )
+    return dpre, dot_nt(features_a, dpre), dot_nt(features_b, swapped), dot_nt(rows, seeds)
+
+
+def near_kernel(
+    place, dout, w_out_t_h, slope, hidden, latent, latent_far, hidden_far, slope_far,
+    first, second, outer, ride, dpre_out,
+    w_out_t, latents_v, hidden_v, slope_v, sems,
 ):
-    sides = 4
-    far_latents, far_hiddens, far_slopes = refs[0:3], refs[3:6], refs[6:9]
-    terms, dpre_out = refs[9:11]
-    w_out_t, latents_v, hiddens_v, slopes_v, sems = refs[11:16]
     copies = Copies(sems)
     xl, core = place[0], place[1]
-    hid, pts = slope.shape
-
+    pts = slope.shape[1]
     mine = (pl.ds(xl, 1), slice(None), pl.ds(core, 1))
     copies.start(w_out_t_h, w_out_t)
     copies.start(latent.at[mine], latents_v.at[0])
-    for k in range(sides - 1):
-        copies.start(far_latents[k].at[mine], latents_v.at[k + 1])
-        copies.start(far_slopes[k], slopes_v.at[k])
-        copies.start(far_hiddens[k].at[mine], hiddens_v.at[k])
-
-    row = lax.broadcasted_iota(jnp.int32, (PAD, pts), 0)
-    last = lax.rem(row, OWN) == OWN - 1
-    seeds = []
-    ride = jnp.zeros((1, pts), f32)
-    for at_x, at_c in ((xl, core), (xl, 1 - core), (1 - xl, core), (1 - xl, 1 - core)):
-        value = dout[:, pl.ds(2 * at_x + at_c, 1)].astype(f32).reshape(PAD, pts)
-        ride = ride + jnp.sum(jnp.where(last, value, 0.0), axis=0, keepdims=True)
-        seeds.append(jnp.where(last, 0.0, value).astype(bf16))
-    copies.finish()
-
-    first = second = out = None
-    for k in range(sides):
-        dh = dot(w_out_t[...], seeds[k])
-        bend = slope[...] if k == 0 else slopes_v[k - 1]
-        dpre = (dh * bend.astype(f32)).astype(bf16)
+    copies.start(latent_far.at[mine], latents_v.at[1])
+    copies.start(slope_far, slope_v)
+    copies.start(hidden_far.at[mine], hidden_v)
+    seeds = [seeds_of(dout, which) for which in (core, 1 - core)]
+    copies.finish()
+    total = [None, None, None]
+    for k, bend in enumerate((slope, slope_v)):
+        rows = hidden_v[...] if k else hidden[pl.ds(xl, 1), :, pl.ds(core, 1)]
+        dpre, *parts = side_terms(
+            seeds[k][0], w_out_t[...], bend[...],
+            latents_v[k, 0, :, 0, 0].reshape(-1, pts),
+            latents_v[k, 0, :, 0, 1].reshape(-1, pts),
+            rows.reshape(-1, pts),
+        )
         if k == 0:
             dpre_out[...] = dpre
-        swapped = jnp.concatenate(
-            [
-                dpre[base + off : base + off + HALF]
-                for base in range(0, hid, PAD)
-                for off in (HALF, 0)
-            ],
-            0,
+        total = [part if old is None else old + part for old, part in zip(total, parts)]
+    first[...], second[...], outer[...] = total
+    ride[...] = jnp.broadcast_to(seeds[0][1] + seeds[1][1], ride.shape)
+
+
+def near(place, dout, w_out_t, slope, hidden, latent, latent_far, hidden_far, slope_far):
+    hid, pts = slope.shape
+    n_z = latent.shape[1]
+    quarter = (1, n_z, 1, 2, 16, pts)
+    return pl.pallas_call(
+        near_kernel,
+        in_specs=[smem(), whole(), hbm(), whole(), whole()] + [hbm()] * 4,
+        out_specs=[whole()] * 5,
+        out_shape=[
+            jax.ShapeDtypeStruct((n_z * 16, hid), f32),
+            jax.ShapeDtypeStruct((n_z * 16, hid), f32),
+            jax.ShapeDtypeStruct((n_z * 32, PAD), f32),
+            jax.ShapeDtypeStruct((8, pts), f32),
+            jax.ShapeDtypeStruct((hid, pts), bf16),
+        ],
+        scratch_shapes=scratch(
+            ((hid, PAD), bf16), ((2, *quarter), bf16), (quarter, bf16), ((hid, pts), bf16),
+            copies=5,
+        ),
+        compiler_params=params(20),
+        cost_estimate=pl.CostEstimate(flops=1 << 30, bytes_accessed=4 << 20, transcendentals=0),
+        name="near",
+    )(
+        place, dout, *in_hbm(w_out_t), slope, hidden, *in_hbm(latent), latent_far,
+        *in_hbm(hidden_far, slope_far),
+    )
+
+
+def rest_kernel(
+    place, dout, first, second, outer, ride_near, w_out_t_h, *refs
+):
+    latents, hiddens, bends = refs[0:2], refs[2:4], refs[4:6]
+    kept, sent = refs[6:8]
+    w_out_t, latents_v, hiddens_v, slopes_v, sems = refs[8:13]
+    copies = Copies(sems)
+    xl, core, xh = place[0], place[1], place[2]
+    pts = dout.shape[-1]
+    hid = first.shape[1]
+    mine = (pl.ds(xl, 1), slice(None), pl.ds(core, 1))
+    copies.start(w_out_t_h, w_out_t)
+    for k in range(2):
+        copies.start(latents[k].at[mine], latents_v.at[k])
+        copies.start(bends[k], slopes_v.at[k])
+        copies.start(hiddens[k].at[mine], hiddens_v.at[k])
+    seeds = [seeds_of(dout, which) for which in (core, 1 - core)]
+    copies.finish()
+    total = [first[...], second[...], outer[...]]
+    for k in range(2):
+        _, *parts = side_terms(
+            seeds[k][0], w_out_t[...], slopes_v[k],
+            latents_v[k, 0, :, 0, 0].reshape(-1, pts),
+            latents_v[k, 0, :, 0, 1].reshape(-1, pts),
+            hiddens_v[k].reshape(-1, pts),
         )
-        a = dot_nt(latents_v[k, 0, :, 0, 0].reshape(-1, pts), dpre)
-        b = dot_nt(latents_v[k, 0, :, 0, 1].reshape(-1, pts), swapped)
-        first = a if first is None else first + a
-        second = b if second is None else second + b
-        if k == 0:
-            rows = hidden[pl.ds(xl, 1), :, pl.ds(core, 1)]
-        else:
-            rows = hiddens_v[k - 1]
-        part = dot_nt(rows.reshape(-1, pts), seeds[k])
-        out = part if out is None else out + part
-    low = lax.rem(lanes(first.shape), PAD) < HALF
-    terms[:, 0:hid] = jnp.where(low, first, second).astype(bf16)
-    terms[:, hid : 2 * hid] = jnp.where(low, second, first).astype(bf16)
-
-    out = out.reshape(-1, 2, 16, PAD)
+        total = [old + part for old, part in zip(total, parts)]
+    ride = ride_near[0:1, :] + seeds[0][1] + seeds[1][1]
+    low = lax.rem(lanes(total[0].shape), PAD) < HALF
+    keep = low == (xh == 0)
+    kept[:, 0:hid] = jnp.where(keep, total[0], total[1]).astype(bf16)
+    sent[:, 0:hid] = jnp.where(keep, total[1], total[0]).astype(bf16)
+
+    out = total[2].reshape(-1, 2, 16, PAD)
     left = out[:, 0].reshape(-1, PAD)
     right = out[:, 1].reshape(-1, PAD)
     lane = lanes((1, PAD))
@@ -437,32 +492,28 @@
     row = lax.rem(lax.broadcasted_iota(jnp.int32, left.shape, 0), 16)
     unused = lax.rem(lanes(left.shape), OWN) == OWN - 1
     left = jnp.where(unused, jnp.where(row == 0, parts, 0.0), left)
-    terms[:, 2 * hid : 2 * hid + PAD] = left.astype(bf16)
-    terms[:, 2 * hid + PAD :] = right.astype(bf16)
-
-
-def backward(place, dout, w_out_t, slope, hidden, latent, far_latents, far_hiddens, far_slopes):
-    hid, pts = slope.shape
-    n_z = latent.shape[1]
-    quarter = (1, n_z, 1, 2, 16, pts)
-    return pl.pallas_call(
-        backward_kernel,
-        in_specs=[smem(), whole(), hbm(), whole(), whole()] + [hbm()] * 10,
+    for ref in (kept, sent):
+        ref[:, hid : hid + PAD] = left.astype(bf16)
+        ref[:, hid + PAD :] = right.astype(bf16)
+
+
+def rest(place, dout, sums, w_out_t, latents, hiddens, bends):
+    first, _, _, ride = sums
+    rows, hid = first.shape
+    pts = ride.shape[1]
+    quarter = (1, latents[0].shape[1], 1, 2, 16, pts)
+    return pl.pallas_call(
+        rest_kernel,
+        in_specs=[smem()] + [whole()] * 5 + [hbm()] * 7,
         out_specs=[whole()] * 2,
-        out_shape=[
-            jax.ShapeDtypeStruct((n_z * 16, 2 * hid + 2 * PAD), bf16),
-            jax.ShapeDtypeStruct((hid, pts), bf16),
-        ],
+        out_shape=[jax.ShapeDtypeStruct((rows, hid + 2 * PAD), bf16)] * 2,
         scratch_shapes=scratch(
-            ((hid, PAD), bf16), ((4, *quarter), bf16), ((3, *quarter), bf16),
-            ((3, hid, pts), bf16), copies=11
-        ),
-        compiler_params=params(28),
-        name="backward",
-    )(
-        place, dout, *in_hbm(w_out_t), slope, hidden,
-        *in_hbm(latent), *far_latents, *in_hbm(*far_hiddens, *far_slopes),
-    )
+            ((hid, PAD), bf16), ((2, *quarter), bf16), ((2, *quarter), bf16),
+            ((2, hid, pts), bf16), copies=7,
+        ),
+        compiler_params=params(20),
+        name="rest",
+    )(place, dout, *sums, *in_hbm(w_out_t), *latents, *in_hbm(*hiddens, *bends))
 
 
 def split_again(tile):
@@ -475,6 +526,24 @@
     return jnp.where(even, high, jnp.where(odd, low, tile))
 
 
+def add_x_kernel(hid, kept, got, out):
+    value = kept[...].astype(f32) + got[...].astype(f32)
+    out[:, 0:hid] = value[:, 0:hid].astype(bf16)
+    out[:, hid : hid + PAD] = split_again(value[:, hid : hid + PAD]).astype(bf16)
+    out[:, hid + PAD :] = value[:, hid + PAD :].astype(bf16)
+
+
+def add_x(kept, got, hid):
+    return pl.pallas_call(
+        functools.partial(add_x_kernel, hid),
+        in_specs=[whole()] * 2,
+        out_specs=whole(),
+        out_shape=jax.ShapeDtypeStruct(kept.shape, bf16),
+        compiler_params=params(8),
+        name="add_x",
+    )(kept, got)
+
+
 def pick(head, k):
     lane = lanes(head.shape)
     mine = (lane == spare(2 * k)) | (lane == spare(2 * k + 1))
@@ -486,15 +555,13 @@
     value = got[0].astype(f32)
     for k in range(1, got.shape[0]):
         value = value + got[k].astype(f32)
-    left = value[:, 2 * hid : 2 * hid + PAD]
+    left = value[:, hid : hid + PAD]
     keep = split_again(left).astype(bf16)
-    right = value[:, 2 * hid + PAD :].astype(bf16)
-    for k in range(out.shape[0]):
-        y, xh = k // 2, k % 2
-        at = xh * hid + y * PAD
-        out_v[k, :, 0:PAD] = value[:, at : at + PAD].astype(bf16)
-        out_v[k, :, PAD : 2 * PAD] = keep
-        out_v[k, :, 2 * PAD :] = right
+    right = value[:, hid + PAD :].astype(bf16)
+    for y in range(out.shape[0]):
+        out_v[y, :, 0:PAD] = value[:, y * PAD : (y + 1) * PAD].astype(bf16)
+        out_v[y, :, PAD : 2 * PAD] = keep
+        out_v[y, :, 2 * PAD :] = right
     copies.start(out_v, out)
     weight_total = pick(left[0:1, :], 1) * (1.0 / copied)
     scale[...] = jnp.broadcast_to(points_all / (weight_total * VARS), scale.shape)
@@ -502,7 +569,7 @@
 
 
 def add_z(got, hid, copied, points_all):
-    shape = (2 * hid // PAD, got.shape[1], 3 * PAD)
+    shape = (hid // PAD, got.shape[1], 3 * PAD)
     return pl.pallas_call(
         functools.partial(add_z_kernel, hid, copied, points_all),
         in_specs=[whole()],
@@ -578,27 +645,32 @@
         me.astype(jnp.int32)[None], late[1], target, area[None, :], var_weight[None, :]
     )
     hidden_below, slope_below = far_forward(w_in, below)
-    dout = pairs(fields, target_own, weight_own, area_sum, n_xl * n_core)
-
-    dout_got = exchange(dout, ENS + ("xl", "c"))
+    dout = pairs(fields, target_own, weight_own, area_sum, n_core)
+
+    dout_got = exchange(dout, ENS + ("c",)).reshape(n_ens, n_core, own, pts)
     beside, below, _ = lax.optimization_barrier((beside, below, dout))
     across = lax.ppermute(beside, "c", swap)
     hidden_beside, slope_beside = far_forward(w_in, beside)
     hidden_across, slope_across = far_forward(w_in, across)
 
+    dout_beside = lax.ppermute(dout_got, "xl", swap)
     groups = lambda value: value.reshape(n_xl, n_z, n_core, 2, 16, pts)
-    terms, dpre = backward(
-        jnp.stack([lax.axis_index("xl"), core]).astype(jnp.int32),
-        dout_got.reshape(n_ens, n_xl * n_core, own, pts),
-        w_out_t, slope, groups(hidden), groups(features),
-        [groups(value) for value in (below, beside, across)],
-        [groups(value) for value in (hidden_below, hidden_beside, hidden_across)],
-        [slope_below, slope_beside, slope_across],
-    )
-
-    got = exchange(terms.reshape(n_z, 16, 2 * hid + 2 * PAD), "z")
-    got, scale = add_z(got, hid, count, points_all)
-    got = exchange(got, ENS)
+    place = jnp.stack([lax.axis_index("xl"), core, lax.axis_index("xh")]).astype(jnp.int32)
+    *sums, dpre = near(
+        place, dout_got, w_out_t, slope, groups(hidden), groups(features),
+        groups(below), groups(hidden_below), slope_below,
+    )
+    kept, sent = rest(
+        place, dout_beside, sums, w_out_t,
+        [groups(value) for value in (beside, across)],
+        [groups(value) for value in (hidden_beside, hidden_across)],
+        [slope_beside, slope_across],
+    )
+
+    got = add_x(kept, lax.ppermute(sent, "xh", swap), hid)
+    got = exchange(got.reshape(n_z, 16, hid + 2 * PAD), "z")
+    got, scale = add_z(got, hid, count * lax.axis_size("xh"), points_all)
+    got = exchange(got, "y")
     grad_lat = grad_latent(w_in, dpre, scale)
     loss, part_in, part_out = finish(
         lax.axis_index("xh").astype(jnp.int32)[None], got, count, points_all, count

time: 106 us -> 119 us (1.12)
  waiting for transfers between devices: 19.7 us -> 35.7 us
  blocking collectives: 29.4 us -> 22.9 us
  Pallas kernels: 27.2 us -> 29 us
    ppermute x0 -> x2, waiting for transfers between devices: none -> 10 us  [the longest x1 10 us: per_device(): got = add_x(kept, lax.ppermute(sent, 'xh', swap), hid)]
    ppermute x0 -> x2, starting transfers between devices: none -> 6.67 us  [the longest x1 3.51 us: per_device(): dout_beside = lax.ppermute(dout_got, 'xl', swap)]
    all_to_all x1, blocking collectives: 29.4 us -> 22.9 us  [exchange(): return lax.all_to_all(pieces, axes, split_axis=0, concat_axis=0, tiled=True)]
    all_to_all x3, waiting for transfers between devices: 19.7 us -> 25.7 us  [exchange(): return lax.all_to_all(pieces, axes, split_axis=0, concat_axis=0, tiled=True)]
    all_to_all x3, starting transfers between devices: 16.6 us -> 11 us  [exchange(): return lax.all_to_all(pieces, axes, split_axis=0, concat_axis=0, tiled=True)]
    pallas_call x1 -> x3, Pallas kernels: 4.38 us -> 6.26 us  [the longest x1 3.11 us: rest(): pl.pallas_call(rest_kernel, in_specs=[smem()] + [whole()] * 5 + [hbm()] *...]
  transfers between devices with their start and end apart: 6 -> 8, of which waited for: 3 -> 4; matrix products, arithmetic and copies ran while one was open for 0% -> 0% of each run, Pallas kernels for 16% -> 17%
where the time goes in v8:
time: 119 us; the launch traced here: 118 us
  waiting for transfers between devices  35.7 us (30%)
  starting transfers between devices  29.3 us (25%)
  Pallas kernels  29 us (24%)
  blocking collectives  22.9 us (19%)
    all_to_all x3, waiting for transfers between devices, exchange(): return lax.all_to_all(pieces, axes, split_axis=0, concat_axis=0, tiled=True)  25.7 us
    all_to_all x1, blocking collectives, exchange(): return lax.all_to_all(pieces, axes, split_axis=0, concat_axis=0, tiled=True)  22.9 us
    all_to_all x3, starting transfers between devices, exchange(): return lax.all_to_all(pieces, axes, split_axis=0, concat_axis=0, tiled=True)  11 us
    pallas_call x3, Pallas kernels, far_forward(): pl.pallas_call(far_kernel, in_specs=[hbm()] * 2, out_specs=[hbm()] * 2, o...  10.9 us
    ppermute x1, waiting for transfers between devices, per_device(): got = add_x(kept, lax.ppermute(sent, 'xh', swap), hid)  10 us
    ppermute x1, starting transfers between devices, per_device(): beside = lax.ppermute(late[0], 'xl', swap)  7.79 us
    pallas_call x1, Pallas kernels, forward(): pl.pallas_call(forward_kernel, in_specs=[hbm()] * 3, out_specs=[whole(),...  3.81 us
    ppermute x1, starting transfers between devices, per_device(): dout_beside = lax.ppermute(dout_got, 'xl', swap)  3.51 us
  transfers between devices with their start and end apart: 8, of which 4 were waited for; matrix products, arithmetic and copies ran while one was open for 0% of the time, Pallas kernels for 17%

profile of v8, /device:TPU:2, one launch (start us, length us, event | category | flops | bytes accessed | tf_op | source)
XLA Modules:
  0.0 117.8 jit_solution(15732285805451370739)
XLA Ops:
  0.6 3.8 %forward.1 = (bf16[1024,256]{1,0:T(8,128)(2,1)S(1)}, bf16[1024,256]{1,0:T(8,128)(2,1)S(1)}, f32[128,256]{1,0:T(8,128)}) custom-call(bf16[1024,1024]{1,0:T(8,128)(2,1)} %w_in.9, bf16[1024,256]{1,0:T(8,128)(2,1)} %bitcast.31, bf16[99,1024]{1,0:T(8,128)(2,1)} %w_out_h), custom_call_target="tpu_custom_call" | custom-call | tf_op jit(solution)/shard_map/forward/pallas_call | solution.py:171
  4.5 1.9 %collective-permute-start.2 = (bf16[1024,256]{1,0:T(8,128)(2,1)S(1)}, bf16[1024,256]{1,0:T(8,128)(2,1)S(1)}, u32[]{:S(2)}, u32[]{:S(2)}) collective-permute-start(bf16[1024,256]{1,0:T(8,128)(2,1)S(1)} %bitcast.33), channel_id=1, source_target_pairs={{0,1},{1,0},{2,3},{3,2},{4,5},{5,4},{6,7},{7,6},{8,9},{9,8},{10,11... | collective-permute-start | bytes 1572872 | tf_op jit(solution)/shard_map/ppermute | solution.py:642
  6.4 7.8 %collective-permute-start.1 = (bf16[1024,256]{1,0:T(8,128)(2,1)S(1)}, bf16[1024,256]{1,0:T(8,128)(2,1)S(1)}, u32[]{:S(2)}, u32[]{:S(2)}) collective-permute-start(bf16[1024,256]{1,0:T(8,128)(2,1)S(1)} %bitcast.34), channel_id=1, source_target_pairs={{0,16},{16,0},{1,17},{17,1},{2,18},{18,2},{3,19},{19,3},{4,20},{20... | collective-permute-start | bytes 1572872 | tf_op jit(solution)/shard_map/ppermute | solution.py:643
  14.2 3.7 %all-to-all-start = ((f32[16,8,256]{2,1,0:T(8,128)}), f32[16,8,256]{2,1,0:T(8,128)S(1)}, u32[]{:S(2)}, u32[]{:S(2)}) async-start(f32[16,8,256]{2,1,0:T(8,128)} %bitcast.36), calls=%async_computation | async-start | bytes 262144 | tf_op jit(solution)/shard_map/all_to_all | solution.py:34
  17.9 2.0 %prepare.1 = (bf16[1024,128]{1,0:T(8,128)(2,1)}, f32[8,256]{1,0:T(8,128)S(1)}, f32[8,256]{1,0:T(8,128)S(1)}, f32[8,128]{1,0:T(8,128)S(1)}) custom-call(s32[1]{0:T(128)} %bitcast.5.owner, bf16[99,1024]{1,0:T(8,128)(2,1)} %w_out_h, f32[99,256]{1,0:T(8,128)} %target_h.1, f32[1,256]{1,0:T(1,128)} %bitcast.40, f32[1,99]{1,0:T(1,128)} %bitcast.41), custom_call_target="tpu_custom_call" | custom-call | flops 268435456 | bytes 1048576 | tf_op jit(solution)/shard_map/prepare/pallas_call | solution.py:257
  19.9 9.7 %all-to-all-done.fields = f32[16,8,256]{2,1,0:T(8,128)S(1)} async-done(((f32[16,8,256]{2,1,0:T(8,128)}), f32[16,8,256]{2,1,0:T(8,128)S(1)}, u32[]{:S(2)}, u32[]{:S(2)}) %all-to-all-start) | async-done | bytes 131104 | tf_op jit(solution)/shard_map/all_to_all | solution.py:34
  29.6 1.2 pairs.1
  30.8 1.9 %collective-permute-start.3 = (bf16[1024,256]{1,0:T(8,128)(2,1)S(1)}, bf16[1024,256]{1,0:T(8,128)(2,1)S(1)}, u32[]{:S(2)}, u32[]{:S(2)}) collective-permute-start(bf16[1024,256]{1,0:T(8,128)(2,1)S(1)} %collective-permute-done.1.latent), channel_id=1, source_target_pairs={{0,1},{1,0},{2,3},{3,2},{4,5},{5,4},{6,7},{7,6},{8,9},{9,8},{10,11... | collective-permute-start | bytes 1572872 | tf_op jit(solution)/shard_map/ppermute | solution.py:652
  32.7 3.9 %all-to-all-start.1 = ((bf16[32,8,256]{2,1,0:T(8,128)(2,1)}), bf16[32,8,256]{2,1,0:T(8,128)(2,1)S(1)}, u32[]{:S(2)}, u32[]{:S(2)}) async-start(bf16[32,8,256]{2,1,0:T(8,128)(2,1)} %pairs.1), calls=%async_computation.1 | async-start | bytes 262144 | tf_op jit(solution)/shard_map/all_to_all | solution.py:34
  36.7 10.6 %all-to-all-done.1 = bf16[32,8,256]{2,1,0:T(8,128)(2,1)S(1)} async-done(((bf16[32,8,256]{2,1,0:T(8,128)(2,1)}), bf16[32,8,256]{2,1,0:T(8,128)(2,1)S(1)}, u32[]{:S(2)}, u32[]{:S(2)}) %all-to-all-start.1) | async-done | bytes 131104 | tf_op jit(solution)/shard_map/all_to_all | solution.py:34
  47.3 3.5 %collective-permute-start = (bf16[16,2,8,256]{3,2,1,0:T(8,128)(2,1)S(1)}, bf16[16,2,8,256]{3,2,1,0:T(8,128)(2,1)S(1)}, u32[]{:S(2)}, u32[]{:S(2)}) collective-permute-start(bf16[16,2,8,256]{3,2,1,0:T(8,128)(2,1)S(1)} %bitcast.26), channel_id=1, source_target_pairs={{0,16},{16,0},{1,17},{17,1},{2,18},{18,2},{3,19},{19,3},{4,20},{20... | collective-permute-start | bytes 393224 | tf_op jit(solution)/shard_map/ppermute | solution.py:656
  50.8 3.6 %far_forward.4 = (bf16[1024,256]{1,0:T(8,128)(2,1)}, bf16[1024,256]{1,0:T(8,128)(2,1)}) custom-call(bf16[1024,1024]{1,0:T(8,128)(2,1)} %w_in.9, bf16[1024,256]{1,0:T(8,128)(2,1)S(1)} %collective-permute-done.1.latent), custom_call_target="tpu_custom_call" | custom-call | flops 536870912 | bytes 4194304 | tf_op jit(solution)/shard_map/far_forward/pallas_call | solution.py:206
  54.4 3.6 %far_forward.3 = (bf16[1024,256]{1,0:T(8,128)(2,1)}, bf16[1024,256]{1,0:T(8,128)(2,1)}) custom-call(bf16[1024,1024]{1,0:T(8,128)(2,1)} %w_in.9, bf16[1024,256]{1,0:T(8,128)(2,1)S(1)} %collective-permute-done.2.latent), custom_call_target="tpu_custom_call" | custom-call | flops 536870912 | bytes 4194304 | tf_op jit(solution)/shard_map/far_forward/pallas_call | solution.py:206
  58.1 2.9 %near.1 = (f32[128,1024]{1,0:T(8,128)S(1)}, f32[128,1024]{1,0:T(8,128)S(1)}, f32[256,128]{1,0:T(8,128)S(1)}, f32[8,256]{1,0:T(8,128)S(1)}, bf16[1024,256]{1,0:T(8,128)(2,1)S(1)}) custom-call(s32[3]{0:T(128)S(1)} %pad_add_fusion.place, bf16[16,2,8,256]{3,2,1,0:T(8,128)(2,1)S(1)} %bitcast.27, bf16[1024,128]{1,0:T(8,128)(2,1)} %get-tuple-element.38.w_out_t_h, ...), custom_call_target="tpu_custom_call" | custom-call | flops 1073741824 | bytes 4194304 | tf_op jit(solution)/shard_map/near/pallas_call | solution.py:424
  61.0 3.6 %far_forward.5 = (bf16[1024,256]{1,0:T(8,128)(2,1)}, bf16[1024,256]{1,0:T(8,128)(2,1)}) custom-call(bf16[1024,1024]{1,0:T(8,128)(2,1)} %w_in.9, bf16[1024,256]{1,0:T(8,128)(2,1)S(1)} %collective-permute-done.3.latent), custom_call_target="tpu_custom_call" | custom-call | flops 536870912 | bytes 4194304 | tf_op jit(solution)/shard_map/far_forward/pallas_call | solution.py:206
  64.7 3.1 %rest.1 = (bf16[128,1280]{1,0:T(8,128)(2,1)S(1)}, bf16[128,1280]{1,0:T(8,128)(2,1)S(1)}) custom-call(s32[3]{0:T(128)S(1)} %pad_add_fusion.place, bf16[16,2,8,256]{3,2,1,0:T(8,128)(2,1)S(1)} %collective-permute-done.dout, f32[128,1024]{1,0:T(8,128)S(1)} %get-tuple-element.45.first, f32[128,1024]{1,0:T(8,128)S(1)} %get-tuple-element.46.second, ...), custom_call_target="tpu_custom_call" | custom-call | tf_op jit(solution)/shard_map/rest/pallas_call | solution.py:505
  67.8 3.2 %collective-permute-start.4 = (bf16[128,1280]{1,0:T(8,128)(2,1)S(1)}, bf16[128,1280]{1,0:T(8,128)(2,1)S(1)}, u32[]{:S(2)}, u32[]{:S(2)}) collective-permute-start(bf16[128,1280]{1,0:T(8,128)(2,1)S(1)} %get-tuple-element.55), channel_id=1, source_target_pairs={{0,32},{32,0},{1,33},{33,1},{2,34},{34,2},{3,35},{35,3},{4,36},{36... | collective-permute-start | bytes 983048 | tf_op jit(solution)/shard_map/ppermute | solution.py:670
  70.9 10.0 %collective-permute-done.4.got = bf16[128,1280]{1,0:T(8,128)(2,1)S(1)} collective-permute-done((bf16[128,1280]{1,0:T(8,128)(2,1)S(1)}, bf16[128,1280]{1,0:T(8,128)(2,1)S(1)}, u32[]{:S(2)}, u32[]{:S(2)}) %collective-permute-start.4) | collective-permute-done | bytes 327712 | tf_op jit(solution)/shard_map/ppermute | solution.py:670
  81.2 22.9 %all_to_all.20.got = bf16[8,16,1280]{2,1,0:T(8,128)(2,1)S(1)} all-to-all(bf16[8,16,1280]{2,1,0:T(8,128)(2,1)S(1)} %bitcast.24), channel_id=1, replica_groups=mesh['y'=8,'xh'=2,'xl'=2,'z'=8,'c'=2] {'z'}, dimensions={0} | all-to-all | bytes 655360 | tf_op jit(solution)/shard_map/all_to_all | solution.py:34
  104.1 0.8 add_z.1
  104.9 3.4 %all-to-all-start.3 = ((bf16[8,16,384]{2,1,0:T(8,128)(2,1)}), bf16[8,16,384]{2,1,0:T(8,128)(2,1)S(1)}, u32[]{:S(2)}, u32[]{:S(2)}) async-start(bf16[8,16,384]{2,1,0:T(8,128)(2,1)} %get-tuple-element.56), calls=%async_computation.3 | async-start | bytes 196608 | tf_op jit(solution)/shard_map/all_to_all | solution.py:34
  108.3 3.2 %grad_latent.1 = bf16[1024,256]{1,0:T(8,128)(2,1)} custom-call(bf16[1024,1024]{1,0:T(8,128)(2,1)} %w_in.9, bf16[1024,256]{1,0:T(8,128)(2,1)S(1)} %get-tuple-element.58.dpre, f32[8,128]{1,0:T(8,128)S(1)} %get-tuple-element.59.scale), custom_call_target="tpu_custom_call" | custom-call | flops 536870912 | bytes 4194304 | tf_op jit(solution)/shard_map/grad_latent/pallas_call | solution.py:295
  111.5 5.4 %all-to-all-done.3.got = bf16[8,16,384]{2,1,0:T(8,128)(2,1)S(1)} async-done(((bf16[8,16,384]{2,1,0:T(8,128)(2,1)}), bf16[8,16,384]{2,1,0:T(8,128)(2,1)S(1)}, u32[]{:S(2)}, u32[]{:S(2)}) %all-to-all-start.3) | async-done | bytes 98336 | tf_op jit(solution)/shard_map/all_to_all | solution.py:34
  117.0 0.9 finish.1
  (8 shorter events, 0.4 us)
Async XLA Ops:
  0.6 3.8 %copy-start = (bf16[1,1024,256]{2,1,0:T(8,128)(2,1)S(1)}, bf16[1,1024,256]{2,1,0:T(8,128)(2,1)}, u32[]{:S(2)}) copy-start(bf16[1,1024,256]{2,1,0:T(8,128)(2,1)} %param.6) | copy-start | bytes 1572868
  4.5 26.3 %collective-permute-start.2 = (bf16[1024,256]{1,0:T(8,128)(2,1)S(1)}, bf16[1024,256]{1,0:T(8,128)(2,1)S(1)}, u32[]{:S(2)}, u32[]{:S(2)}) collective-permute-start(bf16[1024,256]{1,0:T(8,128)(2,1)S(1)} %bitcast.33), channel_id=1, source_target_pairs={{0,1},{1,0},{2,3},{3,2},{4,5},{5,4},{6,7},{7,6},{8,9},{9,8},{10,11... | collective-permute-start | bytes 1572872 | tf_op jit(solution)/shard_map/ppermute | solution.py:642
  6.4 24.4 %collective-permute-start.1 = (bf16[1024,256]{1,0:T(8,128)(2,1)S(1)}, bf16[1024,256]{1,0:T(8,128)(2,1)S(1)}, u32[]{:S(2)}, u32[]{:S(2)}) collective-permute-start(bf16[1024,256]{1,0:T(8,128)(2,1)S(1)} %bitcast.34), channel_id=1, source_target_pairs={{0,16},{16,0},{1,17},{17,1},{2,18},{18,2},{3,19},{19,3},{4,20},{20... | collective-permute-start | bytes 1572872 | tf_op jit(solution)/shard_map/ppermute | solution.py:643
  14.2 15.4 %all-to-all-start = ((f32[16,8,256]{2,1,0:T(8,128)}), f32[16,8,256]{2,1,0:T(8,128)S(1)}, u32[]{:S(2)}, u32[]{:S(2)}) async-start(f32[16,8,256]{2,1,0:T(8,128)} %bitcast.36), calls=%async_computation | async-start | bytes 262144 | tf_op jit(solution)/shard_map/all_to_all | solution.py:34
  30.8 30.2 %collective-permute-start.3 = (bf16[1024,256]{1,0:T(8,128)(2,1)S(1)}, bf16[1024,256]{1,0:T(8,128)(2,1)S(1)}, u32[]{:S(2)}, u32[]{:S(2)}) collective-permute-start(bf16[1024,256]{1,0:T(8,128)(2,1)S(1)} %collective-permute-done.1.latent), channel_id=1, source_target_pairs={{0,1},{1,0},{2,3},{3,2},{4,5},{5,4},{6,7},{7,6},{8,9},{9,8},{10,11... | collective-permute-start | bytes 1572872 | tf_op jit(solution)/shard_map/ppermute | solution.py:652
  32.7 14.5 %all-to-all-start.1 = ((bf16[32,8,256]{2,1,0:T(8,128)(2,1)}), bf16[32,8,256]{2,1,0:T(8,128)(2,1)S(1)}, u32[]{:S(2)}, u32[]{:S(2)}) async-start(bf16[32,8,256]{2,1,0:T(8,128)(2,1)} %pairs.1), calls=%async_computation.1 | async-start | bytes 262144 | tf_op jit(solution)/shard_map/all_to_all | solution.py:34
  47.3 17.4 %collective-permute-start = (bf16[16,2,8,256]{3,2,1,0:T(8,128)(2,1)S(1)}, bf16[16,2,8,256]{3,2,1,0:T(8,128)(2,1)S(1)}, u32[]{:S(2)}, u32[]{:S(2)}) collective-permute-start(bf16[16,2,8,256]{3,2,1,0:T(8,128)(2,1)S(1)} %bitcast.26), channel_id=1, source_target_pairs={{0,16},{16,0},{1,17},{17,1},{2,18},{18,2},{3,19},{19,3},{4,20},{20... | collective-permute-start | bytes 393224 | tf_op jit(solution)/shard_map/ppermute | solution.py:656
  67.8 13.2 %collective-permute-start.4 = (bf16[128,1280]{1,0:T(8,128)(2,1)S(1)}, bf16[128,1280]{1,0:T(8,128)(2,1)S(1)}, u32[]{:S(2)}, u32[]{:S(2)}) collective-permute-start(bf16[128,1280]{1,0:T(8,128)(2,1)S(1)} %get-tuple-element.55), channel_id=1, source_target_pairs={{0,32},{32,0},{1,33},{33,1},{2,34},{34,2},{3,35},{35,3},{4,36},{36... | collective-permute-start | bytes 983048 | tf_op jit(solution)/shard_map/ppermute | solution.py:670
  104.9 12.0 %all-to-all-start.3 = ((bf16[8,16,384]{2,1,0:T(8,128)(2,1)}), bf16[8,16,384]{2,1,0:T(8,128)(2,1)S(1)}, u32[]{:S(2)}, u32[]{:S(2)}) async-start(bf16[8,16,384]{2,1,0:T(8,128)(2,1)} %get-tuple-element.56), calls=%async_computation.3 | async-start | bytes 196608 | tf_op jit(solution)/shard_map/all_to_all | solution.py:34

commit v9 on v6

--- a/solution.py
+++ b/solution.py
@@ -144,15 +144,24 @@
 
 
 def forward_kernel(
-    w_in, latent, w_out, hidden, slope, decoded, w_in_v, latent_v, w_out_v, decoded_v, sems
+    owner, w_in, latent, w_out, target_h, area_h, var_weight_h,
+    hidden, slope, decoded, w_out_t, target, weight, area_sum,
+    w_in_v, latent_v, w_out_v, target_v, area_v, var_weight_v, sems,
 ):
     copies = Copies(sems)
+    rows = copies.start(w_out, w_out_v)
     first = copies.start(latent, latent_v)
-    rows = copies.start(w_out, w_out_v)
     weights = Stream(copies, w_in, w_in_v)
+    copies.start(target_h, target_v)
+    copies.start(area_h, area_v)
+    copies.start(var_weight_h, var_weight_v)
+    copies.wait(rows)
+    table = row_table().astype(bf16)
+    w_out_rows = dot(table, w_out_v[...]).astype(bf16)
+    w_out_t[...] = lax.dot_general(
+        w_out_v[...], table, (((0,), (1,)), ((), ())), preferred_element_type=f32
+    ).astype(bf16)
     copies.wait(first)
-    copies.wait(rows)
-    w_out_rows = dot(row_table().astype(bf16), w_out_v[...]).astype(bf16)
     total = None
     for here, product in products(weights, w_in_v, latent_v):
         value, bend = gelu(product)
@@ -161,30 +170,43 @@
         slope[here, :] = bend.astype(bf16)
         part = dot(w_out_rows[:, here], value)
         total = part if total is None else total + part
-    decoded_v[...] = total
-    copies.start(decoded_v, decoded)
+    decoded[...] = total
     copies.finish()
-
-
-def forward(w_in, latent, w_out):
+    row = lax.broadcasted_iota(jnp.int32, (OWN, VARS), 0)
+    held = (row < OWN - 1) & (lanes((OWN, VARS)) == owner[0] * (OWN - 1) + row)
+    scale = jnp.sum(jnp.where(held, var_weight_v[...], 0.0), axis=1, keepdims=True)
+    weight[...] = area_v[...] * scale
+    target[...] = lax.dot_general(
+        held.astype(f32), target_v[...], (((1,), (0,)), ((), ())),
+        precision=lax.Precision.HIGHEST, preferred_element_type=f32,
+    )
+    area_sum[...] = jnp.broadcast_to(jnp.sum(area_v[...], keepdims=True), area_sum.shape)
+
+
+def forward(owner, w_in, latent, w_out, target, area, var_weight):
     hid, lat = w_in.shape
     pts = latent.shape[1]
     return pl.pallas_call(
         forward_kernel,
-        in_specs=[hbm()] * 3,
-        out_specs=[whole(), whole(), hbm()],
+        in_specs=[smem()] + [hbm()] * 6,
+        out_specs=[whole()] * 7,
         out_shape=[
             jax.ShapeDtypeStruct((hid, pts), bf16),
             jax.ShapeDtypeStruct((hid, pts), bf16),
-            pltpu.HBM((PAD, pts), f32),
+            jax.ShapeDtypeStruct((PAD, pts), f32),
+            jax.ShapeDtypeStruct((hid, PAD), bf16),
+            jax.ShapeDtypeStruct((OWN, pts), f32),
+            jax.ShapeDtypeStruct((OWN, pts), f32),
+            jax.ShapeDtypeStruct((8, PAD), f32),
         ],
         scratch_shapes=scratch(
-            ((hid, lat), bf16), ((lat, pts), bf16), ((VARS, hid), bf16), ((PAD, pts), f32),
-            copies=4 * len(blocks(hid)) + 3,
+            ((hid, lat), bf16), ((lat, pts), bf16), (w_out.shape, bf16), (target.shape, f32),
+            (area.shape, f32), (var_weight.shape, f32),
+            copies=2 * len(blocks(hid)) + 5,
         ),
         compiler_params=params(16),
         name="forward",
-    )(*in_hbm(w_in, latent, w_out))
+    )(owner, *in_hbm(w_in, latent, w_out, target, area, var_weight))
 
 
 def far_kernel(w_in, latent, hidden, slope, w_in_v, hidden_v, slope_v, sems):
@@ -217,59 +239,6 @@
         ),
         name="far_forward",
     )(*in_hbm(w_in), latent)
-
-
-def prepare_kernel(
-    owner, w_out_h, target_h, area_h, var_weight_h, w_out_t, target, weight, area_sum,
-    w_out_v, target_v, area_v, var_weight_v, sems,
-):
-    copies = Copies(sems)
-    inputs = [
-        copies.start(w_out_h, w_out_v),
-        copies.start(target_h, target_v),
-        copies.start(area_h, area_v),
-        copies.start(var_weight_h, var_weight_v),
-    ]
-    copies.wait(inputs[0])
-    w_out_t[...] = lax.dot_general(
-        w_out_v[...], row_table().astype(bf16), (((0,), (1,)), ((), ())),
-        preferred_element_type=f32,
-    ).astype(bf16)
-    for copy in inputs[1:]:
-        copies.wait(copy)
-    row = lax.broadcasted_iota(jnp.int32, (OWN, VARS), 0)
-    held = (row < OWN - 1) & (lanes((OWN, VARS)) == owner[0] * (OWN - 1) + row)
-    scale = jnp.sum(jnp.where(held, var_weight_v[...], 0.0), axis=1, keepdims=True)
-    weight[...] = area_v[...] * scale
-    target[...] = lax.dot_general(
-        held.astype(f32), target_v[...], (((1,), (0,)), ((), ())),
-        precision=lax.Precision.HIGHEST, preferred_element_type=f32,
-    )
-    area_sum[...] = jnp.broadcast_to(jnp.sum(area_v[...], keepdims=True), area_sum.shape)
-    copies.finish()
-
-
-def prepare(owner, w_out, target, area, var_weight):
-    hid = w_out.shape[1]
-    pts = target.shape[1]
-    return pl.pallas_call(
-        prepare_kernel,
-        in_specs=[smem()] + [hbm()] * 4,
-        out_specs=[whole()] * 4,
-        out_shape=[
-            jax.ShapeDtypeStruct((hid, PAD), bf16),
-            jax.ShapeDtypeStruct((OWN, pts), f32),
-            jax.ShapeDtypeStruct((OWN, pts), f32),
-            jax.ShapeDtypeStruct((8, PAD), f32),
-        ],
-        scratch_shapes=scratch(
-            (w_out.shape, bf16), (target.shape, f32), (area.shape, f32), (var_weight.shape, f32),
-            copies=4,
-        ),
-        compiler_params=params(16),
-        cost_estimate=pl.CostEstimate(flops=1 << 28, bytes_accessed=1 << 20, transcendentals=0),
-        name="prepare",
-    )(owner, *in_hbm(w_out, target, area, var_weight))
 
 
 def grad_kernel(w_in, dpre, scale, grad, w_in_v, grad_v, sems):
@@ -593,18 +562,17 @@
 
     count = float(n_ens)
     points_all = float(n_plane * n_core * pts)
-    hidden, slope, decoded = forward(w_in, features, w_out)
+    hidden, slope, decoded, w_out_t, target_own, weight_own, area_sum = forward(
+        me.astype(jnp.int32)[None], w_in, features, w_out, target, area[None, :],
+        var_weight[None, :],
+    )
 
     fields = exchange(decoded.reshape(n_ens, own, pts), ENS)
-    late = lax.optimization_barrier((features, w_out, decoded))
-    far = lax.ppermute(late[0], "c", swap)
-    w_out_t, target_own, weight_own, area_sum = prepare(
-        me.astype(jnp.int32)[None], late[1], target, area[None, :], var_weight[None, :]
-    )
     dout = pairs(fields, target_own, weight_own, area_sum, n_core)
 
     dout_got = exchange(dout, ENS + ("c",))
-    far, _ = lax.optimization_barrier((far, dout))
+    late, _ = lax.optimization_barrier((features, dout))
+    far = lax.ppermute(late, "c", swap)
     hidden_far, slope_far = far_forward(w_in, far)
 
     groups = lambda value: value.reshape(n_plane, 2 * n_core, 16, pts)

time: 104 us -> 102 us (0.981)
  blocking collectives: 43.9 us -> 63.6 us
  waiting for transfers between devices: 22.7 us -> 12.5 us
  starting transfers between devices: 17.9 us -> 9.16 us
  Pallas kernels: 17.8 us -> 16 us
    all_to_all x2 -> x3, blocking collectives: 43.9 us -> 63.6 us  [exchange(): return lax.all_to_all(pieces, axes, split_axis=0, concat_axis=0, tiled=True)]
    all_to_all x3 -> x2, waiting for transfers between devices: 22.7 us -> 12.5 us  [exchange(): return lax.all_to_all(pieces, axes, split_axis=0, concat_axis=0, tiled=True)]
    all_to_all x3 -> x2, starting transfers between devices: 16 us -> 7.24 us  [exchange(): return lax.all_to_all(pieces, axes, split_axis=0, concat_axis=0, tiled=True)]
    pallas_call x2 -> x1, Pallas kernels: 5.28 us -> 3.51 us  [forward(): pl.pallas_call(forward_kernel, in_specs=[smem()] + [hbm()] * 6, out_specs...]
  transfers between devices with their start and end apart: 4 -> 3, of which waited for: 3 -> 2; matrix products, arithmetic and copies ran while one was open for 0% -> 0% of each run, Pallas kernels for 9% -> 7%
where the time goes in v9:
time: 102 us
  blocking collectives  63.6 us (62%)
  Pallas kernels  16 us (16%)
  waiting for transfers between devices  12.5 us (12%)
  starting transfers between devices  9.16 us (9%)
    all_to_all x3, blocking collectives, exchange(): return lax.all_to_all(pieces, axes, split_axis=0, concat_axis=0, tiled=True)  63.6 us
    all_to_all x2, waiting for transfers between devices, exchange(): return lax.all_to_all(pieces, axes, split_axis=0, concat_axis=0, tiled=True)  12.5 us
    all_to_all x2, starting transfers between devices, exchange(): return lax.all_to_all(pieces, axes, split_axis=0, concat_axis=0, tiled=True)  7.24 us
    pallas_call x1, Pallas kernels, far_forward(): pl.pallas_call(far_kernel, in_specs=[hbm(), whole()], out_specs=[hbm()] *...  3.6 us
    pallas_call x1, Pallas kernels, forward(): pl.pallas_call(forward_kernel, in_specs=[smem()] + [hbm()] * 6, out_specs...  3.51 us
    pallas_call x1, Pallas kernels, grad_latent(): pl.pallas_call(grad_kernel, in_specs=[hbm(), whole(), whole()], out_specs...  3.19 us
    pallas_call x1, Pallas kernels, backward(): pl.pallas_call(backward_kernel, in_specs=[smem()] + [whole()] * 3 + [hbm(...  2.55 us
  transfers between devices with their start and end apart: 3, of which 2 were waited for; matrix products, arithmetic and copies ran while one was open for 0% of the time, Pallas kernels for 7%

profile of v9, /device:TPU:2, one launch (start us, length us, event | category | flops | bytes accessed | tf_op | source)
XLA Modules:
  0.0 101.9 jit_solution(4470218988606544911)
XLA Ops:
  0.6 0.0 copy-start
  0.7 3.5 %forward.1 = (bf16[1024,256]{1,0:T(8,128)(2,1)S(1)}, bf16[1024,256]{1,0:T(8,128)(2,1)S(1)}, f32[128,256]{1,0:T(8,128)S(1)}, bf16[1024,128]{1,0:T(8,128)(2,1)S(1)...) custom-call(s32[1]{0:T(128)} %bitcast.2.owner, bf16[1024,1024]{1,0:T(8,128)(2,1)} %w_in.5, ...), custom_call_target="tpu_custom_call" | custom-call | tf_op jit(solution)/shard_map/forward/pallas_call | solution.py:189
  4.2 19.7 %all_to_all.25.fields = f32[16,8,256]{2,1,0:T(8,128)S(1)} all-to-all(f32[16,8,256]{2,1,0:T(8,128)S(1)} %bitcast.21), channel_id=1, replica_groups=mesh['y'=8,'xh'=2,'xl'=2,'z'=8,'c'=2] {'y','xh'}, dimensions={0} | all-to-all | bytes 262144 | tf_op jit(solution)/shard_map/all_to_all | solution.py:35
  23.9 1.1 %pairs.1 = bf16[32,8,256]{2,1,0:T(8,128)(2,1)} custom-call(f32[16,8,256]{2,1,0:T(8,128)S(1)} %all_to_all.25.fields, f32[8,256]{1,0:T(8,128)S(1)} %get-tuple-element.22.target, f32[8,256]{1,0:T(8,128)S(1)} %get-tuple-element.23.weight, f32[8,128]{1,0:T(8,128)S(1)} %get-tuple-element.24.area_sum), custom_call_target="tpu_custom_call" | custom-call | tf_op jit(solution)/shard_map/pairs/pallas_call | solution.py:323
  25.0 0.0 copy-done
  25.0 1.9 %collective-permute-start = (bf16[1024,256]{1,0:T(8,128)(2,1)S(1)}, bf16[1024,256]{1,0:T(8,128)(2,1)S(1)}, u32[]{:S(2)}, u32[]{:S(2)}) collective-permute-start(bf16[1024,256]{1,0:T(8,128)(2,1)S(1)} %bitcast.24), channel_id=1, source_target_pairs={{0,1},{1,0},{2,3},{3,2},{4,5},{5,4},{6,7},{7,6},{8,9},{9,8},{10,11... | collective-permute-start | bytes 1572872 | tf_op jit(solution)/shard_map/ppermute | solution.py:575
  27.0 3.9 %all-to-all-start.1 = ((bf16[32,8,256]{2,1,0:T(8,128)(2,1)}), bf16[32,8,256]{2,1,0:T(8,128)(2,1)S(1)}, u32[]{:S(2)}, u32[]{:S(2)}) async-start(bf16[32,8,256]{2,1,0:T(8,128)(2,1)} %pairs.1), calls=%async_computation.1 | async-start | bytes 262144 | tf_op jit(solution)/shard_map/all_to_all | solution.py:35
  30.8 0.0 collective-permute-done.latent
  30.8 3.6 %far_forward.1 = (bf16[1024,256]{1,0:T(8,128)(2,1)}, bf16[1024,256]{1,0:T(8,128)(2,1)}) custom-call(bf16[1024,1024]{1,0:T(8,128)(2,1)} %w_in.5, bf16[1024,256]{1,0:T(8,128)(2,1)S(1)} %collective-permute-done.latent), custom_call_target="tpu_custom_call" | custom-call | flops 536870912 | bytes 4194304 | tf_op jit(solution)/shard_map/far_forward/pallas_call | solution.py:227
  34.5 7.0 %all-to-all-done.1 = bf16[32,8,256]{2,1,0:T(8,128)(2,1)S(1)} async-done(((bf16[32,8,256]{2,1,0:T(8,128)(2,1)}), bf16[32,8,256]{2,1,0:T(8,128)(2,1)S(1)}, u32[]{:S(2)}, u32[]{:S(2)}) %all-to-all-start.1) | async-done | bytes 131104 | tf_op jit(solution)/shard_map/all_to_all | solution.py:35
  41.5 2.6 %backward.1 = (bf16[4,128,1280]{2,1,0:T(8,128)(2,1)S(1)}, bf16[1024,256]{1,0:T(8,128)(2,1)S(1)}) custom-call(s32[1]{0:T(128)} %bitcast.1.place, bf16[16,2,8,256]{3,2,1,0:T(8,128)(2,1)S(1)} %bitcast.20, bf16[1024,128]{1,0:T(8,128)(2,1)S(1)} %get-tuple-element.25.w_out_t, bf16[1024,256]{1,0:T(8,128)(2,1)S(1)} %get-tuple-element.26.slope_v, ...), custom_call_target="tpu_custom_call" | custom-call | tf_op jit(solution)/shard_map/backward/pallas_call | solution.py:425
  44.0 21.2 %all_to_all.26.got = bf16[4,128,1280]{2,1,0:T(8,128)(2,1)S(1)} all-to-all(bf16[4,128,1280]{2,1,0:T(8,128)(2,1)S(1)} %get-tuple-element.31), channel_id=1, replica_groups=mesh['y'=8,'xh'=2,'xl'=2,'z'=8,'c'=2] {'xh','xl'}, dimensions={0} | all-to-all | bytes 2621440 | tf_op jit(solution)/shard_map/all_to_all | solution.py:35
  65.2 0.3 add_x.1
  65.6 22.7 %all_to_all.27.got = bf16[8,16,1280]{2,1,0:T(8,128)(2,1)S(1)} all-to-all(bf16[8,16,1280]{2,1,0:T(8,128)(2,1)S(1)} %bitcast.18), channel_id=1, replica_groups=mesh['y'=8,'xh'=2,'xl'=2,'z'=8,'c'=2] {'z'}, dimensions={0} | all-to-all | bytes 655360 | tf_op jit(solution)/shard_map/all_to_all | solution.py:35
  88.2 0.8 add_z.1
  89.1 3.4 %all-to-all-start.4 = ((bf16[8,16,384]{2,1,0:T(8,128)(2,1)}), bf16[8,16,384]{2,1,0:T(8,128)(2,1)S(1)}, u32[]{:S(2)}, u32[]{:S(2)}) async-start(bf16[8,16,384]{2,1,0:T(8,128)(2,1)} %get-tuple-element.32), calls=%async_computation.4 | async-start | bytes 196608 | tf_op jit(solution)/shard_map/all_to_all | solution.py:35
  92.4 3.2 %grad_latent.1 = bf16[1024,256]{1,0:T(8,128)(2,1)} custom-call(bf16[1024,1024]{1,0:T(8,128)(2,1)} %w_in.5, bf16[1024,256]{1,0:T(8,128)(2,1)S(1)} %get-tuple-element.34.dpre, f32[8,128]{1,0:T(8,128)S(1)} %get-tuple-element.35.scale), custom_call_target="tpu_custom_call" | custom-call | flops 536870912 | bytes 4194304 | tf_op jit(solution)/shard_map/grad_latent/pallas_call | solution.py:261
  95.6 5.4 %all-to-all-done.4.got = bf16[8,16,384]{2,1,0:T(8,128)(2,1)S(1)} async-done(((bf16[8,16,384]{2,1,0:T(8,128)(2,1)}), bf16[8,16,384]{2,1,0:T(8,128)(2,1)S(1)}, u32[]{:S(2)}, u32[]{:S(2)}) %all-to-all-start.4) | async-done | bytes 98336 | tf_op jit(solution)/shard_map/all_to_all | solution.py:35
  101.1 0.9 finish.1
Async XLA Ops:
  0.6 24.4 %copy-start = (bf16[1,1024,256]{2,1,0:T(8,128)(2,1)S(1)}, bf16[1,1024,256]{2,1,0:T(8,128)(2,1)}, u32[]{:S(2)}) copy-start(bf16[1,1024,256]{2,1,0:T(8,128)(2,1)} %param.6) | copy-start | bytes 1572868
  25.0 5.8 %collective-permute-start = (bf16[1024,256]{1,0:T(8,128)(2,1)S(1)}, bf16[1024,256]{1,0:T(8,128)(2,1)S(1)}, u32[]{:S(2)}, u32[]{:S(2)}) collective-permute-start(bf16[1024,256]{1,0:T(8,128)(2,1)S(1)} %bitcast.24), channel_id=1, source_target_pairs={{0,1},{1,0},{2,3},{3,2},{4,5},{5,4},{6,7},{7,6},{8,9},{9,8},{10,11... | collective-permute-start | bytes 1572872 | tf_op jit(solution)/shard_map/ppermute | solution.py:575
  27.0 14.5 %all-to-all-start.1 = ((bf16[32,8,256]{2,1,0:T(8,128)(2,1)}), bf16[32,8,256]{2,1,0:T(8,128)(2,1)S(1)}, u32[]{:S(2)}, u32[]{:S(2)}) async-start(bf16[32,8,256]{2,1,0:T(8,128)(2,1)} %pairs.1), calls=%async_computation.1 | async-start | bytes 262144 | tf_op jit(solution)/shard_map/all_to_all | solution.py:35
  89.1 12.0 %all-to-all-start.4 = ((bf16[8,16,384]{2,1,0:T(8,128)(2,1)}), bf16[8,16,384]{2,1,0:T(8,128)(2,1)S(1)}, u32[]{:S(2)}, u32[]{:S(2)}) async-start(bf16[8,16,384]{2,1,0:T(8,128)(2,1)} %get-tuple-element.32), calls=%async_computation.4 | async-start | bytes 196608 | tf_op jit(solution)/shard_map/all_to_all | solution.py:35

commit v10 on v6

--- a/solution.py
+++ b/solution.py
@@ -144,7 +144,7 @@
 
 
 def forward_kernel(
-    w_in, latent, w_out, hidden, slope, decoded, w_in_v, latent_v, w_out_v, decoded_v, sems
+    w_in, latent, w_out, hidden, slope, decoded, latent_v, w_in_v, w_out_v, decoded_v, sems
 ):
     copies = Copies(sems)
     first = copies.start(latent, latent_v)
@@ -172,14 +172,15 @@
     return pl.pallas_call(
         forward_kernel,
         in_specs=[hbm()] * 3,
-        out_specs=[whole(), whole(), hbm()],
+        out_specs=[whole(), whole(), hbm(), whole()],
         out_shape=[
             jax.ShapeDtypeStruct((hid, pts), bf16),
             jax.ShapeDtypeStruct((hid, pts), bf16),
             pltpu.HBM((PAD, pts), f32),
+            jax.ShapeDtypeStruct((lat, pts), bf16),
         ],
         scratch_shapes=scratch(
-            ((hid, lat), bf16), ((lat, pts), bf16), ((VARS, hid), bf16), ((PAD, pts), f32),
+            ((hid, lat), bf16), ((VARS, hid), bf16), ((PAD, pts), f32),
             copies=4 * len(blocks(hid)) + 3,
         ),
         compiler_params=params(16),
@@ -593,10 +594,10 @@
 
     count = float(n_ens)
     points_all = float(n_plane * n_core * pts)
-    hidden, slope, decoded = forward(w_in, features, w_out)
+    hidden, slope, decoded, latent_near = forward(w_in, features, w_out)
 
     fields = exchange(decoded.reshape(n_ens, own, pts), ENS)
-    late = lax.optimization_barrier((features, w_out, decoded))
+    late = lax.optimization_barrier((latent_near, w_out, decoded))
     far = lax.ppermute(late[0], "c", swap)
     w_out_t, target_own, weight_own, area_sum = prepare(
         me.astype(jnp.int32)[None], late[1], target, area[None, :], var_weight[None, :]

time: 104 us -> 104 us (level)
  no operation moved by 1% of the time
where the time goes in v10:
time: 104 us; the launch traced here: 103 us
  blocking collectives  43.9 us (42%)
  waiting for transfers between devices  22.7 us (22%)
  starting transfers between devices  17.9 us (17%)
  Pallas kernels  17.7 us (17%)
    all_to_all x2, blocking collectives, exchange(): return lax.all_to_all(pieces, axes, split_axis=0, concat_axis=0, tiled=True)  43.9 us
    all_to_all x3, waiting for transfers between devices, exchange(): return lax.all_to_all(pieces, axes, split_axis=0, concat_axis=0, tiled=True)  22.7 us
    all_to_all x3, starting transfers between devices, exchange(): return lax.all_to_all(pieces, axes, split_axis=0, concat_axis=0, tiled=True)  16 us
    pallas_call x1, Pallas kernels, forward(): pl.pallas_call(forward_kernel, in_specs=[hbm()] * 3, out_specs=[whole(),...  3.76 us
    pallas_call x1, Pallas kernels, far_forward(): pl.pallas_call(far_kernel, in_specs=[hbm(), whole()], out_specs=[hbm()] *...  3.61 us
    pallas_call x1, Pallas kernels, grad_latent(): pl.pallas_call(grad_kernel, in_specs=[hbm(), whole(), whole()], out_specs...  3.19 us
    pallas_call x1, Pallas kernels, backward(): pl.pallas_call(backward_kernel, in_specs=[smem()] + [whole()] * 3 + [hbm(...  2.55 us
  transfers between devices with their start and end apart: 4, of which 3 were waited for; matrix products, arithmetic and copies ran while one was open for 0% of the time, Pallas kernels for 9%

profile of v10, /device:TPU:2, one launch (start us, length us, event | category | flops | bytes accessed | tf_op | source)
XLA Modules:
  0.0 103.0 jit_solution(15917721662066959646)
XLA Ops:
  0.6 3.8 %forward.1 = (bf16[1024,256]{1,0:T(8,128)(2,1)S(1)}, bf16[1024,256]{1,0:T(8,128)(2,1)S(1)}, f32[128,256]{1,0:T(8,128)}, bf16[1024,256]{1,0:T(8,128)(2,1)S(1)}) custom-call(bf16[1024,1024]{1,0:T(8,128)(2,1)} %w_in.5, bf16[1024,256]{1,0:T(8,128)(2,1)} %bitcast.21, bf16[99,1024]{1,0:T(8,128)(2,1)} %w_out_h), custom_call_target="tpu_custom_call" | custom-call | tf_op jit(solution)/shard_map/forward/pallas_call | solution.py:172
  4.4 1.9 %collective-permute-start = (bf16[1024,256]{1,0:T(8,128)(2,1)S(1)}, bf16[1024,256]{1,0:T(8,128)(2,1)S(1)}, u32[]{:S(2)}, u32[]{:S(2)}) collective-permute-start(bf16[1024,256]{1,0:T(8,128)(2,1)S(1)} %get-tuple-element.32), channel_id=1, source_target_pairs={{0,1},{1,0},{2,3},{3,2},{4,5},{5,4},{6,7},{7,6},{8,9},{9,8},{10,11... | collective-permute-start | bytes 1572872 | tf_op jit(solution)/shard_map/ppermute | solution.py:601
  6.3 8.8 %all-to-all-start = ((f32[16,8,256]{2,1,0:T(8,128)}), f32[16,8,256]{2,1,0:T(8,128)S(1)}, u32[]{:S(2)}, u32[]{:S(2)}) async-start(f32[16,8,256]{2,1,0:T(8,128)} %bitcast.25), calls=%async_computation | async-start | bytes 262144 | tf_op jit(solution)/shard_map/all_to_all | solution.py:35
  15.1 1.5 %prepare.1 = (bf16[1024,128]{1,0:T(8,128)(2,1)S(1)}, f32[8,256]{1,0:T(8,128)S(1)}, f32[8,256]{1,0:T(8,128)S(1)}, f32[8,128]{1,0:T(8,128)S(1)}) custom-call(s32[1]{0:T(128)} %bitcast.4.owner, bf16[99,1024]{1,0:T(8,128)(2,1)} %w_out_h, f32[99,256]{1,0:T(8,128)} %target_h.1, f32[1,256]{1,0:T(1,128)} %bitcast.28, f32[1,99]{1,0:T(1,128)} %bitcast.29), custom_call_target="tpu_custom_call" | custom-call | flops 268435456 | bytes 1048576 | tf_op jit(solution)/shard_map/prepare/pallas_call | solution.py:256
  16.6 10.3 %all-to-all-done.fields = f32[16,8,256]{2,1,0:T(8,128)S(1)} async-done(((f32[16,8,256]{2,1,0:T(8,128)}), f32[16,8,256]{2,1,0:T(8,128)S(1)}, u32[]{:S(2)}, u32[]{:S(2)}) %all-to-all-start) | async-done | bytes 131104 | tf_op jit(solution)/shard_map/all_to_all | solution.py:35
  26.9 1.2 %pairs.1 = bf16[32,8,256]{2,1,0:T(8,128)(2,1)} custom-call(f32[16,8,256]{2,1,0:T(8,128)S(1)} %all-to-all-done.fields, f32[8,256]{1,0:T(8,128)S(1)} %get-tuple-element.27.target, f32[8,256]{1,0:T(8,128)S(1)} %get-tuple-element.28.weight, f32[8,128]{1,0:T(8,128)S(1)} %get-tuple-element.29.area_sum), custom_call_target="tpu_custom_call" | custom-call | tf_op jit(solution)/shard_map/pairs/pallas_call | solution.py:355
  28.0 3.9 %all-to-all-start.1 = ((bf16[32,8,256]{2,1,0:T(8,128)(2,1)}), bf16[32,8,256]{2,1,0:T(8,128)(2,1)S(1)}, u32[]{:S(2)}, u32[]{:S(2)}) async-start(bf16[32,8,256]{2,1,0:T(8,128)(2,1)} %pairs.1), calls=%async_computation.1 | async-start | bytes 262144 | tf_op jit(solution)/shard_map/all_to_all | solution.py:35
  31.9 0.0 collective-permute-done.latent
  31.9 3.6 %far_forward.1 = (bf16[1024,256]{1,0:T(8,128)(2,1)}, bf16[1024,256]{1,0:T(8,128)(2,1)}) custom-call(bf16[1024,1024]{1,0:T(8,128)(2,1)} %w_in.5, bf16[1024,256]{1,0:T(8,128)(2,1)S(1)} %collective-permute-done.latent), custom_call_target="tpu_custom_call" | custom-call | flops 536870912 | bytes 4194304 | tf_op jit(solution)/shard_map/far_forward/pallas_call | solution.py:206
  35.5 7.0 %all-to-all-done.1 = bf16[32,8,256]{2,1,0:T(8,128)(2,1)S(1)} async-done(((bf16[32,8,256]{2,1,0:T(8,128)(2,1)}), bf16[32,8,256]{2,1,0:T(8,128)(2,1)S(1)}, u32[]{:S(2)}, u32[]{:S(2)}) %all-to-all-start.1) | async-done | bytes 131104 | tf_op jit(solution)/shard_map/all_to_all | solution.py:35
  42.5 2.6 %backward.1 = (bf16[4,128,1280]{2,1,0:T(8,128)(2,1)S(1)}, bf16[1024,256]{1,0:T(8,128)(2,1)S(1)}) custom-call(s32[1]{0:T(128)} %bitcast.1.place, bf16[16,2,8,256]{3,2,1,0:T(8,128)(2,1)S(1)} %bitcast.20, bf16[1024,128]{1,0:T(8,128)(2,1)S(1)} %get-tuple-element.30.w_out_t, bf16[1024,256]{1,0:T(8,128)(2,1)S(1)} %get-tuple-element.31.slope_v, ...), custom_call_target="tpu_custom_call" | custom-call | tf_op jit(solution)/shard_map/backward/pallas_call | solution.py:457
  45.1 21.2 %all_to_all.25.got = bf16[4,128,1280]{2,1,0:T(8,128)(2,1)S(1)} all-to-all(bf16[4,128,1280]{2,1,0:T(8,128)(2,1)S(1)} %get-tuple-element.37), channel_id=1, replica_groups=mesh['y'=8,'xh'=2,'xl'=2,'z'=8,'c'=2] {'xh','xl'}, dimensions={0} | all-to-all | bytes 2621440 | tf_op jit(solution)/shard_map/all_to_all | solution.py:35
  66.3 0.3 add_x.1
  66.6 22.7 %all_to_all.26.got = bf16[8,16,1280]{2,1,0:T(8,128)(2,1)S(1)} all-to-all(bf16[8,16,1280]{2,1,0:T(8,128)(2,1)S(1)} %bitcast.18), channel_id=1, replica_groups=mesh['y'=8,'xh'=2,'xl'=2,'z'=8,'c'=2] {'z'}, dimensions={0} | all-to-all | bytes 655360 | tf_op jit(solution)/shard_map/all_to_all | solution.py:35
  89.3 0.8 add_z.1
  90.1 3.4 %all-to-all-start.4 = ((bf16[8,16,384]{2,1,0:T(8,128)(2,1)}), bf16[8,16,384]{2,1,0:T(8,128)(2,1)S(1)}, u32[]{:S(2)}, u32[]{:S(2)}) async-start(bf16[8,16,384]{2,1,0:T(8,128)(2,1)} %get-tuple-element.38), calls=%async_computation.4 | async-start | bytes 196608 | tf_op jit(solution)/shard_map/all_to_all | solution.py:35
  93.5 3.2 %grad_latent.1 = bf16[1024,256]{1,0:T(8,128)(2,1)} custom-call(bf16[1024,1024]{1,0:T(8,128)(2,1)} %w_in.5, bf16[1024,256]{1,0:T(8,128)(2,1)S(1)} %get-tuple-element.40.dpre, f32[8,128]{1,0:T(8,128)S(1)} %get-tuple-element.41.scale), custom_call_target="tpu_custom_call" | custom-call | flops 536870912 | bytes 4194304 | tf_op jit(solution)/shard_map/grad_latent/pallas_call | solution.py:293
  96.7 5.4 %all-to-all-done.4.got = bf16[8,16,384]{2,1,0:T(8,128)(2,1)S(1)} async-done(((bf16[8,16,384]{2,1,0:T(8,128)(2,1)}), bf16[8,16,384]{2,1,0:T(8,128)(2,1)S(1)}, u32[]{:S(2)}, u32[]{:S(2)}) %all-to-all-start.4) | async-done | bytes 98336 | tf_op jit(solution)/shard_map/all_to_all | solution.py:35
  102.1 0.9 finish.1
Async XLA Ops:
  4.4 27.5 %collective-permute-start = (bf16[1024,256]{1,0:T(8,128)(2,1)S(1)}, bf16[1024,256]{1,0:T(8,128)(2,1)S(1)}, u32[]{:S(2)}, u32[]{:S(2)}) collective-permute-start(bf16[1024,256]{1,0:T(8,128)(2,1)S(1)} %get-tuple-element.32), channel_id=1, source_target_pairs={{0,1},{1,0},{2,3},{3,2},{4,5},{5,4},{6,7},{7,6},{8,9},{9,8},{10,11... | collective-permute-start | bytes 1572872 | tf_op jit(solution)/shard_map/ppermute | solution.py:601
  6.3 20.5 %all-to-all-start = ((f32[16,8,256]{2,1,0:T(8,128)}), f32[16,8,256]{2,1,0:T(8,128)S(1)}, u32[]{:S(2)}, u32[]{:S(2)}) async-start(f32[16,8,256]{2,1,0:T(8,128)} %bitcast.25), calls=%async_computation | async-start | bytes 262144 | tf_op jit(solution)/shard_map/all_to_all | solution.py:35
  28.0 14.5 %all-to-all-start.1 = ((bf16[32,8,256]{2,1,0:T(8,128)(2,1)}), bf16[32,8,256]{2,1,0:T(8,128)(2,1)S(1)}, u32[]{:S(2)}, u32[]{:S(2)}) async-start(bf16[32,8,256]{2,1,0:T(8,128)(2,1)} %pairs.1), calls=%async_computation.1 | async-start | bytes 262144 | tf_op jit(solution)/shard_map/all_to_all | solution.py:35
  90.1 12.0 %all-to-all-start.4 = ((bf16[8,16,384]{2,1,0:T(8,128)(2,1)}), bf16[8,16,384]{2,1,0:T(8,128)(2,1)S(1)}, u32[]{:S(2)}, u32[]{:S(2)}) async-start(bf16[8,16,384]{2,1,0:T(8,128)(2,1)} %get-tuple-element.38), calls=%async_computation.4 | async-start | bytes 196608 | tf_op jit(solution)/shard_map/all_to_all | solution.py:35
